TPU v7x, 32 devices: a whole 2x2x4 slice. The times are simulated.
32 devices in a mesh: groups: 2 (over x), views: 16 (over z, y, core).
Axes of the slice: x: 2, y: 2, z: 4, core: 2. Of those that a mesh axis runs over, the one named last changes fastest.
Arguments:
- source_rows: bfloat16 [384, 320, 128], P(('groups', 'views')), parts along dimension 0, may hold values from -6 to 6
- route_owner: int32 [384, 1], P(('groups', 'views')), parts along dimension 0, may hold values from 0 to 15; in each aligned block of 12 rows (0 to 11, 12 to 23, ...) at most 2 rows name the same one
- target_row: int32 [384], P(('groups', 'views')), parts along dimension 0, may hold values from 0 to 3
- start_index: int32 [384], P(('groups', 'views')), parts along dimension 0, may hold values from 0 to 15
- reference_rows: bfloat16 [128, 320, 128], P(('groups', 'views')), parts along dimension 0, may hold values from -96 to 96
- conv_weight: float32 [40, 3, 3, 3], replicated, may hold values from -3 to 3
Outputs:
- depth_map: float32 [128, 128], P(('groups', 'views')), parts along dimension 0
There are 2 independent parts, one for each index of `groups`. A program takes and returns all parts, laid end to end along the dimension named above; an argument that names none is the same for every part. Nothing has to cross between parts.
Inputs may be any that keep to these rules, and one draw needn't show every extreme that they name: `route_owner`: among the rows of one device, no owner is named more than 2 times, a bound that some block reaches.
All inputs are finite; a program needn't handle non-finite values.
Results may differ from a plain program's by a relative error of at most 0.0003.
Values may be sent and summed in bfloat16 or wider, within the bound.
No kernel may reach another device: no remote copies, remote signals or barrier semaphores. Data moves between devices by JAX's collectives and lax.ppermute only.
A program may use at most 128 MiB of HBM per device.

v0:
```python
import functools

import jax
import jax.numpy as jnp
from jax import lax
from jax.experimental import pallas as pl
from jax.experimental.pallas import tpu as pltpu
from jax.sharding import PartitionSpec as P


CG = 8
DISP = 96
DSPAN = 16
CAP = 2
SETS = 2

VMEM = pl.BlockSpec(memory_space=pltpu.VMEM)
SMEM = pl.BlockSpec(memory_space=pltpu.SMEM)
ANY = pl.BlockSpec(memory_space=pl.ANY)


def pack_kernel(
    half, span, code_ref, source_ref, note_ref, far_ref, own_ref,
    count_ref, slot_ref, block_ref, sem,
):
    items, channels, pixels = source_ref.shape
    outs = (own_ref, far_ref)
    side = lax.div(lax.axis_index("views"), half)
    lane = lax.broadcasted_iota(jnp.int32, (1, pixels), 1)
    slot_ref[...] = jnp.full_like(slot_ref, -1.0)

    @pl.loop(0, SETS * half)
    def _(j):
        count_ref[j] = 0

    @pl.loop(0, items)
    def _(i):
        owner = lax.div(code_ref[i], span)
        rest = lax.rem(code_ref[i], span)
        home = lax.rem(owner, half)
        for t in range(SETS):

            @pl.when((lax.div(owner, half) == side) == (t == 0))
            def _():
                place = count_ref[t * half + home]
                count_ref[t * half + home] = place + 1
                first = pl.multiple_of(place * channels, channels)
                pltpu.make_async_copy(
                    source_ref.at[i], outs[t].at[home, pl.ds(first, channels), :], sem
                ).start()
                value = jnp.full((1, pixels), rest.astype(jnp.float32))
                line = slot_ref[pl.ds(home, 1), :]
                slot_ref[pl.ds(home, 1), :] = jnp.where(lane == t * CAP + place, value, line)

    height = note_ref.shape[0]
    row = lax.broadcasted_iota(jnp.int32, (height, pixels), 0)
    note = note_ref[...].astype(jnp.float32)

    @pl.loop(0, half)
    def _(j):
        line = jnp.broadcast_to(slot_ref[pl.ds(j, 1), :], (height, pixels))
        block_ref[j] = jnp.where(row == 4, line, note).astype(block_ref.dtype)

    last = pltpu.make_async_copy(
        block_ref, far_ref.at[:, pl.ds(CAP * channels, height), :], sem
    )
    last.start()

    @pl.loop(0, items)
    def _(i):
        pltpu.make_async_copy(
            source_ref.at[0], own_ref.at[0, pl.ds(0, channels), :], sem
        ).wait()

    last.wait()


def pack_rows(codes, source, note, half, span):
    _, channels, pixels = source.shape
    height = note.shape[0]
    lengths = (CAP * channels + height, CAP * channels)
    return pl.pallas_call(
        functools.partial(pack_kernel, half, span),
        out_shape=[jax.ShapeDtypeStruct((half, n, pixels), source.dtype) for n in lengths],
        in_specs=[SMEM, VMEM, VMEM],
        out_specs=[ANY, ANY],
        scratch_shapes=[
            pltpu.SMEM((SETS * half,), jnp.int32),
            pltpu.VMEM((half, pixels), jnp.float32),
            pltpu.VMEM((half, height, pixels), source.dtype),
            pltpu.SemaphoreType.DMA,
        ],
        compiler_params=pltpu.CompilerParams(vmem_limit_bytes=24 << 20),
        name="pack_rows",
    )(codes, source, note)


def left_kernel(reference_ref, left_ref):
    rows, channels, pixels = reference_ref.shape
    i = lax.broadcasted_iota(jnp.int32, (pixels, pixels), 0)
    x = lax.broadcasted_iota(jnp.int32, (pixels, pixels), 1)
    for e in range(3):
        pick = jnp.where(x == pixels - 1 - i + (e - 1), 1.0, 0.0).astype(jnp.bfloat16)
        for r in range(rows):
            moved = lax.dot_general(
                pick,
                reference_ref[r],
                (((1,), (1,)), ((), ())),
                preferred_element_type=jnp.float32,
            )
            left_ref[r, :, e * channels : (e + 1) * channels] = moved.astype(left_ref.dtype)


def stack_left(reference):
    rows, channels, pixels = reference.shape
    return pl.pallas_call(
        left_kernel,
        out_shape=jax.ShapeDtypeStruct((rows, pixels, 3 * channels), reference.dtype),
        in_specs=[VMEM],
        out_specs=VMEM,
        compiler_params=pltpu.CompilerParams(vmem_limit_bytes=24 << 20),
        name="stack_left",
    )(reference)


def split_two(values):
    high = values.astype(jnp.bfloat16)
    return high, (values - high.astype(jnp.float32)).astype(jnp.bfloat16)


def both_parts(values):
    return jnp.concatenate(split_two(values), axis=1)


def shift_left(values, offset):
    lane = lax.broadcasted_iota(jnp.int32, values.shape, 1)
    pixels = values.shape[1]
    moved = pltpu.roll(values, (-offset) % pixels, 1)
    return jnp.where((lane + offset >= 0) & (lane + offset < pixels), moved, 0.0)


def set_kernel(
    t, code_ref, arrived_ref, note_ref, left_ref, weight_ref, edge_ref,
    main_ref, low_ref, high_ref, slot_ref, stack_ref, total_ref, canvas_ref, sems,
):
    room, channels, pixels = slot_ref.shape
    rows = left_ref.shape[0]
    half = note_ref.shape[0]
    tap = pl.program_id(0)

    def slot_code(entry):
        return code_ref[lax.div(entry, CAP) * (SETS * CAP) + t * CAP + lax.rem(entry, CAP)]

    def slot_copy(entry):
        first = pl.multiple_of(lax.rem(entry, CAP) * channels, channels)
        return pltpu.make_async_copy(
            arrived_ref.at[lax.div(entry, CAP), pl.ds(first, channels), :],
            slot_ref.at[entry],
            sems.at[entry],
        )

    @pl.when(tap == 0)
    def _():
        lane = lax.broadcasted_iota(jnp.int32, (channels, pixels), 1)

        @pl.loop(0, room)
        def _(entry):
            @pl.when(slot_code(entry) >= 0)
            def _():
                slot_copy(entry).start()

        total_ref[...] = jnp.zeros_like(total_ref)
        canvas_ref[...] = jnp.zeros_like(canvas_ref)
        owner = lax.rem(lax.axis_index("views") + t * half, SETS * half)
        counts = [0.0] * rows
        for first in (0, 2):
            named = note_ref[:, first, :].astype(jnp.float32).astype(jnp.int32) == owner
            row = lax.div(note_ref[:, first + 1, :].astype(jnp.float32).astype(jnp.int32), DSPAN)
            for r in range(rows):
                counts[r] = counts[r] + jnp.where(named & (row == r), 1.0, 0.0)
        counts = [jnp.maximum(jnp.sum(count), 1.0) for count in counts]

        @pl.loop(0, room)
        def _(entry):
            code = slot_code(entry)

            @pl.when(code >= 0)
            def _():
                slot_copy(entry).wait()
                row = lax.div(code, DSPAN)
                begin = lax.rem(code, DSPAN)
                moved = pltpu.roll(slot_ref[entry].astype(jnp.float32), begin, 1)
                canvas_ref[row] = canvas_ref[row] + jnp.where(lane >= begin, moved, 0.0)

        for r in range(rows):
            mean = canvas_ref[r] / jnp.full((channels, pixels), counts[r])
            for e in range(3):
                stack_ref[r, e * channels : (e + 1) * channels, :] = shift_left(mean, e - 1)
            edge = jnp.broadcast_to(mean[:, :1], (channels, pixels)) * edge_ref[...]
            wide = jnp.dot(
                left_ref[r, :, 2 * channels :],
                both_parts(edge),
                preferred_element_type=jnp.float32,
            )
            total_ref[(rows + 2) * 3 + r] = wide[:, :pixels] + wide[:, pixels:]

    for r in range(rows):
        right = both_parts(stack_ref[r] * weight_ref[0])
        wide = jnp.dot(left_ref[r], right, preferred_element_type=jnp.float32)
        place = (r + 2 - lax.div(tap, 3)) * 3 + lax.rem(tap, 3)
        total_ref[place] = total_ref[place] + (wide[:, :pixels] + wide[:, pixels:])

    @pl.when(tap == pl.num_programs(0) - 1)
    def _():
        x = pixels - 1 - lax.broadcasted_iota(jnp.int32, (pixels, pixels), 0)
        v = lax.broadcasted_iota(jnp.int32, (pixels, pixels), 1)
        inside = (x >= v) & (x - v < DISP)
        border = (x < DISP - 1) & ((v >= pixels - 2) | (v < 1))
        for r in range(rows + 2):
            total = jnp.where(inside, total_ref[3 * r + 1], 0.0)
            for b in (0, 2):
                kept = jnp.where(inside, total_ref[3 * r + b], 0.0)
                total = total + pltpu.roll(kept, (b - 1) % pixels, 1)
            for a in range(3):
                if 0 <= r + a - 2 < rows:
                    edge = total_ref[(rows + 2) * 3 + r + a - 2]
                    moved = pltpu.roll(edge, (-8 * a) % pixels, 1) if a else edge
                    total = total + jnp.where(border, moved, 0.0)
            total = pltpu.roll(total, 0, 1, stride=1, stride_axis=0)
            kept = total.T[pixels - DISP :]
            if r == 0:
                low_ref[0] = kept
            elif r == rows + 1:
                high_ref[0] = kept
            else:
                main_ref[r - 1] = kept


def add_set(t, codes, arrived, note, left, weight, edge):
    rows, pixels, depth = left.shape
    channels = depth // 3
    half = arrived.shape[0]
    room = half * CAP
    shapes = [(n, DISP, pixels) for n in (rows, 1, 1)]
    once = pl.Buffered(1)
    return pl.pallas_call(
        functools.partial(set_kernel, t),
        grid=(weight.shape[0],),
        out_shape=[jax.ShapeDtypeStruct(shape, jnp.float32) for shape in shapes],
        in_specs=[
            SMEM,
            ANY,
            pl.BlockSpec(note.shape, lambda tap: (0, 0, 0), pipeline_mode=once),
            pl.BlockSpec(left.shape, lambda tap: (0, 0, 0), pipeline_mode=once),
            pl.BlockSpec((1,) + weight.shape[1:], lambda tap: (tap, 0, 0)),
            pl.BlockSpec(edge.shape, lambda tap: (0, 0), pipeline_mode=once),
        ],
        out_specs=[pl.BlockSpec(shape, lambda tap: (0, 0, 0)) for shape in shapes],
        scratch_shapes=[
            pltpu.VMEM((room, channels, pixels), arrived.dtype),
            pltpu.VMEM((rows, 3 * channels, pixels), jnp.float32),
            pltpu.VMEM(((rows + 2) * 3 + rows, pixels, pixels), jnp.float32),
            pltpu.VMEM((rows, channels, pixels), jnp.float32),
            pltpu.SemaphoreType.DMA((room,)),
        ],
        compiler_params=pltpu.CompilerParams(vmem_limit_bytes=24 << 20),
        cost_estimate=pl.CostEstimate(
            flops=2 * rows * 9 * pixels * 2 * pixels * 3 * channels,
            bytes_accessed=2 * room * channels * pixels,
            transcendentals=0,
        ),
        name="add_set",
    )(codes, arrived, note, left, weight, edge)


def depth_kernel(own_ref, far_ref, before_ref, before_far_ref, after_ref, after_far_ref, out_ref):
    rows, pixels = out_ref.shape
    level = (DISP - 1) - lax.broadcasted_iota(jnp.int32, (DISP, pixels), 0)
    share = level.astype(jnp.float32) / DISP
    depths = []
    for r in range(rows):
        scores = own_ref[r] + far_ref[r]
        if r == 0:
            scores = scores + (before_ref[0] + before_far_ref[0])
        if r == rows - 1:
            scores = scores + (after_ref[0] + after_far_ref[0])
        weights = jnp.exp(scores - jnp.max(scores, axis=0, keepdims=True))
        bottom = jnp.sum(weights, axis=0, keepdims=True)
        depths.append(jnp.sum(weights * share, axis=0, keepdims=True) / bottom)
    lane = lax.broadcasted_iota(jnp.int32, (8, pixels), 1)
    depth = jnp.concatenate(depths + [depths[0]] * (-rows % 8), axis=0)
    out_ref[...] = jnp.take_along_axis(depth, pixels - 1 - lane, axis=1)[:rows]


def depth_rows(*parts):
    rows, _, pixels = parts[0].shape
    return pl.pallas_call(
        depth_kernel,
        out_shape=jax.ShapeDtypeStruct((rows, pixels), jnp.float32),
        in_specs=[VMEM] * len(parts),
        out_specs=VMEM,
        compiler_params=pltpu.CompilerParams(vmem_limit_bytes=24 << 20),
        name="depth_rows",
    )(*parts)


def compute(source_rows, route_owner, target_row, start_index, reference_rows, conv_weight):
    views = lax.axis_size("views")
    half = views // 2
    rows, channels, pixels = reference_rows.shape
    span = rows * DSPAN
    send = functools.partial(lax.ppermute, axis_name="views")
    home = [(i, (i + half) % views) for i in range(views)]
    groups = [list(range(half)), list(range(half, views))]
    swap = functools.partial(
        lax.all_to_all,
        axis_name="views",
        split_axis=0,
        concat_axis=0,
        tiled=True,
        axis_index_groups=groups,
    )
    owner = route_owner[:, 0]
    rest = target_row * DSPAN + start_index
    named = jnp.stack([owner, rest]).astype(jnp.bfloat16)
    named = jnp.pad(named, ((0, 0), (0, pixels - named.shape[1])), constant_values=-1)
    far_named = send(named, perm=home)
    far_rows = send(reference_rows, perm=home)
    note = jnp.pad(jnp.concatenate([named, far_named]), ((0, 12), (0, 0)))
    packed_far, packed_own = pack_rows(owner * span + rest, source_rows, note, half, span)
    arrived_far = swap(packed_far)
    arrived_own = swap(packed_own)
    note = arrived_far[:, CAP * channels :]
    codes = note[:, 4, : SETS * CAP].astype(jnp.int32).reshape(-1)

    scaled = jnp.repeat(conv_weight / CG, CG, axis=0)
    taps = scaled.transpose(1, 2, 3, 0).reshape(9, -1, 1)
    taps = jnp.broadcast_to(taps, taps.shape[:2] + (pixels,))
    edges = jnp.pad(scaled[..., 2], ((0, 0), (0, 0), (0, 5))).reshape(-1, 24)
    edges = jnp.roll(jnp.pad(edges, ((0, 0), (0, pixels - 24))), -2, 1)
    near, far = stack_left(reference_rows), stack_left(far_rows)

    keep = functools.partial(pltpu.with_memory_space_constraint, memory_space=pltpu.HBM)
    taps, near, far = keep(taps), keep(near), keep(far)
    far_main, far_low, far_high = add_set(1, codes, arrived_far, note, far, taps, edges)
    other_main = send(far_main, perm=home)
    other_low = send(far_low, perm=[(i, j - 1) for i, j in home if j > 0])
    other_high = send(far_high, perm=[(i, j + 1) for i, j in home if j + 1 < views])
    own_main, own_low, own_high = add_set(0, codes, arrived_own, note, near, taps, edges)
    own_low = send(own_low, perm=[(i, i - 1) for i in range(1, views)])
    own_high = send(own_high, perm=[(i, i + 1) for i in range(views - 1)])
    return depth_rows(own_main, other_main, own_high, other_high, own_low, other_low)


def solution(mesh):
    in_specs = (
        P(("groups", "views"), None, None),
        P(("groups", "views"), None),
        P(("groups", "views")),
        P(("groups", "views")),
        P(("groups", "views"), None, None),
        P(),
    )
    out_specs = P(("groups", "views"), None)
    return jax.shard_map(compute, mesh=mesh, in_specs=in_specs, out_specs=out_specs, check_vma=False)
```

profile of v0, /device:TPU:7, one launch (start us, length us, event | category | flops | bytes accessed | tf_op | source)
XLA Modules:
  0.0 112.2 jit_solution(5837397253287486948)
XLA Ops:
  0.0 0.7 convert_bitcast_fusion.1
  0.7 0.7 convert_bitcast_fusion
  1.4 2.4 %collective-permute-start = (bf16[2,128]{1,0:T(2,128)(2,1)S(1)}, bf16[2,128]{1,0:T(2,128)(2,1)S(1)}, u32[]{:S(2)}, u32[]{:S(2)}) collective-permute-start(bf16[2,128]{1,0:T(2,128)(2,1)S(1)} %fusion.6), channel_id=1, source_target_pairs={{0,8},{1,9},{2,10},{3,11},{4,12},{5,13},{6,14},{7,15},{8,0},{9,1},... | collective-permute-start | bytes 1544 | tf_op jit(solution)/shard_map/ppermute | solution.py:327
  3.7 1.0 collective-permute-done
  4.8 1.2 %copy-done.3 = bf16[12,320,128]{2,1,0:T(8,128)(2,1)S(1)} copy-done((bf16[12,320,128]{2,1,0:T(8,128)(2,1)S(1)}, bf16[12,320,128]{2,1,0:T(8,128)(2,1)}, u32[]{:S(2)}) %copy-start.3) | copy-done | bytes 983064
  6.0 2.4 %pack_rows.1 = (bf16[8,656,128]{2,1,0:T(8,128)(2,1)S(1)}, bf16[8,640,128]{2,1,0:T(8,128)(2,1)S(1)}) custom-call(s32[12]{0:T(128)S(1)} %get-tuple-element.22.code_ref, bf16[12,320,128]{2,1,0:T(8,128)(2,1)S(1)} %copy-done.3, bf16[16,128]{1,0:T(8,128)(2,1)S(1)} %fusion.2.note_ref), custom_call_target="tpu_custom_call" | custom-call | tf_op jit(solution)/shard_map/pack_rows/pallas_call | solution.py:82
  8.4 22.6 %all_to_all.10.arrived_ref = bf16[8,656,128]{2,1,0:T(8,128)(2,1)S(1)} all-to-all(bf16[8,656,128]{2,1,0:T(8,128)(2,1)S(1)} %get-tuple-element.13), channel_id=1, replica_groups={{0,1,2,3,4,5,6,7},{8,9,10,11,12,13,14,15},{16,17,18,19,20,21,22,23},{24..., dimensions={0} | all-to-all | bytes 2686976 | tf_op jit(solution)/shard_map/all_to_all | solution.py:331
  31.0 5.1 %all-to-all-start.1 = ((bf16[8,640,128]{2,1,0:T(8,128)(2,1)}), bf16[8,640,128]{2,1,0:T(8,128)(2,1)S(1)}, u32[]{:S(2)}, u32[]{:S(2)}) async-start(bf16[8,640,128]{2,1,0:T(8,128)(2,1)} %copy-done), calls=%async_computation.1 | async-start | bytes 2621440 | tf_op jit(solution)/shard_map/all_to_all | solution.py:332
  36.1 2.4 %collective-permute-start.1 = (bf16[4,320,128]{2,1,0:T(8,128)(2,1)S(1)}, bf16[4,320,128]{2,1,0:T(8,128)(2,1)S(1)}, u32[]{:S(2)}, u32[]{:S(2)}) collective-permute-start(bf16[4,320,128]{2,1,0:T(8,128)(2,1)S(1)} %copy-done.4), channel_id=1, source_target_pairs={{0,8},{1,9},{2,10},{3,11},{4,12},{5,13},{6,14},{7,15},{8,0},{9,1},... | collective-permute-start | bytes 983048 | tf_op jit(solution)/shard_map/ppermute | solution.py:328
  38.5 0.5 stack_left.2.left_ref
  39.1 1.0 copy-done.1
  40.0 1.0 broadcast_in_dim.10
  41.0 1.3 %reshape.14 = f32[320,3,3,3]{0,3,2,1:T(4,128)S(1)} reshape(f32[40,8,3,3,3]{1,0,4,3,2:T(8,128)} %broadcast_in_dim.10) | data formatting | bytes 69120 | tf_op jit(solution)/shard_map/reshape | solution.py:336
  42.5 0.6 pad_bitcast_fusion
  43.1 0.9 copy.13
  44.0 0.1 pad_slice_fusion
  44.1 0.6 copy-done.5
  44.7 1.0 pad_maximum_fusion.edge_ref
  45.7 11.7 %collective-permute-done.1.reference_ref = bf16[4,320,128]{2,1,0:T(8,128)(2,1)S(1)} collective-permute-done((bf16[4,320,128]{2,1,0:T(8,128)(2,1)S(1)}, bf16[4,320,128]{2,1,0:T(8,128)(2,1)S(1)}, u32[]{:S(2)}, u32[]{:S(2)}) %collective-permute-start.1) | collective-permute-done | bytes 327712 | tf_op jit(solution)/shard_map/ppermute | solution.py:328
  57.4 0.5 stack_left.3.left_ref
  57.9 1.0 copy-done.2
  59.0 3.1 %broadcast_in_dim.12.weight_ref = f32[9,960,128]{2,1,0:T(8,128)} broadcast(f32[9,960]{1,0:T(8,128)S(1)} %broadcast_in_dim.11), dimensions={0,1} | broadcast | bytes 4458240 | tf_op jit(solution)/shard_map/broadcast_in_dim | solution.py:338
  62.1 12.0 %add_set.3 = (f32[4,96,128]{2,1,0:T(8,128)S(1)}, f32[1,96,128]{2,1,0:T(8,128)S(1)}, f32[1,96,128]{2,1,0:T(8,128)S(1)}) custom-call(s32[32]{0:T(128)S(1)} %reshape.16.code_ref, bf16[8,656,128]{2,1,0:T(8,128)(2,1)S(1)} %all_to_all.10.arrived_ref, bf16[8,16,128]{2,1,0:T(8,128)(2,1)S(1)} %slice.25.note_ref, bf16[4,128,960]{2,1,0:T(8,128)(2,1)} %copy-done.2, ...), custom_call_target="tpu_custom_call" | custom-call | flops 2264924160 | bytes 1310720 | tf_op jit(solution)/shard_map/add_set/pallas_call | solution.py:246
  74.1 3.2 %collective-permute-start.2 = (f32[4,96,128]{2,1,0:T(8,128)S(1)}, f32[4,96,128]{2,1,0:T(8,128)S(1)}, u32[]{:S(2)}, u32[]{:S(2)}) collective-permute-start(f32[4,96,128]{2,1,0:T(8,128)S(1)} %get-tuple-element.16), channel_id=1, source_target_pairs={{0,8},{1,9},{2,10},{3,11},{4,12},{5,13},{6,14},{7,15},{8,0},{9,1},... | collective-permute-start | bytes 589832 | tf_op jit(solution)/shard_map/ppermute | solution.py:346
  77.3 11.8 %add_set.2 = (f32[4,96,128]{2,1,0:T(8,128)S(1)}, f32[1,96,128]{2,1,0:T(8,128)S(1)}, f32[1,96,128]{2,1,0:T(8,128)S(1)}) custom-call(s32[32]{0:T(128)S(1)} %reshape.16.code_ref, bf16[8,640,128]{2,1,0:T(8,128)(2,1)S(1)} %all-to-all-done.1.arrived_ref, bf16[8,16,128]{2,1,0:T(8,128)(2,1)S(1)} %slice.25.note_ref, bf16[4,128,960]{2,1,0:T(8,128)(2,1)} %copy-done.1, ...), custom_call_target="tpu_custom_call" | custom-call | flops 2264924160 | bytes 1310720 | tf_op jit(solution)/shard_map/add_set/pallas_call | solution.py:246
  89.0 3.9 %collective-permute-start.3 = (f32[1,96,128]{2,1,0:T(8,128)S(1)}, f32[1,96,128]{2,1,0:T(8,128)S(1)}, u32[]{:S(2)}, u32[]{:S(2)}) collective-permute-start(f32[1,96,128]{2,1,0:T(8,128)S(1)} %get-tuple-element.17), channel_id=1, source_target_pairs={{0,1},{1,2},{2,3},{3,4},{4,5},{5,6},{6,7},{7,8},{8,9},{9,10},{10,1... | collective-permute-start | bytes 147464 | tf_op jit(solution)/shard_map/ppermute | solution.py:351
  93.0 7.9 %collective-permute-start.4 = (f32[1,96,128]{2,1,0:T(8,128)S(1)}, f32[1,96,128]{2,1,0:T(8,128)S(1)}, u32[]{:S(2)}, u32[]{:S(2)}) collective-permute-start(f32[1,96,128]{2,1,0:T(8,128)S(1)} %get-tuple-element.18), channel_id=1, source_target_pairs={{0,9},{1,10},{2,11},{3,12},{4,13},{5,14},{6,15},{8,1},{9,2},{10,3}... | collective-permute-start | bytes 147464 | tf_op jit(solution)/shard_map/ppermute | solution.py:348
  100.9 1.9 %collective-permute-start.5 = (f32[1,96,128]{2,1,0:T(8,128)S(1)}, f32[1,96,128]{2,1,0:T(8,128)S(1)}, u32[]{:S(2)}, u32[]{:S(2)}) collective-permute-start(f32[1,96,128]{2,1,0:T(8,128)S(1)} %get-tuple-element.19), channel_id=1, source_target_pairs={{1,0},{2,1},{3,2},{4,3},{5,4},{6,5},{7,6},{8,7},{9,8},{10,9},{11,1... | collective-permute-start | bytes 147464 | tf_op jit(solution)/shard_map/ppermute | solution.py:350
  102.8 1.9 %collective-permute-start.6 = (f32[1,96,128]{2,1,0:T(8,128)S(1)}, f32[1,96,128]{2,1,0:T(8,128)S(1)}, u32[]{:S(2)}, u32[]{:S(2)}) collective-permute-start(f32[1,96,128]{2,1,0:T(8,128)S(1)} %get-tuple-element.20), channel_id=1, source_target_pairs={{0,7},{1,8},{2,9},{3,10},{4,11},{5,12},{6,13},{7,14},{9,0},{10,1},... | collective-permute-start | bytes 147464 | tf_op jit(solution)/shard_map/ppermute | solution.py:347
  104.8 2.4 %collective-permute-done.5.after_ref = f32[1,96,128]{2,1,0:T(8,128)S(1)} collective-permute-done((f32[1,96,128]{2,1,0:T(8,128)S(1)}, f32[1,96,128]{2,1,0:T(8,128)S(1)}, u32[]{:S(2)}, u32[]{:S(2)}) %collective-permute-start.5) | collective-permute-done | bytes 49184 | tf_op jit(solution)/shard_map/ppermute | solution.py:350
  107.2 4.2 %collective-permute-done.6.after_far_ref = f32[1,96,128]{2,1,0:T(8,128)S(1)} collective-permute-done((f32[1,96,128]{2,1,0:T(8,128)S(1)}, f32[1,96,128]{2,1,0:T(8,128)S(1)}, u32[]{:S(2)}, u32[]{:S(2)}) %collective-permute-start.6) | collective-permute-done | bytes 49184 | tf_op jit(solution)/shard_map/ppermute | solution.py:347
  111.5 0.7 depth_rows.1
  (23 shorter events, 0.3 us)
Async XLA Ops:
  1.4 3.4 %collective-permute-start = (bf16[2,128]{1,0:T(2,128)(2,1)S(1)}, bf16[2,128]{1,0:T(2,128)(2,1)S(1)}, u32[]{:S(2)}, u32[]{:S(2)}) collective-permute-start(bf16[2,128]{1,0:T(2,128)(2,1)S(1)} %fusion.6), channel_id=1, source_target_pairs={{0,8},{1,9},{2,10},{3,11},{4,12},{5,13},{6,14},{7,15},{8,0},{9,1},... | collective-permute-start | bytes 1544 | tf_op jit(solution)/shard_map/ppermute | solution.py:327
  4.8 1.2 %copy-start.3 = (bf16[12,320,128]{2,1,0:T(8,128)(2,1)S(1)}, bf16[12,320,128]{2,1,0:T(8,128)(2,1)}, u32[]{:S(2)}) copy-start(bf16[12,320,128]{2,1,0:T(8,128)(2,1)} %source_ref.1) | copy-start | bytes 2949124
  8.4 22.7 %copy-start = (bf16[8,640,128]{2,1,0:T(8,128)(2,1)}, bf16[8,640,128]{2,1,0:T(8,128)(2,1)S(1)}, u32[]{:S(2)}) copy-start(bf16[8,640,128]{2,1,0:T(8,128)(2,1)S(1)} %get-tuple-element.14) | copy-start | bytes 3932164
  31.0 5.1 %copy-start.4 = (bf16[4,320,128]{2,1,0:T(8,128)(2,1)S(1)}, bf16[4,320,128]{2,1,0:T(8,128)(2,1)}, u32[]{:S(2)}) copy-start(bf16[4,320,128]{2,1,0:T(8,128)(2,1)} %reference_ref.1) | copy-start | bytes 983044
  31.0 46.3 %all-to-all-start.1 = ((bf16[8,640,128]{2,1,0:T(8,128)(2,1)}), bf16[8,640,128]{2,1,0:T(8,128)(2,1)S(1)}, u32[]{:S(2)}, u32[]{:S(2)}) async-start(bf16[8,640,128]{2,1,0:T(8,128)(2,1)} %copy-done), calls=%async_computation.1 | async-start | bytes 2621440 | tf_op jit(solution)/shard_map/all_to_all | solution.py:332
  36.1 3.9 %copy-start.6 = (f32[40,3,3,3]{0,3,2,1:T(4,128)S(1)}, f32[40,3,3,3]{0,3,2,1:T(4,128)}, u32[]{:S(2)}) copy-start(f32[40,3,3,3]{0,3,2,1:T(4,128)} %param.11) | copy-start | bytes 12964
  36.1 21.3 %collective-permute-start.1 = (bf16[4,320,128]{2,1,0:T(8,128)(2,1)S(1)}, bf16[4,320,128]{2,1,0:T(8,128)(2,1)S(1)}, u32[]{:S(2)}, u32[]{:S(2)}) collective-permute-start(bf16[4,320,128]{2,1,0:T(8,128)(2,1)S(1)} %copy-done.4), channel_id=1, source_target_pairs={{0,8},{1,9},{2,10},{3,11},{4,12},{5,13},{6,14},{7,15},{8,0},{9,1},... | collective-permute-start | bytes 983048 | tf_op jit(solution)/shard_map/ppermute | solution.py:328
  39.0 1.0 copy-start.1
  44.0 0.7 copy-start.5
  57.9 1.0 copy-start.2
  74.1 37.3 %collective-permute-start.2 = (f32[4,96,128]{2,1,0:T(8,128)S(1)}, f32[4,96,128]{2,1,0:T(8,128)S(1)}, u32[]{:S(2)}, u32[]{:S(2)}) collective-permute-start(f32[4,96,128]{2,1,0:T(8,128)S(1)} %get-tuple-element.16), channel_id=1, source_target_pairs={{0,8},{1,9},{2,10},{3,11},{4,12},{5,13},{6,14},{7,15},{8,0},{9,1},... | collective-permute-start | bytes 589832 | tf_op jit(solution)/shard_map/ppermute | solution.py:346
  89.0 15.7 %collective-permute-start.3 = (f32[1,96,128]{2,1,0:T(8,128)S(1)}, f32[1,96,128]{2,1,0:T(8,128)S(1)}, u32[]{:S(2)}, u32[]{:S(2)}) collective-permute-start(f32[1,96,128]{2,1,0:T(8,128)S(1)} %get-tuple-element.17), channel_id=1, source_target_pairs={{0,1},{1,2},{2,3},{3,4},{4,5},{5,6},{6,7},{7,8},{8,9},{9,10},{10,1... | collective-permute-start | bytes 147464 | tf_op jit(solution)/shard_map/ppermute | solution.py:351
  93.0 11.8 %collective-permute-start.4 = (f32[1,96,128]{2,1,0:T(8,128)S(1)}, f32[1,96,128]{2,1,0:T(8,128)S(1)}, u32[]{:S(2)}, u32[]{:S(2)}) collective-permute-start(f32[1,96,128]{2,1,0:T(8,128)S(1)} %get-tuple-element.18), channel_id=1, source_target_pairs={{0,9},{1,10},{2,11},{3,12},{4,13},{5,14},{6,15},{8,1},{9,2},{10,3}... | collective-permute-start | bytes 147464 | tf_op jit(solution)/shard_map/ppermute | solution.py:348
  100.9 6.3 %collective-permute-start.5 = (f32[1,96,128]{2,1,0:T(8,128)S(1)}, f32[1,96,128]{2,1,0:T(8,128)S(1)}, u32[]{:S(2)}, u32[]{:S(2)}) collective-permute-start(f32[1,96,128]{2,1,0:T(8,128)S(1)} %get-tuple-element.19), channel_id=1, source_target_pairs={{1,0},{2,1},{3,2},{4,3},{5,4},{6,5},{7,6},{8,7},{9,8},{10,9},{11,1... | collective-permute-start | bytes 147464 | tf_op jit(solution)/shard_map/ppermute | solution.py:350
  102.8 8.6 %collective-permute-start.6 = (f32[1,96,128]{2,1,0:T(8,128)S(1)}, f32[1,96,128]{2,1,0:T(8,128)S(1)}, u32[]{:S(2)}, u32[]{:S(2)}) collective-permute-start(f32[1,96,128]{2,1,0:T(8,128)S(1)} %get-tuple-element.20), channel_id=1, source_target_pairs={{0,7},{1,8},{2,9},{3,10},{4,11},{5,12},{6,13},{7,14},{9,0},{10,1},... | collective-permute-start | bytes 147464 | tf_op jit(solution)/shard_map/ppermute | solution.py:347
where the time goes:
time: 113 us; the launch traced here: 112 us
  starting transfers between devices  28.7 us (25%)
  Pallas kernels  27.9 us (25%)
  blocking collectives  22.6 us (20%)
  waiting for transfers between devices  19.4 us (17%)
  local copies, waits for them, and re-layouts  10.9 us (10%)
  other arithmetic  2.42 us (2%)
    pallas_call x2, Pallas kernels, add_set(): pl.pallas_call(functools.partial(set_kernel, t), grid=(weight.shape[0],),...  23.7 us
    all_to_all x1, blocking collectives, compute(): arrived_far = swap(packed_far)  22.6 us
    ppermute x1, waiting for transfers between devices, compute(): far_rows = send(reference_rows, perm=home)  11.7 us
    ppermute x1, starting transfers between devices, compute(): send(far_high, perm=[(i, j + 1) for i, j in home if j + 1 < views])  7.92 us
    all_to_all x1, starting transfers between devices, compute(): arrived_own = swap(packed_own)  5.12 us
    ppermute x1, waiting for transfers between devices, compute(): other_low = send(far_low, perm=[(i, j - 1) for i, j in home if j > 0])  4.23 us
    ppermute x1, starting transfers between devices, compute(): own_high = send(own_high, perm=[(i, i + 1) for i in range(views - 1)])  3.94 us
    unnamed x15, local copies, waits for them, and re-layouts  3.7 us
  transfers between devices with their start and end apart: 8, of which 4 were waited for; matrix products, arithmetic and copies ran while one was open for 7% of the time, Pallas kernels for 22%

commit v1 on v0

v1 whole, which is shorter than its diff:
```python
import functools

import jax
import jax.numpy as jnp
from jax import lax
from jax.experimental import pallas as pl
from jax.experimental.pallas import tpu as pltpu
from jax.sharding import PartitionSpec as P


CG = 8
DISP = 96
DSPAN = 16
CAP = 2
SETS = 2

VMEM = pl.BlockSpec(memory_space=pltpu.VMEM)
SMEM = pl.BlockSpec(memory_space=pltpu.SMEM)
ANY = pl.BlockSpec(memory_space=pl.ANY)


def pack_kernel(
    half, span, code_ref, source_ref, note_ref, far_ref, *rest
):
    own_refs = rest[:-4]
    count_ref, slot_ref, block_ref, sem = rest[-4:]
    items, channels, pixels = source_ref.shape
    side = lax.div(lax.axis_index("views"), half)
    here = lax.rem(lax.axis_index("views"), half)
    lane = lax.broadcasted_iota(jnp.int32, (1, pixels), 1)
    slot_ref[...] = jnp.full_like(slot_ref, -1.0)

    @pl.loop(0, SETS * half)
    def _(j):
        count_ref[j] = 0

    @pl.loop(0, items)
    def _(i):
        owner = lax.div(code_ref[i], span)
        rest = lax.rem(code_ref[i], span)
        home = lax.rem(owner, half)
        for t in range(SETS):

            @pl.when((lax.div(owner, half) == side) == (t == 0))
            def _():
                place = count_ref[t * half + home]
                count_ref[t * half + home] = place + 1
                first = pl.multiple_of(place * channels, channels)
                if t == 0 and len(own_refs) > 1:
                    for k, own_ref in enumerate(own_refs):

                        @pl.when(home == here ^ k)
                        def _():
                            target = own_ref.at[pl.ds(first, channels), :]
                            pltpu.make_async_copy(source_ref.at[i], target, sem).start()
                else:
                    target = (own_refs[0], far_ref)[t].at[home, pl.ds(first, channels), :]
                    pltpu.make_async_copy(source_ref.at[i], target, sem).start()
                value = jnp.full((1, pixels), rest.astype(jnp.float32))
                line = slot_ref[pl.ds(home, 1), :]
                slot_ref[pl.ds(home, 1), :] = jnp.where(lane == t * CAP + place, value, line)

    height = note_ref.shape[0]
    row = lax.broadcasted_iota(jnp.int32, (height, pixels), 0)
    note = note_ref[...].astype(jnp.float32)

    @pl.loop(0, half)
    def _(j):
        line = jnp.broadcast_to(slot_ref[pl.ds(j, 1), :], (height, pixels))
        block_ref[j] = jnp.where(row == 4, line, note).astype(block_ref.dtype)

    last = pltpu.make_async_copy(
        block_ref, far_ref.at[:, pl.ds(CAP * channels, height), :], sem
    )
    last.start()

    @pl.loop(0, items)
    def _(i):
        pltpu.make_async_copy(
            source_ref.at[0], far_ref.at[0, pl.ds(0, channels), :], sem
        ).wait()

    last.wait()


def pack_rows(codes, source, note, half, span, apart):
    _, channels, pixels = source.shape
    height = note.shape[0]
    length = CAP * channels
    shapes = [(half, length + height, pixels)]
    shapes += [(length, pixels)] * half if apart else [(half, length, pixels)]
    return pl.pallas_call(
        functools.partial(pack_kernel, half, span),
        out_shape=[jax.ShapeDtypeStruct(shape, source.dtype) for shape in shapes],
        in_specs=[SMEM, VMEM, VMEM],
        out_specs=[ANY] * len(shapes),
        scratch_shapes=[
            pltpu.SMEM((SETS * half,), jnp.int32),
            pltpu.VMEM((half, pixels), jnp.float32),
            pltpu.VMEM((half, height, pixels), source.dtype),
            pltpu.SemaphoreType.DMA,
        ],
        compiler_params=pltpu.CompilerParams(vmem_limit_bytes=16 << 20),
        name="pack_rows",
    )(codes, source, note)


def split_two(values):
    high = values.astype(jnp.bfloat16)
    return high, (values - high.astype(jnp.float32)).astype(jnp.bfloat16)


def both_parts(values):
    return jnp.concatenate(split_two(values), axis=1)


def shift_left(values, offset):
    lane = lax.broadcasted_iota(jnp.int32, values.shape, 1)
    pixels = values.shape[1]
    moved = pltpu.roll(values, (-offset) % pixels, 1)
    return jnp.where((lane + offset >= 0) & (lane + offset < pixels), moved, 0.0)


def left_kernel(reference_ref, left_ref):
    rows, channels, pixels = reference_ref.shape
    i = lax.broadcasted_iota(jnp.int32, (pixels, pixels), 0)
    x = lax.broadcasted_iota(jnp.int32, (pixels, pixels), 1)
    for e in range(3):
        pick = jnp.where(x == pixels - 1 - i + (e - 1), 1.0, 0.0).astype(jnp.bfloat16)
        for r in range(rows):
            moved = lax.dot_general(
                pick,
                reference_ref[r],
                (((1,), (1,)), ((), ())),
                preferred_element_type=jnp.float32,
            )
            left_ref[r, :, e * channels : (e + 1) * channels] = moved.astype(left_ref.dtype)


def stack_left(reference):
    rows, channels, pixels = reference.shape
    return pl.pallas_call(
        left_kernel,
        out_shape=jax.ShapeDtypeStruct((rows, pixels, 3 * channels), reference.dtype),
        in_specs=[VMEM],
        out_specs=VMEM,
        compiler_params=pltpu.CompilerParams(vmem_limit_bytes=8 << 20),
        name="stack_left",
    )(reference)


def set_kernel(
    t, code_ref, note_ref, left_ref, weight_ref, edge_ref, *rest
):
    arrived_refs = rest[:-7]
    main_ref, least_ref, most_ref, stack_ref, wide_ref, total_ref, canvas_ref = rest[-7:]
    rows, channels, pixels = canvas_ref.shape
    half = note_ref.shape[0]
    lane = lax.broadcasted_iota(jnp.int32, (channels, pixels), 1)
    canvas_ref[...] = jnp.zeros_like(canvas_ref)
    owner = lax.rem(lax.axis_index("views") + t * half, SETS * half)
    counts = [0.0] * rows
    for first in (0, 2):
        named = note_ref[:, first, :].astype(jnp.float32).astype(jnp.int32) == owner
        row = lax.div(note_ref[:, first + 1, :].astype(jnp.float32).astype(jnp.int32), DSPAN)
        for r in range(rows):
            counts[r] = counts[r] + jnp.where(named & (row == r), 1.0, 0.0)
    counts = [1.0 / jnp.full((8, pixels), jnp.maximum(jnp.sum(c), 1.0)) for c in counts]

    def add_slots(home, arrived):
        for place in range(CAP):
            code = code_ref[home * (SETS * CAP) + t * CAP + place]

            @pl.when(code >= 0)
            def _():
                row = lax.div(code, DSPAN)
                begin = lax.rem(code, DSPAN)
                part = arrived[place * channels : (place + 1) * channels, :]
                moved = pltpu.roll(part.astype(jnp.float32), begin, 1)
                canvas_ref[row] = canvas_ref[row] + jnp.where(lane >= begin, moved, 0.0)

    if len(arrived_refs) > 1:
        for k, arrived_ref in enumerate(arrived_refs):
            add_slots(lax.rem(lax.axis_index("views"), half) ^ k, arrived_ref)
    else:

        @pl.loop(0, half)
        def _(home):
            add_slots(home, arrived_refs[0].at[home])

    for r in range(rows):
        mean = canvas_ref[r] * jnp.concatenate([counts[r]] * (channels // 8), axis=0)
        for e in range(3):
            stack_ref[r, e * channels : (e + 1) * channels, :] = shift_left(mean, e - 1)
        edge = jnp.broadcast_to(mean[:, :1], (channels, pixels)) * edge_ref[...]
        wide = jnp.dot(
            left_ref[r, :, 2 * channels :], both_parts(edge), preferred_element_type=jnp.float32
        )
        total_ref[(rows + 2) * 3 + r] = wide[:, :pixels] + wide[:, pixels:]

    done = set()
    for tap in range(9):
        wide_ref[...] = jnp.broadcast_to(weight_ref[:, tap : tap + 1], wide_ref.shape)
        for r in range(rows):
            right = both_parts(stack_ref[r] * wide_ref[...])
            wide = jnp.dot(left_ref[r], right, preferred_element_type=jnp.float32)
            part = wide[:, :pixels] + wide[:, pixels:]
            place = (r + 2 - tap // 3) * 3 + tap % 3
            total_ref[place] = total_ref[place] + part if place in done else part
            done.add(place)

    x = pixels - 1 - lax.broadcasted_iota(jnp.int32, (pixels, pixels), 0)
    v = lax.broadcasted_iota(jnp.int32, (pixels, pixels), 1)
    inside = (x >= v) & (x - v < DISP)
    border = (x < DISP - 1) & ((v >= pixels - 2) | (v < 1))
    for r in range(rows + 2):
        total = jnp.where(inside, total_ref[3 * r + 1], 0.0)
        for b in (0, 2):
            kept = jnp.where(inside, total_ref[3 * r + b], 0.0)
            total = total + pltpu.roll(kept, (b - 1) % pixels, 1)
        for a in range(3):
            if 0 <= r + a - 2 < rows:
                edge = total_ref[(rows + 2) * 3 + r + a - 2]
                moved = pltpu.roll(edge, (-8 * a) % pixels, 1) if a else edge
                total = total + jnp.where(border, moved, 0.0)
        total = pltpu.roll(total, 0, 1, stride=1, stride_axis=0)
        kept = total.T[pixels - DISP :]
        if r == 0:
            least_ref[0] = kept
        elif r == rows + 1:
            most_ref[0] = kept
        else:
            main_ref[r - 1] = kept


def add_set(t, codes, note, left, weight, edge, *arrived):
    rows, pixels, depth = left.shape
    channels = depth // 3
    shapes = [(n, DISP, pixels) for n in (rows, 1, 1)]
    return pl.pallas_call(
        functools.partial(set_kernel, t),
        out_shape=[jax.ShapeDtypeStruct(shape, jnp.float32) for shape in shapes],
        in_specs=[SMEM] + [VMEM] * (4 + len(arrived)),
        out_specs=[VMEM] * 3,
        scratch_shapes=[
            pltpu.VMEM((rows, depth, pixels), jnp.float32),
            pltpu.VMEM((depth, pixels), jnp.float32),
            pltpu.VMEM(((rows + 2) * 3 + rows, pixels, pixels), jnp.float32),
            pltpu.VMEM((rows, channels, pixels), jnp.float32),
        ],
        compiler_params=pltpu.CompilerParams(
            vmem_limit_bytes=(11 << 20) + sum(2 * part.size for part in arrived)
        ),
        cost_estimate=pl.CostEstimate(
            flops=2 * rows * 9 * pixels * 2 * pixels * depth,
            bytes_accessed=2 * sum(part.size for part in arrived),
            transcendentals=0,
        ),
        name="add_set",
    )(codes, note, left, weight, edge, *arrived)


def depth_kernel(own_ref, far_ref, before_ref, before_far_ref, after_ref, after_far_ref, out_ref):
    rows, pixels = out_ref.shape
    level = (DISP - 1) - lax.broadcasted_iota(jnp.int32, (DISP, pixels), 0)
    share = level.astype(jnp.float32) / DISP
    depths = []
    for r in range(rows):
        scores = own_ref[r] + far_ref[r]
        if r == 0:
            scores = scores + (before_ref[0] + before_far_ref[0])
        if r == rows - 1:
            scores = scores + (after_ref[0] + after_far_ref[0])
        weights = jnp.exp(scores - jnp.max(scores, axis=0, keepdims=True))
        bottom = jnp.sum(weights, axis=0, keepdims=True)
        depths.append(jnp.sum(weights * share, axis=0, keepdims=True) / bottom)
    lane = lax.broadcasted_iota(jnp.int32, (8, pixels), 1)
    depth = jnp.concatenate(depths + [depths[0]] * (-rows % 8), axis=0)
    out_ref[...] = jnp.take_along_axis(depth, pixels - 1 - lane, axis=1)[:rows]


def depth_rows(*parts):
    rows, _, pixels = parts[0].shape
    return pl.pallas_call(
        depth_kernel,
        out_shape=jax.ShapeDtypeStruct((rows, pixels), jnp.float32),
        in_specs=[VMEM] * len(parts),
        out_specs=VMEM,
        compiler_params=pltpu.CompilerParams(vmem_limit_bytes=4 << 20),
        name="depth_rows",
    )(*parts)


def compute(source_rows, route_owner, target_row, start_index, reference_rows, conv_weight):
    views = lax.axis_size("views")
    half = views // 2
    rows, channels, pixels = reference_rows.shape
    span = rows * DSPAN
    send = functools.partial(lax.ppermute, axis_name="views")
    home = [(i, (i + half) % views) for i in range(views)]
    groups = [list(range(half)), list(range(half, views))]
    swap = functools.partial(
        lax.all_to_all,
        axis_name="views",
        split_axis=0,
        concat_axis=0,
        tiled=True,
        axis_index_groups=groups,
    )
    owner = route_owner[:, 0]
    rest = target_row * DSPAN + start_index
    named = jnp.stack([owner, rest]).astype(jnp.bfloat16)
    named = jnp.pad(named, ((0, 0), (0, pixels - named.shape[1])), constant_values=-1)
    far_named = send(named, perm=home)
    far_rows = send(reference_rows, perm=home)
    note = jnp.pad(jnp.concatenate([named, far_named]), ((0, 12), (0, 0)))
    apart = half <= 8
    packed_far, *packed_own = pack_rows(
        owner * span + rest, source_rows, note, half, span, apart
    )
    arrived_far = swap(packed_far)
    if apart:
        arrived_own = packed_own[:1] + [None] * (half - 1)
        for k in sorted(range(1, half), key=lambda k: (k < half // 2, -k % 2, -k)):
            arrived_own[k] = send(packed_own[k], perm=[(i, i ^ k) for i in range(views)])
    else:
        arrived_own = [swap(packed_own[0])]
    note = arrived_far[:, CAP * channels :]
    codes = note[:, 4, : SETS * CAP].astype(jnp.int32).reshape(-1)

    scaled = jnp.repeat(conv_weight / CG, CG, axis=0)
    taps = scaled.transpose(3, 0, 1, 2).reshape(-1, 9)
    taps = jnp.pad(taps, ((0, 0), (0, pixels - 9)))
    edges = jnp.pad(scaled[..., 2], ((0, 0), (0, 0), (0, 5))).reshape(-1, 24)
    edges = jnp.roll(jnp.pad(edges, ((0, 0), (0, pixels - 24))), -2, 1)
    near, far = stack_left(reference_rows), stack_left(far_rows)
    far_main, far_low, far_high = add_set(1, codes, note, far, taps, edges, arrived_far)
    other_main = send(far_main, perm=home)
    other_low = send(far_low, perm=[(i, j - 1) for i, j in home if j > 0])
    other_high = send(far_high, perm=[(i, j + 1) for i, j in home if j + 1 < views])
    own_main, own_low, own_high = add_set(0, codes, note, near, taps, edges, *arrived_own)
    own_low = send(own_low, perm=[(i, i - 1) for i in range(1, views)])
    own_high = send(own_high, perm=[(i, i + 1) for i in range(views - 1)])
    return depth_rows(own_main, other_main, own_high, other_high, own_low, other_low)


def solution(mesh):
    in_specs = (
        P(("groups", "views"), None, None),
        P(("groups", "views"), None),
        P(("groups", "views")),
        P(("groups", "views")),
        P(("groups", "views"), None, None),
        P(),
    )
    out_specs = P(("groups", "views"), None)
    return jax.shard_map(compute, mesh=mesh, in_specs=in_specs, out_specs=out_specs, check_vma=False)
```

time: 113 us -> 83.3 us (0.74)
  the two profiles are of different devices: /device:TPU:7 before, /device:TPU:1 now
where the time goes in v1:
time: 83.3 us; the launch traced here: 82.8 us
  starting transfers between devices  35.9 us (43%)
  waiting for transfers between devices  18.2 us (22%)
  Pallas kernels  16.1 us (19%)
  local copies, waits for them, and re-layouts  10.2 us (12%)
  other arithmetic  2.17 us (3%)
    pallas_call x2, Pallas kernels, add_set(): pl.pallas_call(functools.partial(set_kernel, t), out_shape=[jax.ShapeDtyp...  12.4 us
    ppermute x1, waiting for transfers between devices, compute(): far_rows = send(reference_rows, perm=home)  11.3 us
    ppermute x7, starting transfers between devices, compute(): send(packed_own[k], perm=[(i, i ^ k) for i in range(views)])  10.7 us
    unnamed x25, local copies, waits for them, and re-layouts  6.82 us
    ppermute x1, starting transfers between devices, compute(): send(far_high, perm=[(i, j + 1) for i, j in home if j + 1 < views])  5.97 us
    all_to_all x1, starting transfers between devices, compute(): arrived_far = swap(packed_far)  5.96 us
    ppermute x1, waiting for transfers between devices, compute(): other_low = send(far_low, perm=[(i, j - 1) for i, j in home if j > 0])  4.95 us
    ppermute x1, starting transfers between devices, compute(): own_high = send(own_high, perm=[(i, i + 1) for i in range(views - 1)])  3.98 us
  transfers between devices with their start and end apart: 15, of which 5 were waited for; matrix products, arithmetic and copies ran while one was open for 5% of the time, Pallas kernels for 16%

profile of v1, /device:TPU:1, one launch (start us, length us, event | category | flops | bytes accessed | tf_op | source)
XLA Modules:
  0.0 82.8 jit_solution(12072825167482144321)
XLA Ops:
  0.0 0.7 convert_bitcast_fusion.1
  0.7 0.7 convert_bitcast_fusion
  1.4 3.2 %collective-permute-start = (bf16[2,128]{1,0:T(2,128)(2,1)S(1)}, bf16[2,128]{1,0:T(2,128)(2,1)S(1)}, u32[]{:S(2)}, u32[]{:S(2)}) collective-permute-start(bf16[2,128]{1,0:T(2,128)(2,1)S(1)} %fusion.6), channel_id=1, source_target_pairs={{0,8},{1,9},{2,10},{3,11},{4,12},{5,13},{6,14},{7,15},{8,0},{9,1},... | collective-permute-start | bytes 1544 | tf_op jit(solution)/shard_map/ppermute | solution.py:314
  4.6 1.0 %collective-permute-done = bf16[2,128]{1,0:T(2,128)(2,1)S(1)} collective-permute-done((bf16[2,128]{1,0:T(2,128)(2,1)S(1)}, bf16[2,128]{1,0:T(2,128)(2,1)S(1)}, u32[]{:S(2)}, u32[]{:S(2)}) %collective-permute-start) | collective-permute-done | bytes 544 | tf_op jit(solution)/shard_map/ppermute | solution.py:314
  5.5 1.2 %copy-done = bf16[12,320,128]{2,1,0:T(8,128)(2,1)S(1)} copy-done((bf16[12,320,128]{2,1,0:T(8,128)(2,1)S(1)}, bf16[12,320,128]{2,1,0:T(8,128)(2,1)}, u32[]{:S(2)}) %copy-start) | copy-done | bytes 983064
  6.7 1.9 %pack_rows.1 = (bf16[8,656,128]{2,1,0:T(8,128)(2,1)}, bf16[640,128]{1,0:T(8,128)(2,1)S(1)}, bf16[640,128]{1,0:T(8,128)(2,1)}, bf16[640,128]{1,0:T(8,128)(2,1)}, ...) custom-call(s32[12]{0:T(128)S(1)} %get-tuple-element.36.code_ref, ...), custom_call_target="tpu_custom_call" | custom-call | tf_op jit(solution)/shard_map/pack_rows/pallas_call | solution.py:92
  8.6 0.7 copy-done.7
  9.9 0.7 copy-done.10
  10.6 6.0 %all-to-all-start = ((bf16[8,656,128]{2,1,0:T(8,128)(2,1)}), bf16[8,656,128]{2,1,0:T(8,128)(2,1)S(1)}, u32[]{:S(2)}, u32[]{:S(2)}) async-start(bf16[8,656,128]{2,1,0:T(8,128)(2,1)} %get-tuple-element.20), calls=%async_computation | async-start | bytes 2686976 | tf_op jit(solution)/shard_map/all_to_all | solution.py:321
  16.6 2.2 %collective-permute-start.8 = (bf16[4,320,128]{2,1,0:T(8,128)(2,1)S(1)}, bf16[4,320,128]{2,1,0:T(8,128)(2,1)S(1)}, u32[]{:S(2)}, u32[]{:S(2)}) collective-permute-start(bf16[4,320,128]{2,1,0:T(8,128)(2,1)S(1)} %copy-done.3), channel_id=1, source_target_pairs={{0,8},{1,9},{2,10},{3,11},{4,12},{5,13},{6,14},{7,15},{8,0},{9,1},... | collective-permute-start | bytes 983048 | tf_op jit(solution)/shard_map/ppermute | solution.py:315
  19.9 1.7 %collective-permute-start.2 = (bf16[640,128]{1,0:T(8,128)(2,1)}, bf16[640,128]{1,0:T(8,128)(2,1)}, u32[]{:S(2)}, u32[]{:S(2)}) collective-permute-start(bf16[640,128]{1,0:T(8,128)(2,1)} %get-tuple-element.23), channel_id=1, source_target_pairs={{0,2},{1,3},{2,0},{3,1},{4,6},{5,7},{6,4},{7,5},{8,10},{9,11},{10,... | collective-permute-start | bytes 491528 | tf_op jit(solution)/shard_map/ppermute | solution.py:325
  21.6 0.8 pad_maximum_fusion.edge_ref
  22.9 0.7 reshape.16
  23.6 1.0 %copy.13 = f32[960,9]{1,0:T(8,128)S(1)} copy(f32[960,9]{0,1:T(8,128)} %reshape.16) | data formatting | bytes 69120 | tf_op jit(solution)/shard_map/reshape | solution.py:332
  24.7 0.8 %pad.22.weight_ref = f32[960,128]{1,0:T(8,128)} pad(f32[960,9]{1,0:T(8,128)S(1)} %copy.13, f32[]{:T(128)} %constant.14.clone.1), padding=0_0x0_119 | pad | bytes 526084 | tf_op jit(solution)/shard_map/jit(_pad)/pad | solution.py:333
  25.6 1.6 %collective-permute-start.4 = (bf16[640,128]{1,0:T(8,128)(2,1)}, bf16[640,128]{1,0:T(8,128)(2,1)}, u32[]{:S(2)}, u32[]{:S(2)}) collective-permute-start(bf16[640,128]{1,0:T(8,128)(2,1)} %get-tuple-element.25), channel_id=1, source_target_pairs={{0,4},{1,5},{2,6},{3,7},{4,0},{5,1},{6,2},{7,3},{8,12},{9,13},{10,... | collective-permute-start | bytes 491528 | tf_op jit(solution)/shard_map/ppermute | solution.py:325
  27.2 11.3 %collective-permute-done.8.reference_ref = bf16[4,320,128]{2,1,0:T(8,128)(2,1)S(1)} collective-permute-done((bf16[4,320,128]{2,1,0:T(8,128)(2,1)S(1)}, bf16[4,320,128]{2,1,0:T(8,128)(2,1)S(1)}, u32[]{:S(2)}, u32[]{:S(2)}) %collective-permute-start.8) | collective-permute-done | bytes 327712 | tf_op jit(solution)/shard_map/ppermute | solution.py:315
  38.5 0.7 copy-done.4
  39.3 5.3 %collective-permute-start.5 = (bf16[640,128]{1,0:T(8,128)(2,1)}, bf16[640,128]{1,0:T(8,128)(2,1)}, u32[]{:S(2)}, u32[]{:S(2)}) collective-permute-start(bf16[640,128]{1,0:T(8,128)(2,1)} %get-tuple-element.26), channel_id=1, source_target_pairs={{0,5},{1,4},{2,7},{3,6},{4,1},{5,0},{6,3},{7,2},{8,13},{9,12},{10,... | collective-permute-start | bytes 491528 | tf_op jit(solution)/shard_map/ppermute | solution.py:325
  44.6 1.0 %copy-done.5 = bf16[4,320,128]{2,1,0:T(8,128)(2,1)S(1)} copy-done((bf16[4,320,128]{2,1,0:T(8,128)(2,1)S(1)}, bf16[4,320,128]{2,1,0:T(8,128)(2,1)}, u32[]{:S(2)}) %copy-start.5) | copy-done | bytes 327704
  46.3 1.5 %collective-permute-start.7 = (bf16[640,128]{1,0:T(8,128)(2,1)}, bf16[640,128]{1,0:T(8,128)(2,1)S(1)}, u32[]{:S(2)}, u32[]{:S(2)}) collective-permute-start(bf16[640,128]{1,0:T(8,128)(2,1)} %copy-done.9), channel_id=1, source_target_pairs={{0,7},{1,6},{2,5},{3,4},{4,3},{5,2},{6,1},{7,0},{8,15},{9,14},{10,... | collective-permute-start | bytes 491528 | tf_op jit(solution)/shard_map/ppermute | solution.py:325
  47.8 1.0 %copy-done.1 = f32[960,128]{1,0:T(8,128)S(1)} copy-done((f32[960,128]{1,0:T(8,128)S(1)}, f32[960,128]{1,0:T(8,128)}, u32[]{:S(2)}) %copy-start.1) | copy-done | bytes 491544
  48.8 0.9 %copy-done.6 = f32[320,128]{1,0:T(8,128)S(1)} copy-done((f32[320,128]{1,0:T(8,128)S(1)}, f32[320,128]{1,0:T(8,128)}, u32[]{:S(2)}) %copy-start.6) | copy-done | bytes 163864
  49.7 6.0 %add_set.3 = (f32[4,96,128]{2,1,0:T(8,128)S(1)}, f32[1,96,128]{2,1,0:T(8,128)S(1)}, f32[1,96,128]{2,1,0:T(8,128)S(1)}) custom-call(s32[32]{0:T(128)S(1)} %reshape.18.code_ref, bf16[8,16,128]{2,1,0:T(8,128)(2,1)S(1)} %slice.25.note_ref, bf16[4,128,960]{2,1,0:T(8,128)(2,1)S(1)} %stack_left.3.left_ref, f32[960,128]{1,0:T(8,128)S(1)} %copy-done.1, ...), custom_call_target="tpu_custom_call" | custom-call | flops 2264924160 | bytes 1343488 | tf_op jit(solution)/shard_map/add_set/pallas_call | solution.py:240
  56.0 6.4 %add_set.2 = (f32[4,96,128]{2,1,0:T(8,128)S(1)}, f32[1,96,128]{2,1,0:T(8,128)S(1)}, f32[1,96,128]{2,1,0:T(8,128)S(1)}) custom-call(s32[32]{0:T(128)S(1)} %reshape.18.code_ref, bf16[8,16,128]{2,1,0:T(8,128)(2,1)S(1)} %slice.25.note_ref, bf16[4,128,960]{2,1,0:T(8,128)(2,1)S(1)} %stack_left.2.left_ref, f32[960,128]{1,0:T(8,128)S(1)} %copy-done.2, ...), custom_call_target="tpu_custom_call" | custom-call | flops 2264924160 | bytes 1310720 | tf_op jit(solution)/shard_map/add_set/pallas_call | solution.py:240
  62.4 4.0 %collective-permute-start.10 = (f32[1,96,128]{2,1,0:T(8,128)S(1)}, f32[1,96,128]{2,1,0:T(8,128)S(1)}, u32[]{:S(2)}, u32[]{:S(2)}) collective-permute-start(f32[1,96,128]{2,1,0:T(8,128)S(1)} %get-tuple-element.31), channel_id=1, source_target_pairs={{0,1},{1,2},{2,3},{3,4},{4,5},{5,6},{6,7},{7,8},{8,9},{9,10},{10,1... | collective-permute-start | bytes 147464 | tf_op jit(solution)/shard_map/ppermute | solution.py:343
  66.4 1.9 %collective-permute-start.12 = (f32[1,96,128]{2,1,0:T(8,128)S(1)}, f32[1,96,128]{2,1,0:T(8,128)S(1)}, u32[]{:S(2)}, u32[]{:S(2)}) collective-permute-start(f32[1,96,128]{2,1,0:T(8,128)S(1)} %get-tuple-element.33), channel_id=1, source_target_pairs={{1,0},{2,1},{3,2},{4,3},{5,4},{6,5},{7,6},{8,7},{9,8},{10,9},{11,1... | collective-permute-start | bytes 147464 | tf_op jit(solution)/shard_map/ppermute | solution.py:342
  68.3 6.0 %collective-permute-start.11 = (f32[1,96,128]{2,1,0:T(8,128)S(1)}, f32[1,96,128]{2,1,0:T(8,128)S(1)}, u32[]{:S(2)}, u32[]{:S(2)}) collective-permute-start(f32[1,96,128]{2,1,0:T(8,128)S(1)} %get-tuple-element.32), channel_id=1, source_target_pairs={{0,9},{1,10},{2,11},{3,12},{4,13},{5,14},{6,15},{8,1},{9,2},{10,3}... | collective-permute-start | bytes 147464 | tf_op jit(solution)/shard_map/ppermute | solution.py:340
  74.3 2.0 %collective-permute-start.13 = (f32[1,96,128]{2,1,0:T(8,128)S(1)}, f32[1,96,128]{2,1,0:T(8,128)S(1)}, u32[]{:S(2)}, u32[]{:S(2)}) collective-permute-start(f32[1,96,128]{2,1,0:T(8,128)S(1)} %get-tuple-element.34), channel_id=1, source_target_pairs={{0,7},{1,8},{2,9},{3,10},{4,11},{5,12},{6,13},{7,14},{9,0},{10,1},... | collective-permute-start | bytes 147464 | tf_op jit(solution)/shard_map/ppermute | solution.py:339
  76.4 0.8 collective-permute-done.11.before_far_ref
  77.1 5.0 %collective-permute-done.13.after_far_ref = f32[1,96,128]{2,1,0:T(8,128)S(1)} collective-permute-done((f32[1,96,128]{2,1,0:T(8,128)S(1)}, f32[1,96,128]{2,1,0:T(8,128)S(1)}, u32[]{:S(2)}, u32[]{:S(2)}) %collective-permute-start.13) | collective-permute-done | bytes 49184 | tf_op jit(solution)/shard_map/ppermute | solution.py:339
  82.1 0.7 depth_rows.1
  (47 shorter events, 3.4 us)
Async XLA Ops:
  1.4 4.2 %collective-permute-start = (bf16[2,128]{1,0:T(2,128)(2,1)S(1)}, bf16[2,128]{1,0:T(2,128)(2,1)S(1)}, u32[]{:S(2)}, u32[]{:S(2)}) collective-permute-start(bf16[2,128]{1,0:T(2,128)(2,1)S(1)} %fusion.6), channel_id=1, source_target_pairs={{0,8},{1,9},{2,10},{3,11},{4,12},{5,13},{6,14},{7,15},{8,0},{9,1},... | collective-permute-start | bytes 1544 | tf_op jit(solution)/shard_map/ppermute | solution.py:314
  5.5 1.2 %copy-start = (bf16[12,320,128]{2,1,0:T(8,128)(2,1)S(1)}, bf16[12,320,128]{2,1,0:T(8,128)(2,1)}, u32[]{:S(2)}) copy-start(bf16[12,320,128]{2,1,0:T(8,128)(2,1)} %source_ref.1) | copy-start | bytes 2949124
  8.6 0.7 copy-start.7
  9.3 0.6 copy-start.9
  9.9 0.7 copy-start.10
  10.6 6.0 %copy-start.3 = (bf16[4,320,128]{2,1,0:T(8,128)(2,1)S(1)}, bf16[4,320,128]{2,1,0:T(8,128)(2,1)}, u32[]{:S(2)}) copy-start(bf16[4,320,128]{2,1,0:T(8,128)(2,1)} %reference_ref.1) | copy-start | bytes 983044
  10.6 8.2 %copy-start.11 = (f32[40,3,3,3]{0,3,2,1:T(4,128)S(1)}, f32[40,3,3,3]{0,3,2,1:T(4,128)}, u32[]{:S(2)}) copy-start(f32[40,3,3,3]{0,3,2,1:T(4,128)} %param.11) | copy-start | bytes 12964
  10.6 35.5 %all-to-all-start = ((bf16[8,656,128]{2,1,0:T(8,128)(2,1)}), bf16[8,656,128]{2,1,0:T(8,128)(2,1)S(1)}, u32[]{:S(2)}, u32[]{:S(2)}) async-start(bf16[8,656,128]{2,1,0:T(8,128)(2,1)} %get-tuple-element.20), calls=%async_computation | async-start | bytes 2686976 | tf_op jit(solution)/shard_map/all_to_all | solution.py:321
  16.6 22.0 %collective-permute-start.8 = (bf16[4,320,128]{2,1,0:T(8,128)(2,1)S(1)}, bf16[4,320,128]{2,1,0:T(8,128)(2,1)S(1)}, u32[]{:S(2)}, u32[]{:S(2)}) collective-permute-start(bf16[4,320,128]{2,1,0:T(8,128)(2,1)S(1)} %copy-done.3), channel_id=1, source_target_pairs={{0,8},{1,9},{2,10},{3,11},{4,12},{5,13},{6,14},{7,15},{8,0},{9,1},... | collective-permute-start | bytes 983048 | tf_op jit(solution)/shard_map/ppermute | solution.py:315
  19.5 26.7 %collective-permute-start.1 = (bf16[640,128]{1,0:T(8,128)(2,1)}, bf16[640,128]{1,0:T(8,128)(2,1)}, u32[]{:S(2)}, u32[]{:S(2)}) collective-permute-start(bf16[640,128]{1,0:T(8,128)(2,1)} %get-tuple-element.22), channel_id=1, source_target_pairs={{0,1},{1,0},{2,3},{3,2},{4,5},{5,4},{6,7},{7,6},{8,9},{9,8},{10,11... | collective-permute-start | bytes 491528 | tf_op jit(solution)/shard_map/ppermute | solution.py:325
  19.9 26.4 %collective-permute-start.2 = (bf16[640,128]{1,0:T(8,128)(2,1)}, bf16[640,128]{1,0:T(8,128)(2,1)}, u32[]{:S(2)}, u32[]{:S(2)}) collective-permute-start(bf16[640,128]{1,0:T(8,128)(2,1)} %get-tuple-element.23), channel_id=1, source_target_pairs={{0,2},{1,3},{2,0},{3,1},{4,6},{5,7},{6,4},{7,5},{8,10},{9,11},{10,... | collective-permute-start | bytes 491528 | tf_op jit(solution)/shard_map/ppermute | solution.py:325
  25.5 30.2 %collective-permute-start.3 = (bf16[640,128]{1,0:T(8,128)(2,1)}, bf16[640,128]{1,0:T(8,128)(2,1)}, u32[]{:S(2)}, u32[]{:S(2)}) collective-permute-start(bf16[640,128]{1,0:T(8,128)(2,1)} %get-tuple-element.24), channel_id=1, source_target_pairs={{0,3},{1,2},{2,1},{3,0},{4,7},{5,6},{6,5},{7,4},{8,11},{9,10},{10,... | collective-permute-start | bytes 491528 | tf_op jit(solution)/shard_map/ppermute | solution.py:325
  25.6 30.2 %collective-permute-start.4 = (bf16[640,128]{1,0:T(8,128)(2,1)}, bf16[640,128]{1,0:T(8,128)(2,1)}, u32[]{:S(2)}, u32[]{:S(2)}) collective-permute-start(bf16[640,128]{1,0:T(8,128)(2,1)} %get-tuple-element.25), channel_id=1, source_target_pairs={{0,4},{1,5},{2,6},{3,7},{4,0},{5,1},{6,2},{7,3},{8,12},{9,13},{10,... | collective-permute-start | bytes 491528 | tf_op jit(solution)/shard_map/ppermute | solution.py:325
  38.5 0.7 copy-start.4
  39.3 16.6 %collective-permute-start.5 = (bf16[640,128]{1,0:T(8,128)(2,1)}, bf16[640,128]{1,0:T(8,128)(2,1)}, u32[]{:S(2)}, u32[]{:S(2)}) collective-permute-start(bf16[640,128]{1,0:T(8,128)(2,1)} %get-tuple-element.26), channel_id=1, source_target_pairs={{0,5},{1,4},{2,7},{3,6},{4,1},{5,0},{6,3},{7,2},{8,13},{9,12},{10,... | collective-permute-start | bytes 491528 | tf_op jit(solution)/shard_map/ppermute | solution.py:325
  44.6 1.0 %copy-start.5 = (bf16[4,320,128]{2,1,0:T(8,128)(2,1)S(1)}, bf16[4,320,128]{2,1,0:T(8,128)(2,1)}, u32[]{:S(2)}) copy-start(bf16[4,320,128]{2,1,0:T(8,128)(2,1)} %copy-done.4) | copy-start | bytes 983044
  46.2 9.6 %collective-permute-start.6 = (bf16[640,128]{1,0:T(8,128)(2,1)}, bf16[640,128]{1,0:T(8,128)(2,1)S(1)}, u32[]{:S(2)}, u32[]{:S(2)}) collective-permute-start(bf16[640,128]{1,0:T(8,128)(2,1)} %copy-done.10), channel_id=1, source_target_pairs={{0,6},{1,7},{2,4},{3,5},{4,2},{5,3},{6,0},{7,1},{8,14},{9,15},{10,... | collective-permute-start | bytes 491528 | tf_op jit(solution)/shard_map/ppermute | solution.py:325
  46.3 9.7 %collective-permute-start.7 = (bf16[640,128]{1,0:T(8,128)(2,1)}, bf16[640,128]{1,0:T(8,128)(2,1)S(1)}, u32[]{:S(2)}, u32[]{:S(2)}) collective-permute-start(bf16[640,128]{1,0:T(8,128)(2,1)} %copy-done.9), channel_id=1, source_target_pairs={{0,7},{1,6},{2,5},{3,4},{4,3},{5,2},{6,1},{7,0},{8,15},{9,14},{10,... | collective-permute-start | bytes 491528 | tf_op jit(solution)/shard_map/ppermute | solution.py:325
  47.8 1.0 %copy-start.1 = (f32[960,128]{1,0:T(8,128)S(1)}, f32[960,128]{1,0:T(8,128)}, u32[]{:S(2)}) copy-start(f32[960,128]{1,0:T(8,128)} %pad.22.weight_ref) | copy-start | bytes 1474564
  48.8 0.9 %copy-start.6 = (f32[320,128]{1,0:T(8,128)S(1)}, f32[320,128]{1,0:T(8,128)}, u32[]{:S(2)}) copy-start(f32[320,128]{1,0:T(8,128)} %pad_maximum_fusion.edge_ref) | copy-start | bytes 491524
  49.7 6.2 %copy-start.2 = (f32[960,128]{1,0:T(8,128)S(1)}, f32[960,128]{1,0:T(8,128)}, u32[]{:S(2)}) copy-start(f32[960,128]{1,0:T(8,128)} %pad.22.weight_ref) | copy-start | bytes 1474564
  49.7 6.2 %copy-start.8 = (bf16[640,128]{1,0:T(8,128)(2,1)S(1)}, bf16[640,128]{1,0:T(8,128)(2,1)}, u32[]{:S(2)}) copy-start(bf16[640,128]{1,0:T(8,128)(2,1)} %copy-done.7) | copy-start | bytes 491524
  55.7 26.3 %collective-permute-start.9 = (f32[4,96,128]{2,1,0:T(8,128)S(1)}, f32[4,96,128]{2,1,0:T(8,128)S(1)}, u32[]{:S(2)}, u32[]{:S(2)}) collective-permute-start(f32[4,96,128]{2,1,0:T(8,128)S(1)} %get-tuple-element.30), channel_id=1, source_target_pairs={{0,8},{1,9},{2,10},{3,11},{4,12},{5,13},{6,14},{7,15},{8,0},{9,1},... | collective-permute-start | bytes 589832 | tf_op jit(solution)/shard_map/ppermute | solution.py:338
  62.4 13.9 %collective-permute-start.10 = (f32[1,96,128]{2,1,0:T(8,128)S(1)}, f32[1,96,128]{2,1,0:T(8,128)S(1)}, u32[]{:S(2)}, u32[]{:S(2)}) collective-permute-start(f32[1,96,128]{2,1,0:T(8,128)S(1)} %get-tuple-element.31), channel_id=1, source_target_pairs={{0,1},{1,2},{2,3},{3,4},{4,5},{5,6},{6,7},{7,8},{8,9},{9,10},{10,1... | collective-permute-start | bytes 147464 | tf_op jit(solution)/shard_map/ppermute | solution.py:343
  66.4 9.9 %collective-permute-start.12 = (f32[1,96,128]{2,1,0:T(8,128)S(1)}, f32[1,96,128]{2,1,0:T(8,128)S(1)}, u32[]{:S(2)}, u32[]{:S(2)}) collective-permute-start(f32[1,96,128]{2,1,0:T(8,128)S(1)} %get-tuple-element.33), channel_id=1, source_target_pairs={{1,0},{2,1},{3,2},{4,3},{5,4},{6,5},{7,6},{8,7},{9,8},{10,9},{11,1... | collective-permute-start | bytes 147464 | tf_op jit(solution)/shard_map/ppermute | solution.py:342
  68.3 8.8 %collective-permute-start.11 = (f32[1,96,128]{2,1,0:T(8,128)S(1)}, f32[1,96,128]{2,1,0:T(8,128)S(1)}, u32[]{:S(2)}, u32[]{:S(2)}) collective-permute-start(f32[1,96,128]{2,1,0:T(8,128)S(1)} %get-tuple-element.32), channel_id=1, source_target_pairs={{0,9},{1,10},{2,11},{3,12},{4,13},{5,14},{6,15},{8,1},{9,2},{10,3}... | collective-permute-start | bytes 147464 | tf_op jit(solution)/shard_map/ppermute | solution.py:340
  74.3 7.7 %collective-permute-start.13 = (f32[1,96,128]{2,1,0:T(8,128)S(1)}, f32[1,96,128]{2,1,0:T(8,128)S(1)}, u32[]{:S(2)}, u32[]{:S(2)}) collective-permute-start(f32[1,96,128]{2,1,0:T(8,128)S(1)} %get-tuple-element.34), channel_id=1, source_target_pairs={{0,7},{1,8},{2,9},{3,10},{4,11},{5,12},{6,13},{7,14},{9,0},{10,1},... | collective-permute-start | bytes 147464 | tf_op jit(solution)/shard_map/ppermute | solution.py:339

commit v2 on v1

--- a/solution.py
+++ b/solution.py
@@ -13,17 +13,16 @@
 DSPAN = 16
 CAP = 2
 SETS = 2
+NOTE = 16
 
 VMEM = pl.BlockSpec(memory_space=pltpu.VMEM)
 SMEM = pl.BlockSpec(memory_space=pltpu.SMEM)
 ANY = pl.BlockSpec(memory_space=pl.ANY)
 
 
-def pack_kernel(
-    half, span, code_ref, source_ref, note_ref, far_ref, *rest
-):
-    own_refs = rest[:-4]
-    count_ref, slot_ref, block_ref, sem = rest[-4:]
+def pack_kernel(half, apart, route_ref, target_ref, start_ref, source_ref, far_ref, *rest):
+    own_refs = rest[:-3]
+    slot_ref, count_ref, sem = rest[-3:]
     items, channels, pixels = source_ref.shape
     side = lax.div(lax.axis_index("views"), half)
     here = lax.rem(lax.axis_index("views"), half)
@@ -36,8 +35,8 @@
 
     @pl.loop(0, items)
     def _(i):
-        owner = lax.div(code_ref[i], span)
-        rest = lax.rem(code_ref[i], span)
+        owner = route_ref[i]
+        rest = target_ref[i] * DSPAN + start_ref[i]
         home = lax.rem(owner, half)
         for t in range(SETS):
 
@@ -46,7 +45,7 @@
                 place = count_ref[t * half + home]
                 count_ref[t * half + home] = place + 1
                 first = pl.multiple_of(place * channels, channels)
-                if t == 0 and len(own_refs) > 1:
+                if t == 0 and apart:
                     for k, own_ref in enumerate(own_refs):
 
                         @pl.when(home == here ^ k)
@@ -60,49 +59,64 @@
                 line = slot_ref[pl.ds(home, 1), :]
                 slot_ref[pl.ds(home, 1), :] = jnp.where(lane == t * CAP + place, value, line)
 
-    height = note_ref.shape[0]
-    row = lax.broadcasted_iota(jnp.int32, (height, pixels), 0)
-    note = note_ref[...].astype(jnp.float32)
-
-    @pl.loop(0, half)
-    def _(j):
-        line = jnp.broadcast_to(slot_ref[pl.ds(j, 1), :], (height, pixels))
-        block_ref[j] = jnp.where(row == 4, line, note).astype(block_ref.dtype)
-
-    last = pltpu.make_async_copy(
-        block_ref, far_ref.at[:, pl.ds(CAP * channels, height), :], sem
-    )
-    last.start()
-
     @pl.loop(0, items)
     def _(i):
         pltpu.make_async_copy(
             source_ref.at[0], far_ref.at[0, pl.ds(0, channels), :], sem
         ).wait()
 
-    last.wait()
-
-
-def pack_rows(codes, source, note, half, span, apart):
+
+def pack_rows(route, target, start, source, half, apart):
     _, channels, pixels = source.shape
-    height = note.shape[0]
     length = CAP * channels
-    shapes = [(half, length + height, pixels)]
+    shapes = [(half, length + NOTE, pixels)]
     shapes += [(length, pixels)] * half if apart else [(half, length, pixels)]
-    return pl.pallas_call(
-        functools.partial(pack_kernel, half, span),
-        out_shape=[jax.ShapeDtypeStruct(shape, source.dtype) for shape in shapes],
-        in_specs=[SMEM, VMEM, VMEM],
-        out_specs=[ANY] * len(shapes),
+    outs = [jax.ShapeDtypeStruct(shape, source.dtype) for shape in shapes]
+    return pl.pallas_call(
+        functools.partial(pack_kernel, half, apart),
+        out_shape=outs + [jax.ShapeDtypeStruct((half, pixels), jnp.float32)],
+        in_specs=[SMEM, SMEM, SMEM, VMEM],
+        out_specs=[pl.BlockSpec(memory_space=pltpu.HBM)] * len(shapes) + [VMEM],
+        scratch_shapes=[pltpu.SMEM((SETS * half,), jnp.int32), pltpu.SemaphoreType.DMA],
+        compiler_params=pltpu.CompilerParams(vmem_limit_bytes=16 << 20),
+        name="pack_rows",
+    )(keep(route), keep(target), keep(start), keep(source))
+
+
+def note_kernel(packed_ref, slot_ref, near_ref, far_ref, out_ref, block_ref, sem):
+    half, pixels = slot_ref.shape
+    fixed = [near_ref[...].astype(jnp.float32), far_ref[...].astype(jnp.float32)]
+    rest = jnp.zeros((NOTE - 5, pixels), jnp.float32)
+
+    @pl.loop(0, half)
+    def _(j):
+        lines = fixed + [slot_ref[pl.ds(j, 1), :], rest]
+        block_ref[j] = jnp.concatenate(lines, axis=0).astype(block_ref.dtype)
+
+    first = out_ref.shape[1] - NOTE
+    copy = pltpu.make_async_copy(block_ref, out_ref.at[:, pl.ds(first, NOTE), :], sem)
+    copy.start()
+    copy.wait()
+
+
+def add_note(packed, slots, near, far):
+    return pl.pallas_call(
+        note_kernel,
+        out_shape=jax.ShapeDtypeStruct(packed.shape, packed.dtype),
+        in_specs=[ANY, VMEM, VMEM, VMEM],
+        out_specs=ANY,
         scratch_shapes=[
-            pltpu.SMEM((SETS * half,), jnp.int32),
-            pltpu.VMEM((half, pixels), jnp.float32),
-            pltpu.VMEM((half, height, pixels), source.dtype),
+            pltpu.VMEM((packed.shape[0], NOTE, packed.shape[2]), packed.dtype),
             pltpu.SemaphoreType.DMA,
         ],
-        compiler_params=pltpu.CompilerParams(vmem_limit_bytes=16 << 20),
-        name="pack_rows",
-    )(codes, source, note)
+        input_output_aliases={0: 0},
+        compiler_params=pltpu.CompilerParams(vmem_limit_bytes=4 << 20),
+        name="add_note",
+    )(packed, slots, near, far)
+
+
+def keep(values):
+    return pltpu.with_memory_space_constraint(values, pltpu.HBM)
 
 
 def split_two(values):
@@ -152,9 +166,17 @@
 def set_kernel(
     t, code_ref, note_ref, left_ref, weight_ref, edge_ref, *rest
 ):
-    arrived_refs = rest[:-7]
-    main_ref, least_ref, most_ref, stack_ref, wide_ref, total_ref, canvas_ref = rest[-7:]
+    arrived_refs = rest[:-11]
+    main_ref, least_ref, most_ref = rest[-11:-8]
+    stack_ref, wide_ref, total_ref, canvas_ref, *fetched, sems = rest[-8:]
     rows, channels, pixels = canvas_ref.shape
+    fetches = [
+        pltpu.make_async_copy(source, target, sems.at[n])
+        for n, (source, target) in enumerate(zip((left_ref, weight_ref, edge_ref), fetched))
+    ]
+    for fetch in fetches:
+        fetch.start()
+    left_ref, weight_ref, edge_ref = fetched
     half = note_ref.shape[0]
     lane = lax.broadcasted_iota(jnp.int32, (channels, pixels), 1)
     canvas_ref[...] = jnp.zeros_like(canvas_ref)
@@ -188,6 +210,8 @@
         def _(home):
             add_slots(home, arrived_refs[0].at[home])
 
+    for fetch in fetches:
+        fetch.wait()
     for r in range(rows):
         mean = canvas_ref[r] * jnp.concatenate([counts[r]] * (channels // 8), axis=0)
         for e in range(3):
@@ -237,16 +261,21 @@
     rows, pixels, depth = left.shape
     channels = depth // 3
     shapes = [(n, DISP, pixels) for n in (rows, 1, 1)]
+    left, weight, edge = keep(left), keep(weight), keep(edge)
     return pl.pallas_call(
         functools.partial(set_kernel, t),
         out_shape=[jax.ShapeDtypeStruct(shape, jnp.float32) for shape in shapes],
-        in_specs=[SMEM] + [VMEM] * (4 + len(arrived)),
+        in_specs=[SMEM, VMEM, ANY, ANY, ANY] + [VMEM] * len(arrived),
         out_specs=[VMEM] * 3,
         scratch_shapes=[
             pltpu.VMEM((rows, depth, pixels), jnp.float32),
             pltpu.VMEM((depth, pixels), jnp.float32),
             pltpu.VMEM(((rows + 2) * 3 + rows, pixels, pixels), jnp.float32),
             pltpu.VMEM((rows, channels, pixels), jnp.float32),
+            pltpu.VMEM(left.shape, left.dtype),
+            pltpu.VMEM(weight.shape, weight.dtype),
+            pltpu.VMEM(edge.shape, edge.dtype),
+            pltpu.SemaphoreType.DMA((3,)),
         ],
         compiler_params=pltpu.CompilerParams(
             vmem_limit_bytes=(11 << 20) + sum(2 * part.size for part in arrived)
@@ -294,8 +323,7 @@
 def compute(source_rows, route_owner, target_row, start_index, reference_rows, conv_weight):
     views = lax.axis_size("views")
     half = views // 2
-    rows, channels, pixels = reference_rows.shape
-    span = rows * DSPAN
+    _, channels, pixels = reference_rows.shape
     send = functools.partial(lax.ppermute, axis_name="views")
     home = [(i, (i + half) % views) for i in range(views)]
     groups = [list(range(half)), list(range(half, views))]
@@ -313,11 +341,11 @@
     named = jnp.pad(named, ((0, 0), (0, pixels - named.shape[1])), constant_values=-1)
     far_named = send(named, perm=home)
     far_rows = send(reference_rows, perm=home)
-    note = jnp.pad(jnp.concatenate([named, far_named]), ((0, 12), (0, 0)))
     apart = half <= 8
-    packed_far, *packed_own = pack_rows(
-        owner * span + rest, source_rows, note, half, span, apart
+    packed_far, *packed_own, slots = pack_rows(
+        owner, target_row, start_index, source_rows, half, apart
     )
+    packed_far = add_note(packed_far, slots, named, far_named)
     arrived_far = swap(packed_far)
     if apart:
         arrived_own = packed_own[:1] + [None] * (half - 1)

time: 83.3 us -> 79.2 us (0.951)
  starting transfers between devices: 35.9 us -> 31.5 us
  waiting for transfers between devices: 18.2 us -> 14 us
  local copies, waits for them, and re-layouts: 10.2 us -> 12 us
  Pallas kernels: 16.1 us -> 17.9 us
  other arithmetic: 2.17 us -> 3.06 us
    unnamed x25 -> x9, local copies, waits for them, and re-layouts: 6.82 us -> 1.97 us
    ppermute x1, waiting for transfers between devices: 11.3 us -> 7.61 us  [compute(): far_rows = send(reference_rows, perm=home)]
    reshape x2, local copies, waits for them, and re-layouts: 0.11 us -> 2.17 us  [compute(): edges = jnp.pad(scaled[..., 2], ((0, 0), (0, 0), (0, 5))).reshape(-1, 24)]
    ppermute x1, starting transfers between devices: 5.97 us -> 4.02 us  [compute(): send(far_high, perm=[(i, j + 1) for i, j in home if j + 1 < views])]
    ppermute x7, waiting for transfers between devices: 0.14 us -> 1.92 us  [compute(): send(packed_own[k], perm=[(i, i ^ k) for i in range(views)])]
    ppermute x1, waiting for transfers between devices: 4.95 us -> 3.36 us  [compute(): other_low = send(far_low, perm=[(i, j - 1) for i, j in home if j > 0])]
    pallas_call x1 -> x2, Pallas kernels: 1.88 us -> 3.39 us  [the longest x1 2.7 us: pack_rows(): pl.pallas_call(functools.partial(pack_kernel, half, apart), out_shape=out...]
    ppermute x7, starting transfers between devices: 10.7 us -> 9.39 us  [compute(): send(packed_own[k], perm=[(i, i ^ k) for i in range(views)])]
  transfers between devices with their start and end apart: 15 -> 15, of which waited for: 5 -> 4; matrix products, arithmetic and copies ran while one was open for 5% -> 15% of each run, Pallas kernels for 16% -> 21%
where the time goes in v2:
time: 79.2 us; the launch traced here: 78.6 us
  starting transfers between devices  31.5 us (40%)
  Pallas kernels  17.9 us (23%)
  waiting for transfers between devices  14 us (18%)
  local copies, waits for them, and re-layouts  12 us (15%)
  other arithmetic  3.06 us (4%)
    pallas_call x2, Pallas kernels, add_set(): pl.pallas_call(functools.partial(set_kernel, t), out_shape=[jax.ShapeDtyp...  12.7 us
    ppermute x7, starting transfers between devices, compute(): send(packed_own[k], perm=[(i, i ^ k) for i in range(views)])  9.39 us
    ppermute x1, waiting for transfers between devices, compute(): far_rows = send(reference_rows, perm=home)  7.61 us
    all_to_all x1, starting transfers between devices, compute(): arrived_far = swap(packed_far)  5.16 us
    ppermute x1, starting transfers between devices, compute(): send(far_high, perm=[(i, j + 1) for i, j in home if j + 1 < views])  4.02 us
    ppermute x1, starting transfers between devices, compute(): own_high = send(own_high, perm=[(i, i + 1) for i in range(views - 1)])  3.38 us
    ppermute x1, waiting for transfers between devices, compute(): other_low = send(far_low, perm=[(i, j - 1) for i, j in home if j > 0])  3.36 us
    ppermute x1, starting transfers between devices, compute(): far_named = send(named, perm=home)  3.19 us
  transfers between devices with their start and end apart: 15, of which 4 were waited for; matrix products, arithmetic and copies ran while one was open for 15% of the time, Pallas kernels for 21%

profile of v2, /device:TPU:1, one launch (start us, length us, event | category | flops | bytes accessed | tf_op | source)
XLA Modules:
  0.0 78.6 jit_solution(16439246405562235394)
XLA Ops:
  0.0 0.7 convert_bitcast_fusion.1
  0.7 0.7 convert_bitcast_fusion
  1.3 3.2 %collective-permute-start = (bf16[2,128]{1,0:T(2,128)(2,1)S(1)}, bf16[2,128]{1,0:T(2,128)(2,1)S(1)}, u32[]{:S(2)}, u32[]{:S(2)}) collective-permute-start(bf16[2,128]{1,0:T(2,128)(2,1)S(1)} %fusion.3.near_ref), channel_id=1, source_target_pairs={{0,8},{1,9},{2,10},{3,11},{4,12},{5,13},{6,14},{7,15},{8,0},{9,1},... | collective-permute-start | bytes 1544 | tf_op jit(solution)/shard_map/ppermute | solution.py:342
  4.5 2.7 %pack_rows.1 = (bf16[8,656,128]{2,1,0:T(8,128)(2,1)}, bf16[640,128]{1,0:T(8,128)(2,1)S(1)}, bf16[640,128]{1,0:T(8,128)(2,1)}, bf16[640,128]{1,0:T(8,128)(2,1)}, ...) custom-call(s32[12]{0:T(128)} %bitcast.21, ...), custom_call_target="tpu_custom_call" | custom-call | tf_op jit(solution)/shard_map/pack_rows/pallas_call | solution.py:75
  7.3 0.7 add_note.1
  8.0 5.2 %all-to-all-start = ((bf16[8,656,128]{2,1,0:T(8,128)(2,1)}), bf16[8,656,128]{2,1,0:T(8,128)(2,1)S(1)}, u32[]{:S(2)}, u32[]{:S(2)}) async-start(bf16[8,656,128]{2,1,0:T(8,128)(2,1)} %add_note.1), calls=%async_computation | async-start | bytes 2686976 | tf_op jit(solution)/shard_map/all_to_all | solution.py:349
  13.1 1.7 %collective-permute-start.2 = (bf16[640,128]{1,0:T(8,128)(2,1)}, bf16[640,128]{1,0:T(8,128)(2,1)S(1)}, u32[]{:S(2)}, u32[]{:S(2)}) collective-permute-start(bf16[640,128]{1,0:T(8,128)(2,1)} %get-tuple-element.25), channel_id=1, source_target_pairs={{0,2},{1,3},{2,0},{3,1},{4,6},{5,7},{6,4},{7,5},{8,10},{9,11},{10,... | collective-permute-start | bytes 491528 | tf_op jit(solution)/shard_map/ppermute | solution.py:353
  15.3 1.4 %collective-permute-start.4 = (bf16[640,128]{1,0:T(8,128)(2,1)S(1)}, bf16[640,128]{1,0:T(8,128)(2,1)}, u32[]{:S(2)}, u32[]{:S(2)}) collective-permute-start(bf16[640,128]{1,0:T(8,128)(2,1)S(1)} %get-tuple-element.27), channel_id=1, source_target_pairs={{0,4},{1,5},{2,6},{3,7},{4,0},{5,1},{6,2},{7,3},{8,12},{9,13},{10,... | collective-permute-start | bytes 491528 | tf_op jit(solution)/shard_map/ppermute | solution.py:353
  16.6 1.2 %collective-permute-start.8 = (bf16[4,320,128]{2,1,0:T(8,128)(2,1)S(1)}, bf16[4,320,128]{2,1,0:T(8,128)(2,1)S(1)}, u32[]{:S(2)}, u32[]{:S(2)}) collective-permute-start(bf16[4,320,128]{2,1,0:T(8,128)(2,1)S(1)} %copy-done.2), channel_id=1, source_target_pairs={{0,8},{1,9},{2,10},{3,11},{4,12},{5,13},{6,14},{7,15},{8,0},{9,1},... | collective-permute-start | bytes 983048 | tf_op jit(solution)/shard_map/ppermute | solution.py:343
  17.9 1.0 %broadcast_in_dim.3 = f32[40,8,3,3,3]{1,0,4,3,2:T(8,128)} broadcast(f32[40,3,3,3]{0,3,2,1:T(4,128)S(1)} %broadcast_multiply_fusion), dimensions={0,2,3,4} | broadcast | bytes 38880 | tf_op jit(solution)/shard_map/broadcast_in_dim | solution.py:359
  18.9 1.3 %reshape.13 = f32[320,3,3,3]{0,3,2,1:T(4,128)S(1)} reshape(f32[40,8,3,3,3]{1,0,4,3,2:T(8,128)} %broadcast_in_dim.3) | data formatting | bytes 69120 | tf_op jit(solution)/shard_map/reshape | solution.py:359
  20.8 1.6 %copy.15 = f32[320,24]{1,0:T(8,128)} copy(f32[320,24]{0,1:T(8,128)} %pad_bitcast_fusion) | data formatting | bytes 61440 | tf_op jit(solution)/shard_map/reshape | solution.py:362
  22.4 1.0 %pad_slice_fusion = f32[320,126]{1,0:T(8,128)S(1)} fusion(f32[320,24]{1,0:T(8,128)} %copy.15), kind=kLoop, calls=%fused_computation.1 | loop fusion | bytes 192000 | tf_op jit(solution)/shard_map/jit(_roll_static)/slice | solution.py:363
  23.4 1.7 %pad_maximum_fusion.edge_ref = f32[320,128]{1,0:T(8,128)} fusion(f32[320,2]{1,0:T(8,128)} %bitcast.18, f32[320,126]{1,0:T(8,128)S(1)} %pad_slice_fusion), kind=kLoop, calls=%fused_computation | loop fusion | flops 40960 | bytes 327680 | tf_op jit(solution)/shard_map/jit(_roll_static)/concatenate | solution.py:363
  25.6 1.0 %copy-done = bf16[4,128,960]{2,1,0:T(8,128)(2,1)} copy-done((bf16[4,128,960]{2,1,0:T(8,128)(2,1)}, bf16[4,128,960]{2,1,0:T(8,128)(2,1)S(1)}, u32[]{:S(2)}) %copy-start) | copy-done | bytes 983064
  26.6 0.7 reshape.14
  27.3 1.9 %copy.14 = f32[960,9]{1,0:T(8,128)} copy(f32[960,9]{0,1:T(8,128)} %reshape.14) | data formatting | bytes 69120 | tf_op jit(solution)/shard_map/reshape | solution.py:360
  29.2 1.8 %pad.17.weight_ref = f32[960,128]{1,0:T(8,128)} pad(f32[960,9]{1,0:T(8,128)} %copy.14, f32[]{:T(128)} %constant.10.clone.1), padding=0_0x0_119 | pad | bytes 526084 | tf_op jit(solution)/shard_map/jit(_pad)/pad | solution.py:361
  31.0 7.6 %collective-permute-done.8.reference_ref = bf16[4,320,128]{2,1,0:T(8,128)(2,1)S(1)} collective-permute-done((bf16[4,320,128]{2,1,0:T(8,128)(2,1)S(1)}, bf16[4,320,128]{2,1,0:T(8,128)(2,1)S(1)}, u32[]{:S(2)}, u32[]{:S(2)}) %collective-permute-start.8) | collective-permute-done | bytes 327712 | tf_op jit(solution)/shard_map/ppermute | solution.py:343
  38.6 3.8 %collective-permute-start.5 = (bf16[640,128]{1,0:T(8,128)(2,1)S(1)}, bf16[640,128]{1,0:T(8,128)(2,1)S(1)}, u32[]{:S(2)}, u32[]{:S(2)}) collective-permute-start(bf16[640,128]{1,0:T(8,128)(2,1)S(1)} %get-tuple-element.28), channel_id=1, source_target_pairs={{0,5},{1,4},{2,7},{3,6},{4,1},{5,0},{6,3},{7,2},{8,13},{9,12},{10,... | collective-permute-start | bytes 491528 | tf_op jit(solution)/shard_map/ppermute | solution.py:353
  42.9 1.0 %copy-done.1 = bf16[4,128,960]{2,1,0:T(8,128)(2,1)} copy-done((bf16[4,128,960]{2,1,0:T(8,128)(2,1)}, bf16[4,128,960]{2,1,0:T(8,128)(2,1)S(1)}, u32[]{:S(2)}) %copy-start.1) | copy-done | bytes 983064
  44.2 2.0 %collective-permute-start.7 = (bf16[640,128]{1,0:T(8,128)(2,1)S(1)}, bf16[640,128]{1,0:T(8,128)(2,1)S(1)}, u32[]{:S(2)}, u32[]{:S(2)}) collective-permute-start(bf16[640,128]{1,0:T(8,128)(2,1)S(1)} %get-tuple-element.30), channel_id=1, source_target_pairs={{0,7},{1,6},{2,5},{3,4},{4,3},{5,2},{6,1},{7,0},{8,15},{9,14},{10,... | collective-permute-start | bytes 491528 | tf_op jit(solution)/shard_map/ppermute | solution.py:353
  46.2 6.2 %add_set.3 = (f32[4,96,128]{2,1,0:T(8,128)S(1)}, f32[1,96,128]{2,1,0:T(8,128)S(1)}, f32[1,96,128]{2,1,0:T(8,128)S(1)}) custom-call(s32[32]{0:T(128)S(1)} %reshape.16.code_ref, bf16[8,16,128]{2,1,0:T(8,128)(2,1)S(1)} %slice.25.note_ref, bf16[4,128,960]{2,1,0:T(8,128)(2,1)} %copy-done.1, f32[960,128]{1,0:T(8,128)} %pad.17.weight_ref, ...), custom_call_target="tpu_custom_call" | custom-call | flops 2264924160 | bytes 1343488 | tf_op jit(solution)/shard_map/add_set/pallas_call | solution.py:265
  52.8 1.9 %collective-permute-done.7.rest_7_ = bf16[640,128]{1,0:T(8,128)(2,1)S(1)} collective-permute-done((bf16[640,128]{1,0:T(8,128)(2,1)S(1)}, bf16[640,128]{1,0:T(8,128)(2,1)S(1)}, u32[]{:S(2)}, u32[]{:S(2)}) %collective-permute-start.7) | collective-permute-done | bytes 163872 | tf_op jit(solution)/shard_map/ppermute | solution.py:353
  54.7 6.5 %add_set.2 = (f32[4,96,128]{2,1,0:T(8,128)S(1)}, f32[1,96,128]{2,1,0:T(8,128)S(1)}, f32[1,96,128]{2,1,0:T(8,128)S(1)}) custom-call(s32[32]{0:T(128)S(1)} %reshape.16.code_ref, bf16[8,16,128]{2,1,0:T(8,128)(2,1)S(1)} %slice.25.note_ref, bf16[4,128,960]{2,1,0:T(8,128)(2,1)} %copy-done, f32[960,128]{1,0:T(8,128)} %pad.17.weight_ref, ...), custom_call_target="tpu_custom_call" | custom-call | flops 2264924160 | bytes 1310720 | tf_op jit(solution)/shard_map/add_set/pallas_call | solution.py:265
  61.3 3.4 %collective-permute-start.10 = (f32[1,96,128]{2,1,0:T(8,128)S(1)}, f32[1,96,128]{2,1,0:T(8,128)S(1)}, u32[]{:S(2)}, u32[]{:S(2)}) collective-permute-start(f32[1,96,128]{2,1,0:T(8,128)S(1)} %get-tuple-element.33), channel_id=1, source_target_pairs={{0,1},{1,2},{2,3},{3,4},{4,5},{5,6},{6,7},{7,8},{8,9},{9,10},{10,1... | collective-permute-start | bytes 147464 | tf_op jit(solution)/shard_map/ppermute | solution.py:371
  64.7 1.9 %collective-permute-start.12 = (f32[1,96,128]{2,1,0:T(8,128)S(1)}, f32[1,96,128]{2,1,0:T(8,128)S(1)}, u32[]{:S(2)}, u32[]{:S(2)}) collective-permute-start(f32[1,96,128]{2,1,0:T(8,128)S(1)} %get-tuple-element.35), channel_id=1, source_target_pairs={{1,0},{2,1},{3,2},{4,3},{5,4},{6,5},{7,6},{8,7},{9,8},{10,9},{11,1... | collective-permute-start | bytes 147464 | tf_op jit(solution)/shard_map/ppermute | solution.py:370
  66.6 4.0 %collective-permute-start.11 = (f32[1,96,128]{2,1,0:T(8,128)S(1)}, f32[1,96,128]{2,1,0:T(8,128)S(1)}, u32[]{:S(2)}, u32[]{:S(2)}) collective-permute-start(f32[1,96,128]{2,1,0:T(8,128)S(1)} %get-tuple-element.34), channel_id=1, source_target_pairs={{0,9},{1,10},{2,11},{3,12},{4,13},{5,14},{6,15},{8,1},{9,2},{10,3}... | collective-permute-start | bytes 147464 | tf_op jit(solution)/shard_map/ppermute | solution.py:368
  70.6 2.8 %collective-permute-start.13 = (f32[1,96,128]{2,1,0:T(8,128)S(1)}, f32[1,96,128]{2,1,0:T(8,128)S(1)}, u32[]{:S(2)}, u32[]{:S(2)}) collective-permute-start(f32[1,96,128]{2,1,0:T(8,128)S(1)} %get-tuple-element.36), channel_id=1, source_target_pairs={{0,7},{1,8},{2,9},{3,10},{4,11},{5,12},{6,13},{7,14},{9,0},{10,1},... | collective-permute-start | bytes 147464 | tf_op jit(solution)/shard_map/ppermute | solution.py:367
  73.4 1.1 %collective-permute-done.11.before_far_ref = f32[1,96,128]{2,1,0:T(8,128)S(1)} collective-permute-done((f32[1,96,128]{2,1,0:T(8,128)S(1)}, f32[1,96,128]{2,1,0:T(8,128)S(1)}, u32[]{:S(2)}, u32[]{:S(2)}) %collective-permute-start.11) | collective-permute-done | bytes 49184 | tf_op jit(solution)/shard_map/ppermute | solution.py:368
  74.5 3.4 %collective-permute-done.13.after_far_ref = f32[1,96,128]{2,1,0:T(8,128)S(1)} collective-permute-done((f32[1,96,128]{2,1,0:T(8,128)S(1)}, f32[1,96,128]{2,1,0:T(8,128)S(1)}, u32[]{:S(2)}, u32[]{:S(2)}) %collective-permute-start.13) | collective-permute-done | bytes 49184 | tf_op jit(solution)/shard_map/ppermute | solution.py:367
  77.9 0.7 depth_rows.1
  (31 shorter events, 2.8 us)
Async XLA Ops:
  1.3 5.9 %collective-permute-start = (bf16[2,128]{1,0:T(2,128)(2,1)S(1)}, bf16[2,128]{1,0:T(2,128)(2,1)S(1)}, u32[]{:S(2)}, u32[]{:S(2)}) collective-permute-start(bf16[2,128]{1,0:T(2,128)(2,1)S(1)} %fusion.3.near_ref), channel_id=1, source_target_pairs={{0,8},{1,9},{2,10},{3,11},{4,12},{5,13},{6,14},{7,15},{8,0},{9,1},... | collective-permute-start | bytes 1544 | tf_op jit(solution)/shard_map/ppermute | solution.py:342
  8.0 8.7 %copy-start.2 = (bf16[4,320,128]{2,1,0:T(8,128)(2,1)S(1)}, bf16[4,320,128]{2,1,0:T(8,128)(2,1)}, u32[]{:S(2)}) copy-start(bf16[4,320,128]{2,1,0:T(8,128)(2,1)} %reference_ref.1) | copy-start | bytes 983044
  8.0 9.9 %copy-start.3 = (f32[40,3,3,3]{0,3,2,1:T(4,128)S(1)}, f32[40,3,3,3]{0,3,2,1:T(4,128)}, u32[]{:S(2)}) copy-start(f32[40,3,3,3]{0,3,2,1:T(4,128)} %param.11) | copy-start | bytes 12964
  8.0 35.9 %all-to-all-start = ((bf16[8,656,128]{2,1,0:T(8,128)(2,1)}), bf16[8,656,128]{2,1,0:T(8,128)(2,1)S(1)}, u32[]{:S(2)}, u32[]{:S(2)}) async-start(bf16[8,656,128]{2,1,0:T(8,128)(2,1)} %add_note.1), calls=%async_computation | async-start | bytes 2686976 | tf_op jit(solution)/shard_map/all_to_all | solution.py:349
  13.1 30.9 %collective-permute-start.1 = (bf16[640,128]{1,0:T(8,128)(2,1)}, bf16[640,128]{1,0:T(8,128)(2,1)S(1)}, u32[]{:S(2)}, u32[]{:S(2)}) collective-permute-start(bf16[640,128]{1,0:T(8,128)(2,1)} %get-tuple-element.24), channel_id=1, source_target_pairs={{0,1},{1,0},{2,3},{3,2},{4,5},{5,4},{6,7},{7,6},{8,9},{9,8},{10,11... | collective-permute-start | bytes 491528 | tf_op jit(solution)/shard_map/ppermute | solution.py:353
  13.1 31.0 %collective-permute-start.2 = (bf16[640,128]{1,0:T(8,128)(2,1)}, bf16[640,128]{1,0:T(8,128)(2,1)S(1)}, u32[]{:S(2)}, u32[]{:S(2)}) collective-permute-start(bf16[640,128]{1,0:T(8,128)(2,1)} %get-tuple-element.25), channel_id=1, source_target_pairs={{0,2},{1,3},{2,0},{3,1},{4,6},{5,7},{6,4},{7,5},{8,10},{9,11},{10,... | collective-permute-start | bytes 491528 | tf_op jit(solution)/shard_map/ppermute | solution.py:353
  14.9 37.5 %collective-permute-start.3 = (bf16[640,128]{1,0:T(8,128)(2,1)S(1)}, bf16[640,128]{1,0:T(8,128)(2,1)S(1)}, u32[]{:S(2)}, u32[]{:S(2)}) collective-permute-start(bf16[640,128]{1,0:T(8,128)(2,1)S(1)} %get-tuple-element.26), channel_id=1, source_target_pairs={{0,3},{1,2},{2,1},{3,0},{4,7},{5,6},{6,5},{7,4},{8,11},{9,10},{10,... | collective-permute-start | bytes 491528 | tf_op jit(solution)/shard_map/ppermute | solution.py:353
  15.3 37.5 %collective-permute-start.4 = (bf16[640,128]{1,0:T(8,128)(2,1)S(1)}, bf16[640,128]{1,0:T(8,128)(2,1)}, u32[]{:S(2)}, u32[]{:S(2)}) collective-permute-start(bf16[640,128]{1,0:T(8,128)(2,1)S(1)} %get-tuple-element.27), channel_id=1, source_target_pairs={{0,4},{1,5},{2,6},{3,7},{4,0},{5,1},{6,2},{7,3},{8,12},{9,13},{10,... | collective-permute-start | bytes 491528 | tf_op jit(solution)/shard_map/ppermute | solution.py:353
  16.6 22.0 %collective-permute-start.8 = (bf16[4,320,128]{2,1,0:T(8,128)(2,1)S(1)}, bf16[4,320,128]{2,1,0:T(8,128)(2,1)S(1)}, u32[]{:S(2)}, u32[]{:S(2)}) collective-permute-start(bf16[4,320,128]{2,1,0:T(8,128)(2,1)S(1)} %copy-done.2), channel_id=1, source_target_pairs={{0,8},{1,9},{2,10},{3,11},{4,12},{5,13},{6,14},{7,15},{8,0},{9,1},... | collective-permute-start | bytes 983048 | tf_op jit(solution)/shard_map/ppermute | solution.py:343
  25.6 1.0 %copy-start = (bf16[4,128,960]{2,1,0:T(8,128)(2,1)}, bf16[4,128,960]{2,1,0:T(8,128)(2,1)S(1)}, u32[]{:S(2)}) copy-start(bf16[4,128,960]{2,1,0:T(8,128)(2,1)S(1)} %stack_left.2.left_ref) | copy-start | bytes 2949124
  38.6 14.2 %collective-permute-start.5 = (bf16[640,128]{1,0:T(8,128)(2,1)S(1)}, bf16[640,128]{1,0:T(8,128)(2,1)S(1)}, u32[]{:S(2)}, u32[]{:S(2)}) collective-permute-start(bf16[640,128]{1,0:T(8,128)(2,1)S(1)} %get-tuple-element.28), channel_id=1, source_target_pairs={{0,5},{1,4},{2,7},{3,6},{4,1},{5,0},{6,3},{7,2},{8,13},{9,12},{10,... | collective-permute-start | bytes 491528 | tf_op jit(solution)/shard_map/ppermute | solution.py:353
  42.9 1.0 %copy-start.1 = (bf16[4,128,960]{2,1,0:T(8,128)(2,1)}, bf16[4,128,960]{2,1,0:T(8,128)(2,1)S(1)}, u32[]{:S(2)}) copy-start(bf16[4,128,960]{2,1,0:T(8,128)(2,1)S(1)} %stack_left.3.left_ref) | copy-start | bytes 2949124
  44.0 8.8 %collective-permute-start.6 = (bf16[640,128]{1,0:T(8,128)(2,1)S(1)}, bf16[640,128]{1,0:T(8,128)(2,1)S(1)}, u32[]{:S(2)}, u32[]{:S(2)}) collective-permute-start(bf16[640,128]{1,0:T(8,128)(2,1)S(1)} %get-tuple-element.29), channel_id=1, source_target_pairs={{0,6},{1,7},{2,4},{3,5},{4,2},{5,3},{6,0},{7,1},{8,14},{9,15},{10,... | collective-permute-start | bytes 491528 | tf_op jit(solution)/shard_map/ppermute | solution.py:353
  44.2 10.6 %collective-permute-start.7 = (bf16[640,128]{1,0:T(8,128)(2,1)S(1)}, bf16[640,128]{1,0:T(8,128)(2,1)S(1)}, u32[]{:S(2)}, u32[]{:S(2)}) collective-permute-start(bf16[640,128]{1,0:T(8,128)(2,1)S(1)} %get-tuple-element.30), channel_id=1, source_target_pairs={{0,7},{1,6},{2,5},{3,4},{4,3},{5,2},{6,1},{7,0},{8,15},{9,14},{10,... | collective-permute-start | bytes 491528 | tf_op jit(solution)/shard_map/ppermute | solution.py:353
  52.4 25.5 %collective-permute-start.9 = (f32[4,96,128]{2,1,0:T(8,128)S(1)}, f32[4,96,128]{2,1,0:T(8,128)S(1)}, u32[]{:S(2)}, u32[]{:S(2)}) collective-permute-start(f32[4,96,128]{2,1,0:T(8,128)S(1)} %get-tuple-element.32), channel_id=1, source_target_pairs={{0,8},{1,9},{2,10},{3,11},{4,12},{5,13},{6,14},{7,15},{8,0},{9,1},... | collective-permute-start | bytes 589832 | tf_op jit(solution)/shard_map/ppermute | solution.py:366
  61.3 12.1 %collective-permute-start.10 = (f32[1,96,128]{2,1,0:T(8,128)S(1)}, f32[1,96,128]{2,1,0:T(8,128)S(1)}, u32[]{:S(2)}, u32[]{:S(2)}) collective-permute-start(f32[1,96,128]{2,1,0:T(8,128)S(1)} %get-tuple-element.33), channel_id=1, source_target_pairs={{0,1},{1,2},{2,3},{3,4},{4,5},{5,6},{6,7},{7,8},{8,9},{9,10},{10,1... | collective-permute-start | bytes 147464 | tf_op jit(solution)/shard_map/ppermute | solution.py:371
  64.7 8.7 %collective-permute-start.12 = (f32[1,96,128]{2,1,0:T(8,128)S(1)}, f32[1,96,128]{2,1,0:T(8,128)S(1)}, u32[]{:S(2)}, u32[]{:S(2)}) collective-permute-start(f32[1,96,128]{2,1,0:T(8,128)S(1)} %get-tuple-element.35), channel_id=1, source_target_pairs={{1,0},{2,1},{3,2},{4,3},{5,4},{6,5},{7,6},{8,7},{9,8},{10,9},{11,1... | collective-permute-start | bytes 147464 | tf_op jit(solution)/shard_map/ppermute | solution.py:370
  66.6 7.9 %collective-permute-start.11 = (f32[1,96,128]{2,1,0:T(8,128)S(1)}, f32[1,96,128]{2,1,0:T(8,128)S(1)}, u32[]{:S(2)}, u32[]{:S(2)}) collective-permute-start(f32[1,96,128]{2,1,0:T(8,128)S(1)} %get-tuple-element.34), channel_id=1, source_target_pairs={{0,9},{1,10},{2,11},{3,12},{4,13},{5,14},{6,15},{8,1},{9,2},{10,3}... | collective-permute-start | bytes 147464 | tf_op jit(solution)/shard_map/ppermute | solution.py:368
  70.6 7.2 %collective-permute-start.13 = (f32[1,96,128]{2,1,0:T(8,128)S(1)}, f32[1,96,128]{2,1,0:T(8,128)S(1)}, u32[]{:S(2)}, u32[]{:S(2)}) collective-permute-start(f32[1,96,128]{2,1,0:T(8,128)S(1)} %get-tuple-element.36), channel_id=1, source_target_pairs={{0,7},{1,8},{2,9},{3,10},{4,11},{5,12},{6,13},{7,14},{9,0},{10,1},... | collective-permute-start | bytes 147464 | tf_op jit(solution)/shard_map/ppermute | solution.py:367

commit v3 on v2

--- a/solution.py
+++ b/solution.py
@@ -20,8 +20,8 @@
 ANY = pl.BlockSpec(memory_space=pl.ANY)
 
 
-def pack_kernel(half, apart, route_ref, target_ref, start_ref, source_ref, far_ref, *rest):
-    own_refs = rest[:-3]
+def pack_kernel(half, apart, route_ref, target_ref, start_ref, source_ref, *rest):
+    packed_refs = rest[:-3]
     slot_ref, count_ref, sem = rest[-3:]
     items, channels, pixels = source_ref.shape
     side = lax.div(lax.axis_index("views"), half)
@@ -45,15 +45,16 @@
                 place = count_ref[t * half + home]
                 count_ref[t * half + home] = place + 1
                 first = pl.multiple_of(place * channels, channels)
-                if t == 0 and apart:
-                    for k, own_ref in enumerate(own_refs):
+                if apart:
+                    for k in range(half):
 
                         @pl.when(home == here ^ k)
                         def _():
-                            target = own_ref.at[pl.ds(first, channels), :]
+                            target = packed_refs[(1 - t) * half + k]
+                            target = target.at[pl.ds(first, channels), :]
                             pltpu.make_async_copy(source_ref.at[i], target, sem).start()
                 else:
-                    target = (own_refs[0], far_ref)[t].at[home, pl.ds(first, channels), :]
+                    target = packed_refs[1 - t].at[home, pl.ds(first, channels), :]
                     pltpu.make_async_copy(source_ref.at[i], target, sem).start()
                 value = jnp.full((1, pixels), rest.astype(jnp.float32))
                 line = slot_ref[pl.ds(home, 1), :]
@@ -61,16 +62,17 @@
 
     @pl.loop(0, items)
     def _(i):
-        pltpu.make_async_copy(
-            source_ref.at[0], far_ref.at[0, pl.ds(0, channels), :], sem
-        ).wait()
+        target = packed_refs[0] if apart else packed_refs[0].at[0]
+        pltpu.make_async_copy(source_ref.at[0], target.at[pl.ds(0, channels), :], sem).wait()
 
 
 def pack_rows(route, target, start, source, half, apart):
     _, channels, pixels = source.shape
-    length = CAP * channels
-    shapes = [(half, length + NOTE, pixels)]
-    shapes += [(length, pixels)] * half if apart else [(half, length, pixels)]
+    lengths = (CAP * channels + NOTE, CAP * channels)
+    if apart:
+        shapes = [(length, pixels) for length in lengths for _ in range(half)]
+    else:
+        shapes = [(half, length, pixels) for length in lengths]
     outs = [jax.ShapeDtypeStruct(shape, source.dtype) for shape in shapes]
     return pl.pallas_call(
         functools.partial(pack_kernel, half, apart),
@@ -83,36 +85,53 @@
     )(keep(route), keep(target), keep(start), keep(source))
 
 
-def note_kernel(packed_ref, slot_ref, near_ref, far_ref, out_ref, block_ref, sem):
+def note_kernel(count, slot_ref, near_ref, far_ref, *rest):
+    out_refs = rest[count:-2]
+    block_ref, sems = rest[-2:]
     half, pixels = slot_ref.shape
+    here = lax.rem(lax.axis_index("views"), half)
     fixed = [near_ref[...].astype(jnp.float32), far_ref[...].astype(jnp.float32)]
-    rest = jnp.zeros((NOTE - 5, pixels), jnp.float32)
-
-    @pl.loop(0, half)
-    def _(j):
-        lines = fixed + [slot_ref[pl.ds(j, 1), :], rest]
-        block_ref[j] = jnp.concatenate(lines, axis=0).astype(block_ref.dtype)
-
-    first = out_ref.shape[1] - NOTE
-    copy = pltpu.make_async_copy(block_ref, out_ref.at[:, pl.ds(first, NOTE), :], sem)
-    copy.start()
-    copy.wait()
+    blank = jnp.zeros((NOTE - 5, pixels), jnp.float32)
+    copies = []
+    for k in range(count):
+        for j in [here ^ k] if count > 1 else []:
+            lines = fixed + [slot_ref[pl.ds(j, 1), :], blank]
+            block_ref[k] = jnp.concatenate(lines, axis=0).astype(block_ref.dtype)
+            first = out_refs[k].shape[0] - NOTE
+            target = out_refs[k].at[pl.ds(first, NOTE), :]
+            copies.append(pltpu.make_async_copy(block_ref.at[k], target, sems.at[k]))
+    if count == 1:
+
+        @pl.loop(0, half)
+        def _(j):
+            lines = fixed + [slot_ref[pl.ds(j, 1), :], blank]
+            block_ref[j] = jnp.concatenate(lines, axis=0).astype(block_ref.dtype)
+
+        first = out_refs[0].shape[1] - NOTE
+        target = out_refs[0].at[:, pl.ds(first, NOTE), :]
+        copies.append(pltpu.make_async_copy(block_ref, target, sems.at[0]))
+    for copy in copies:
+        copy.start()
+    for copy in copies:
+        copy.wait()
 
 
 def add_note(packed, slots, near, far):
+    count = len(packed)
+    hbm = pl.BlockSpec(memory_space=pltpu.HBM)
     return pl.pallas_call(
-        note_kernel,
-        out_shape=jax.ShapeDtypeStruct(packed.shape, packed.dtype),
-        in_specs=[ANY, VMEM, VMEM, VMEM],
-        out_specs=ANY,
+        functools.partial(note_kernel, count),
+        out_shape=[jax.ShapeDtypeStruct(part.shape, part.dtype) for part in packed],
+        in_specs=[VMEM, VMEM, VMEM] + [hbm] * count,
+        out_specs=[hbm] * count,
         scratch_shapes=[
-            pltpu.VMEM((packed.shape[0], NOTE, packed.shape[2]), packed.dtype),
-            pltpu.SemaphoreType.DMA,
+            pltpu.VMEM((slots.shape[0], NOTE, slots.shape[1]), packed[0].dtype),
+            pltpu.SemaphoreType.DMA((count,)),
         ],
-        input_output_aliases={0: 0},
+        input_output_aliases={3 + k: k for k in range(count)},
         compiler_params=pltpu.CompilerParams(vmem_limit_bytes=4 << 20),
         name="add_note",
-    )(packed, slots, near, far)
+    )(slots, near, far, *packed)
 
 
 def keep(values):
@@ -203,7 +222,7 @@
 
     if len(arrived_refs) > 1:
         for k, arrived_ref in enumerate(arrived_refs):
-            add_slots(lax.rem(lax.axis_index("views"), half) ^ k, arrived_ref)
+            add_slots(k, arrived_ref)
     else:
 
         @pl.loop(0, half)
@@ -342,18 +361,27 @@
     far_named = send(named, perm=home)
     far_rows = send(reference_rows, perm=home)
     apart = half <= 8
-    packed_far, *packed_own, slots = pack_rows(
+    *packed, slots = pack_rows(
         owner, target_row, start_index, source_rows, half, apart
     )
-    packed_far = add_note(packed_far, slots, named, far_named)
-    arrived_far = swap(packed_far)
+    count = len(packed) // SETS
+    packed_far = list(add_note(packed[:count], slots, named, far_named))
+    packed_own = list(packed[count:])
+
+    def swap_all(parts):
+        if not apart:
+            return [swap(parts[0])]
+        arrived = parts[:1] + [None] * (half - 1)
+        for k in sorted(range(1, half), key=lambda k: (k < half // 2, -k % 2, -k)):
+            arrived[k] = send(parts[k], perm=[(i, i ^ k) for i in range(views)])
+        return arrived
+
+    arrived_far = swap_all(packed_far)
+    arrived_own = swap_all(packed_own)
     if apart:
-        arrived_own = packed_own[:1] + [None] * (half - 1)
-        for k in sorted(range(1, half), key=lambda k: (k < half // 2, -k % 2, -k)):
-            arrived_own[k] = send(packed_own[k], perm=[(i, i ^ k) for i in range(views)])
+        note = jnp.stack([part[CAP * channels :] for part in arrived_far])
     else:
-        arrived_own = [swap(packed_own[0])]
-    note = arrived_far[:, CAP * channels :]
+        note = arrived_far[0][:, CAP * channels :]
     codes = note[:, 4, : SETS * CAP].astype(jnp.int32).reshape(-1)
 
     scaled = jnp.repeat(conv_weight / CG, CG, axis=0)
@@ -362,7 +390,7 @@
     edges = jnp.pad(scaled[..., 2], ((0, 0), (0, 0), (0, 5))).reshape(-1, 24)
     edges = jnp.roll(jnp.pad(edges, ((0, 0), (0, pixels - 24))), -2, 1)
     near, far = stack_left(reference_rows), stack_left(far_rows)
-    far_main, far_low, far_high = add_set(1, codes, note, far, taps, edges, arrived_far)
+    far_main, far_low, far_high = add_set(1, codes, note, far, taps, edges, *arrived_far)
     other_main = send(far_main, perm=home)
     other_low = send(far_low, perm=[(i, j - 1) for i, j in home if j > 0])
     other_high = send(far_high, perm=[(i, j + 1) for i, j in home if j + 1 < views])

time: 79.2 us -> 99.8 us (1.26)
  the two profiles are of different devices: /device:TPU:1 before, /device:TPU:7 now
where the time goes in v3:
time: 99.8 us; the launch traced here: 99.4 us
  starting transfers between devices  36.6 us (37%)
  waiting for transfers between devices  35.6 us (36%)
  Pallas kernels  17.6 us (18%)
  local copies, waits for them, and re-layouts  7.84 us (8%)
  other arithmetic  1.53 us (2%)
    ppermute x14, waiting for transfers between devices, swap_all(): arrived[k] = send(parts[k], perm=[(i, i ^ k) for i in range(views)])  29.4 us
    ppermute x14, starting transfers between devices, swap_all(): arrived[k] = send(parts[k], perm=[(i, i ^ k) for i in range(views)])  18.1 us
    pallas_call x2, Pallas kernels, add_set(): pl.pallas_call(functools.partial(set_kernel, t), out_shape=[jax.ShapeDtyp...  12.3 us
    ppermute x1, waiting for transfers between devices, compute(): other_low = send(far_low, perm=[(i, j - 1) for i, j in home if j > 0])  6.15 us
    ppermute x1, starting transfers between devices, compute(): send(far_high, perm=[(i, j + 1) for i, j in home if j + 1 < views])  6.12 us
    ppermute x1, starting transfers between devices, compute(): own_high = send(own_high, perm=[(i, i + 1) for i in range(views - 1)])  3.65 us
    pallas_call x1, Pallas kernels, pack_rows(): pl.pallas_call(functools.partial(pack_kernel, half, apart), out_shape=out...  3.34 us
    ppermute x1, starting transfers between devices, compute(): other_main = send(far_main, perm=home)  2.49 us
  transfers between devices with their start and end apart: 21, of which 8 were waited for; matrix products, arithmetic and copies ran while one was open for 7% of the time, Pallas kernels for 17%

profile of v3, /device:TPU:7, one launch (start us, length us, event | category | flops | bytes accessed | tf_op | source)
XLA Modules:
  0.0 99.4 jit_solution(7245417460742085226)
XLA Ops:
  0.7 2.4 %collective-permute-start = (bf16[2,128]{1,0:T(2,128)(2,1)S(1)}, bf16[2,128]{1,0:T(2,128)(2,1)S(1)}, u32[]{:S(2)}, u32[]{:S(2)}) collective-permute-start(bf16[2,128]{1,0:T(2,128)(2,1)S(1)} %fusion.3.near_ref), channel_id=1, source_target_pairs={{0,8},{1,9},{2,10},{3,11},{4,12},{5,13},{6,14},{7,15},{8,0},{9,1},... | collective-permute-start | bytes 1544 | tf_op jit(solution)/shard_map/ppermute | solution.py:361
  3.2 3.3 %pack_rows.1 = (bf16[656,128]{1,0:T(8,128)(2,1)S(1)}, bf16[656,128]{1,0:T(8,128)(2,1)S(1)}, bf16[656,128]{1,0:T(8,128)(2,1)S(1)}, bf16[656,128]{1,0:T(8,128)(2,1...) custom-call(s32[12]{0:T(128)} %bitcast.51, ...), custom_call_target="tpu_custom_call" | custom-call | tf_op jit(solution)/shard_map/pack_rows/pallas_call | solution.py:77
  6.5 1.4 %collective-permute-start.10 = (bf16[640,128]{1,0:T(8,128)(2,1)}, bf16[640,128]{1,0:T(8,128)(2,1)S(1)}, u32[]{:S(2)}, u32[]{:S(2)}) collective-permute-start(bf16[640,128]{1,0:T(8,128)(2,1)} %get-tuple-element.56), channel_id=1, source_target_pairs={{0,3},{1,2},{2,1},{3,0},{4,7},{5,6},{6,5},{7,4},{8,11},{9,10},{10,... | collective-permute-start | bytes 491528 | tf_op jit(solution)/shard_map/ppermute | solution.py:376
  7.9 1.7 %collective-permute-start.11 = (bf16[640,128]{1,0:T(8,128)(2,1)}, bf16[640,128]{1,0:T(8,128)(2,1)S(1)}, u32[]{:S(2)}, u32[]{:S(2)}) collective-permute-start(bf16[640,128]{1,0:T(8,128)(2,1)} %get-tuple-element.57), channel_id=1, source_target_pairs={{0,4},{1,5},{2,6},{3,7},{4,0},{5,1},{6,2},{7,3},{8,12},{9,13},{10,... | collective-permute-start | bytes 491528 | tf_op jit(solution)/shard_map/ppermute | solution.py:376
  10.0 1.0 %broadcast_in_dim.3 = f32[40,8,3,3,3]{1,0,4,3,2:T(8,128)} broadcast(f32[40,3,3,3]{0,3,2,1:T(4,128)S(1)} %broadcast_multiply_fusion), dimensions={0,2,3,4} | broadcast | bytes 38880 | tf_op jit(solution)/shard_map/broadcast_in_dim | solution.py:387
  11.0 1.3 %reshape.13 = f32[320,3,3,3]{0,3,2,1:T(4,128)S(1)} reshape(f32[40,8,3,3,3]{1,0,4,3,2:T(8,128)} %broadcast_in_dim.3) | data formatting | bytes 69120 | tf_op jit(solution)/shard_map/reshape | solution.py:387
  14.1 1.0 %copy-done = bf16[4,128,960]{2,1,0:T(8,128)(2,1)} copy-done((bf16[4,128,960]{2,1,0:T(8,128)(2,1)}, bf16[4,128,960]{2,1,0:T(8,128)(2,1)S(1)}, u32[]{:S(2)}) %copy-start) | copy-done | bytes 983064
  15.2 1.0 %copy.21 = f32[960,9]{1,0:T(8,128)} copy(f32[960,9]{0,1:T(8,128)S(1)} %reshape.14) | data formatting | bytes 69120 | tf_op jit(solution)/shard_map/reshape | solution.py:388
  16.2 1.9 %pad.17.weight_ref = f32[960,128]{1,0:T(8,128)} pad(f32[960,9]{1,0:T(8,128)} %copy.21, f32[]{:T(128)} %constant.10.clone.1), padding=0_0x0_119 | pad | bytes 526084 | tf_op jit(solution)/shard_map/jit(_pad)/pad | solution.py:389
  18.4 1.3 %collective-permute-done.1.rest_1_ = bf16[656,128]{1,0:T(8,128)(2,1)S(1)} collective-permute-done((bf16[656,128]{1,0:T(8,128)(2,1)S(1)}, bf16[656,128]{1,0:T(8,128)(2,1)S(1)}, u32[]{:S(2)}, u32[]{:S(2)}) %collective-permute-start.1) | collective-permute-done | bytes 167968 | tf_op jit(solution)/shard_map/ppermute | solution.py:376
  19.7 1.1 %collective-permute-start.2 = (bf16[656,128]{1,0:T(8,128)(2,1)S(1)}, bf16[656,128]{1,0:T(8,128)(2,1)S(1)}, u32[]{:S(2)}, u32[]{:S(2)}) collective-permute-start(bf16[656,128]{1,0:T(8,128)(2,1)S(1)} %get-tuple-element.47), channel_id=1, source_target_pairs={{0,2},{1,3},{2,0},{3,1},{4,6},{5,7},{6,4},{7,5},{8,10},{9,11},{10,... | collective-permute-start | bytes 503816 | tf_op jit(solution)/shard_map/ppermute | solution.py:376
  20.8 4.6 %collective-permute-done.2.rest_2_ = bf16[656,128]{1,0:T(8,128)(2,1)S(1)} collective-permute-done((bf16[656,128]{1,0:T(8,128)(2,1)S(1)}, bf16[656,128]{1,0:T(8,128)(2,1)S(1)}, u32[]{:S(2)}, u32[]{:S(2)}) %collective-permute-start.2) | collective-permute-done | bytes 167968 | tf_op jit(solution)/shard_map/ppermute | solution.py:376
  25.4 2.0 %collective-permute-start.3 = (bf16[656,128]{1,0:T(8,128)(2,1)S(1)}, bf16[656,128]{1,0:T(8,128)(2,1)S(1)}, u32[]{:S(2)}, u32[]{:S(2)}) collective-permute-start(bf16[656,128]{1,0:T(8,128)(2,1)S(1)} %get-tuple-element.48), channel_id=1, source_target_pairs={{0,3},{1,2},{2,1},{3,0},{4,7},{5,6},{6,5},{7,4},{8,11},{9,10},{10,... | collective-permute-start | bytes 503816 | tf_op jit(solution)/shard_map/ppermute | solution.py:376
  27.4 5.1 %collective-permute-done.3.rest_3_ = bf16[656,128]{1,0:T(8,128)(2,1)S(1)} collective-permute-done((bf16[656,128]{1,0:T(8,128)(2,1)S(1)}, bf16[656,128]{1,0:T(8,128)(2,1)S(1)}, u32[]{:S(2)}, u32[]{:S(2)}) %collective-permute-start.3) | collective-permute-done | bytes 167968 | tf_op jit(solution)/shard_map/ppermute | solution.py:376
  33.1 4.8 %collective-permute-done.4.rest_4_ = bf16[656,128]{1,0:T(8,128)(2,1)S(1)} collective-permute-done((bf16[656,128]{1,0:T(8,128)(2,1)S(1)}, bf16[656,128]{1,0:T(8,128)(2,1)S(1)}, u32[]{:S(2)}, u32[]{:S(2)}) %collective-permute-start.4) | collective-permute-done | bytes 167968 | tf_op jit(solution)/shard_map/ppermute | solution.py:376
  37.9 1.7 %collective-permute-start.5 = (bf16[656,128]{1,0:T(8,128)(2,1)S(1)}, bf16[656,128]{1,0:T(8,128)(2,1)S(1)}, u32[]{:S(2)}, u32[]{:S(2)}) collective-permute-start(bf16[656,128]{1,0:T(8,128)(2,1)S(1)} %get-tuple-element.50), channel_id=1, source_target_pairs={{0,5},{1,4},{2,7},{3,6},{4,1},{5,0},{6,3},{7,2},{8,13},{9,12},{10,... | collective-permute-start | bytes 503816 | tf_op jit(solution)/shard_map/ppermute | solution.py:376
  39.7 4.5 %collective-permute-done.5.rest_5_ = bf16[656,128]{1,0:T(8,128)(2,1)S(1)} collective-permute-done((bf16[656,128]{1,0:T(8,128)(2,1)S(1)}, bf16[656,128]{1,0:T(8,128)(2,1)S(1)}, u32[]{:S(2)}, u32[]{:S(2)}) %collective-permute-start.5) | collective-permute-done | bytes 167968 | tf_op jit(solution)/shard_map/ppermute | solution.py:376
  45.0 5.0 %collective-permute-done.6.rest_6_ = bf16[656,128]{1,0:T(8,128)(2,1)S(1)} collective-permute-done((bf16[656,128]{1,0:T(8,128)(2,1)S(1)}, bf16[656,128]{1,0:T(8,128)(2,1)S(1)}, u32[]{:S(2)}, u32[]{:S(2)}) %collective-permute-start.6) | collective-permute-done | bytes 167968 | tf_op jit(solution)/shard_map/ppermute | solution.py:376
  49.9 2.5 %collective-permute-start.7 = (bf16[656,128]{1,0:T(8,128)(2,1)S(1)}, bf16[656,128]{1,0:T(8,128)(2,1)S(1)}, u32[]{:S(2)}, u32[]{:S(2)}) collective-permute-start(bf16[656,128]{1,0:T(8,128)(2,1)S(1)} %get-tuple-element.52), channel_id=1, source_target_pairs={{0,7},{1,6},{2,5},{3,4},{4,3},{5,2},{6,1},{7,0},{8,15},{9,14},{10,... | collective-permute-start | bytes 503816 | tf_op jit(solution)/shard_map/ppermute | solution.py:376
  52.5 4.1 %collective-permute-done.7.rest_7_ = bf16[656,128]{1,0:T(8,128)(2,1)S(1)} collective-permute-done((bf16[656,128]{1,0:T(8,128)(2,1)S(1)}, bf16[656,128]{1,0:T(8,128)(2,1)S(1)}, u32[]{:S(2)}, u32[]{:S(2)}) %collective-permute-start.7) | collective-permute-done | bytes 167968 | tf_op jit(solution)/shard_map/ppermute | solution.py:376
  56.6 2.2 %collective-permute-start.13 = (bf16[640,128]{1,0:T(8,128)(2,1)S(1)}, bf16[640,128]{1,0:T(8,128)(2,1)S(1)}, u32[]{:S(2)}, u32[]{:S(2)}) collective-permute-start(bf16[640,128]{1,0:T(8,128)(2,1)S(1)} %get-tuple-element.59), channel_id=1, source_target_pairs={{0,6},{1,7},{2,4},{3,5},{4,2},{5,3},{6,0},{7,1},{8,14},{9,15},{10,... | collective-permute-start | bytes 491528 | tf_op jit(solution)/shard_map/ppermute | solution.py:376
  58.8 2.0 %collective-permute-start.14 = (bf16[640,128]{1,0:T(8,128)(2,1)S(1)}, bf16[640,128]{1,0:T(8,128)(2,1)S(1)}, u32[]{:S(2)}, u32[]{:S(2)}) collective-permute-start(bf16[640,128]{1,0:T(8,128)(2,1)S(1)} %get-tuple-element.60), channel_id=1, source_target_pairs={{0,7},{1,6},{2,5},{3,4},{4,3},{5,2},{6,1},{7,0},{8,15},{9,14},{10,... | collective-permute-start | bytes 491528 | tf_op jit(solution)/shard_map/ppermute | solution.py:376
  61.4 1.0 copy-done.1
  62.3 1.6 %collective-permute-start.9 = (bf16[640,128]{1,0:T(8,128)(2,1)S(1)}, bf16[640,128]{1,0:T(8,128)(2,1)S(1)}, u32[]{:S(2)}, u32[]{:S(2)}) collective-permute-start(bf16[640,128]{1,0:T(8,128)(2,1)S(1)} %get-tuple-element.55), channel_id=1, source_target_pairs={{0,2},{1,3},{2,0},{3,1},{4,6},{5,7},{6,4},{7,5},{8,10},{9,11},{10,... | collective-permute-start | bytes 491528 | tf_op jit(solution)/shard_map/ppermute | solution.py:376
  63.9 6.2 %add_set.3 = (f32[4,96,128]{2,1,0:T(8,128)S(1)}, f32[1,96,128]{2,1,0:T(8,128)S(1)}, f32[1,96,128]{2,1,0:T(8,128)S(1)}) custom-call(s32[32]{0:T(128)S(1)} %reshape.16.code_ref, bf16[8,16,128]{2,1,0:T(8,128)(2,1)S(1)} %constant_dynamic-update-slice_fusion.note_ref, bf16[4,128,960]{2,1,0:T(8,128)(2,1)} %copy-done.1, f32[960,128]{1,0:T(8,128)} %pad.17.weight_ref, ...), custom_call_target="tpu_custom_call" | custom-call | flops 2264924160 | bytes 1343488 | tf_op jit(solution)/shard_map/add_set/pallas_call | solution.py:284
  70.1 2.5 %collective-permute-start.16 = (f32[4,96,128]{2,1,0:T(8,128)S(1)}, f32[4,96,128]{2,1,0:T(8,128)S(1)}, u32[]{:S(2)}, u32[]{:S(2)}) collective-permute-start(f32[4,96,128]{2,1,0:T(8,128)S(1)} %get-tuple-element.62), channel_id=1, source_target_pairs={{0,8},{1,9},{2,10},{3,11},{4,12},{5,13},{6,14},{7,15},{8,0},{9,1},... | collective-permute-start | bytes 589832 | tf_op jit(solution)/shard_map/ppermute | solution.py:394
  72.6 6.2 %add_set.2 = (f32[4,96,128]{2,1,0:T(8,128)S(1)}, f32[1,96,128]{2,1,0:T(8,128)S(1)}, f32[1,96,128]{2,1,0:T(8,128)S(1)}) custom-call(s32[32]{0:T(128)S(1)} %reshape.16.code_ref, bf16[8,16,128]{2,1,0:T(8,128)(2,1)S(1)} %constant_dynamic-update-slice_fusion.note_ref, bf16[4,128,960]{2,1,0:T(8,128)(2,1)} %copy-done, f32[960,128]{1,0:T(8,128)} %pad.17.weight_ref, ...), custom_call_target="tpu_custom_call" | custom-call | flops 2264924160 | bytes 1310720 | tf_op jit(solution)/shard_map/add_set/pallas_call | solution.py:284
  78.8 3.7 %collective-permute-start.17 = (f32[1,96,128]{2,1,0:T(8,128)S(1)}, f32[1,96,128]{2,1,0:T(8,128)S(1)}, u32[]{:S(2)}, u32[]{:S(2)}) collective-permute-start(f32[1,96,128]{2,1,0:T(8,128)S(1)} %get-tuple-element.63), channel_id=1, source_target_pairs={{0,1},{1,2},{2,3},{3,4},{4,5},{5,6},{6,7},{7,8},{8,9},{9,10},{10,1... | collective-permute-start | bytes 147464 | tf_op jit(solution)/shard_map/ppermute | solution.py:399
  82.5 1.9 %collective-permute-start.19 = (f32[1,96,128]{2,1,0:T(8,128)S(1)}, f32[1,96,128]{2,1,0:T(8,128)S(1)}, u32[]{:S(2)}, u32[]{:S(2)}) collective-permute-start(f32[1,96,128]{2,1,0:T(8,128)S(1)} %get-tuple-element.65), channel_id=1, source_target_pairs={{1,0},{2,1},{3,2},{4,3},{5,4},{6,5},{7,6},{8,7},{9,8},{10,9},{11,1... | collective-permute-start | bytes 147464 | tf_op jit(solution)/shard_map/ppermute | solution.py:398
  84.4 6.1 %collective-permute-start.18 = (f32[1,96,128]{2,1,0:T(8,128)S(1)}, f32[1,96,128]{2,1,0:T(8,128)S(1)}, u32[]{:S(2)}, u32[]{:S(2)}) collective-permute-start(f32[1,96,128]{2,1,0:T(8,128)S(1)} %get-tuple-element.64), channel_id=1, source_target_pairs={{0,9},{1,10},{2,11},{3,12},{4,13},{5,14},{6,15},{8,1},{9,2},{10,3}... | collective-permute-start | bytes 147464 | tf_op jit(solution)/shard_map/ppermute | solution.py:396
  90.5 1.9 %collective-permute-start.20 = (f32[1,96,128]{2,1,0:T(8,128)S(1)}, f32[1,96,128]{2,1,0:T(8,128)S(1)}, u32[]{:S(2)}, u32[]{:S(2)}) collective-permute-start(f32[1,96,128]{2,1,0:T(8,128)S(1)} %get-tuple-element.66), channel_id=1, source_target_pairs={{0,7},{1,8},{2,9},{3,10},{4,11},{5,12},{6,13},{7,14},{9,0},{10,1},... | collective-permute-start | bytes 147464 | tf_op jit(solution)/shard_map/ppermute | solution.py:395
  92.5 6.1 %collective-permute-done.20.after_far_ref = f32[1,96,128]{2,1,0:T(8,128)S(1)} collective-permute-done((f32[1,96,128]{2,1,0:T(8,128)S(1)}, f32[1,96,128]{2,1,0:T(8,128)S(1)}, u32[]{:S(2)}, u32[]{:S(2)}) %collective-permute-start.20) | collective-permute-done | bytes 49184 | tf_op jit(solution)/shard_map/ppermute | solution.py:395
  (54 shorter events, 6.0 us)
Async XLA Ops:
  0.0 0.7 copy-start.4
  0.0 0.7 copy-start.5
  0.7 17.4 %collective-permute-start = (bf16[2,128]{1,0:T(2,128)(2,1)S(1)}, bf16[2,128]{1,0:T(2,128)(2,1)S(1)}, u32[]{:S(2)}, u32[]{:S(2)}) collective-permute-start(bf16[2,128]{1,0:T(2,128)(2,1)S(1)} %fusion.3.near_ref), channel_id=1, source_target_pairs={{0,8},{1,9},{2,10},{3,11},{4,12},{5,13},{6,14},{7,15},{8,0},{9,1},... | collective-permute-start | bytes 1544 | tf_op jit(solution)/shard_map/ppermute | solution.py:361
  3.1 55.7 %collective-permute-start.15 = (bf16[4,320,128]{2,1,0:T(8,128)(2,1)}, bf16[4,320,128]{2,1,0:T(8,128)(2,1)S(1)}, u32[]{:S(2)}, u32[]{:S(2)}) collective-permute-start(bf16[4,320,128]{2,1,0:T(8,128)(2,1)} %reference_ref.1), channel_id=1, source_target_pairs={{0,8},{1,9},{2,10},{3,11},{4,12},{5,13},{6,14},{7,15},{8,0},{9,1},... | collective-permute-start | bytes 983048 | tf_op jit(solution)/shard_map/ppermute | solution.py:362
  3.2 6.8 %copy-start.3 = (f32[40,3,3,3]{0,3,2,1:T(4,128)S(1)}, f32[40,3,3,3]{0,3,2,1:T(4,128)}, u32[]{:S(2)}) copy-start(f32[40,3,3,3]{0,3,2,1:T(4,128)} %param.11) | copy-start | bytes 12964
  6.5 55.8 %collective-permute-start.10 = (bf16[640,128]{1,0:T(8,128)(2,1)}, bf16[640,128]{1,0:T(8,128)(2,1)S(1)}, u32[]{:S(2)}, u32[]{:S(2)}) collective-permute-start(bf16[640,128]{1,0:T(8,128)(2,1)} %get-tuple-element.56), channel_id=1, source_target_pairs={{0,3},{1,2},{2,1},{3,0},{4,7},{5,6},{6,5},{7,4},{8,11},{9,10},{10,... | collective-permute-start | bytes 491528 | tf_op jit(solution)/shard_map/ppermute | solution.py:376
  7.9 54.4 %collective-permute-start.11 = (bf16[640,128]{1,0:T(8,128)(2,1)}, bf16[640,128]{1,0:T(8,128)(2,1)S(1)}, u32[]{:S(2)}, u32[]{:S(2)}) collective-permute-start(bf16[640,128]{1,0:T(8,128)(2,1)} %get-tuple-element.57), channel_id=1, source_target_pairs={{0,4},{1,5},{2,6},{3,7},{4,0},{5,1},{6,2},{7,3},{8,12},{9,13},{10,... | collective-permute-start | bytes 491528 | tf_op jit(solution)/shard_map/ppermute | solution.py:376
  9.6 60.5 %collective-permute-start.12 = (bf16[640,128]{1,0:T(8,128)(2,1)S(1)}, bf16[640,128]{1,0:T(8,128)(2,1)S(1)}, u32[]{:S(2)}, u32[]{:S(2)}) collective-permute-start(bf16[640,128]{1,0:T(8,128)(2,1)S(1)} %get-tuple-element.58), channel_id=1, source_target_pairs={{0,5},{1,4},{2,7},{3,6},{4,1},{5,0},{6,3},{7,2},{8,13},{9,12},{10,... | collective-permute-start | bytes 491528 | tf_op jit(solution)/shard_map/ppermute | solution.py:376
  12.6 1.0 copy-start.2
  14.1 1.0 %copy-start = (bf16[4,128,960]{2,1,0:T(8,128)(2,1)}, bf16[4,128,960]{2,1,0:T(8,128)(2,1)S(1)}, u32[]{:S(2)}) copy-start(bf16[4,128,960]{2,1,0:T(8,128)(2,1)S(1)} %stack_left.2.left_ref) | copy-start | bytes 2949124
  18.2 1.5 %collective-permute-start.1 = (bf16[656,128]{1,0:T(8,128)(2,1)S(1)}, bf16[656,128]{1,0:T(8,128)(2,1)S(1)}, u32[]{:S(2)}, u32[]{:S(2)}) collective-permute-start(bf16[656,128]{1,0:T(8,128)(2,1)S(1)} %get-tuple-element.46), channel_id=1, source_target_pairs={{0,1},{1,0},{2,3},{3,2},{4,5},{5,4},{6,7},{7,6},{8,9},{9,8},{10,11... | collective-permute-start | bytes 503816 | tf_op jit(solution)/shard_map/ppermute | solution.py:376
  19.7 5.7 %collective-permute-start.2 = (bf16[656,128]{1,0:T(8,128)(2,1)S(1)}, bf16[656,128]{1,0:T(8,128)(2,1)S(1)}, u32[]{:S(2)}, u32[]{:S(2)}) collective-permute-start(bf16[656,128]{1,0:T(8,128)(2,1)S(1)} %get-tuple-element.47), channel_id=1, source_target_pairs={{0,2},{1,3},{2,0},{3,1},{4,6},{5,7},{6,4},{7,5},{8,10},{9,11},{10,... | collective-permute-start | bytes 503816 | tf_op jit(solution)/shard_map/ppermute | solution.py:376
  25.4 7.1 %collective-permute-start.3 = (bf16[656,128]{1,0:T(8,128)(2,1)S(1)}, bf16[656,128]{1,0:T(8,128)(2,1)S(1)}, u32[]{:S(2)}, u32[]{:S(2)}) collective-permute-start(bf16[656,128]{1,0:T(8,128)(2,1)S(1)} %get-tuple-element.48), channel_id=1, source_target_pairs={{0,3},{1,2},{2,1},{3,0},{4,7},{5,6},{6,5},{7,4},{8,11},{9,10},{10,... | collective-permute-start | bytes 503816 | tf_op jit(solution)/shard_map/ppermute | solution.py:376
  32.5 5.4 %collective-permute-start.4 = (bf16[656,128]{1,0:T(8,128)(2,1)S(1)}, bf16[656,128]{1,0:T(8,128)(2,1)S(1)}, u32[]{:S(2)}, u32[]{:S(2)}) collective-permute-start(bf16[656,128]{1,0:T(8,128)(2,1)S(1)} %get-tuple-element.49), channel_id=1, source_target_pairs={{0,4},{1,5},{2,6},{3,7},{4,0},{5,1},{6,2},{7,3},{8,12},{9,13},{10,... | collective-permute-start | bytes 503816 | tf_op jit(solution)/shard_map/ppermute | solution.py:376
  37.9 6.3 %collective-permute-start.5 = (bf16[656,128]{1,0:T(8,128)(2,1)S(1)}, bf16[656,128]{1,0:T(8,128)(2,1)S(1)}, u32[]{:S(2)}, u32[]{:S(2)}) collective-permute-start(bf16[656,128]{1,0:T(8,128)(2,1)S(1)} %get-tuple-element.50), channel_id=1, source_target_pairs={{0,5},{1,4},{2,7},{3,6},{4,1},{5,0},{6,3},{7,2},{8,13},{9,12},{10,... | collective-permute-start | bytes 503816 | tf_op jit(solution)/shard_map/ppermute | solution.py:376
  44.2 5.7 %collective-permute-start.6 = (bf16[656,128]{1,0:T(8,128)(2,1)S(1)}, bf16[656,128]{1,0:T(8,128)(2,1)S(1)}, u32[]{:S(2)}, u32[]{:S(2)}) collective-permute-start(bf16[656,128]{1,0:T(8,128)(2,1)S(1)} %get-tuple-element.51), channel_id=1, source_target_pairs={{0,6},{1,7},{2,4},{3,5},{4,2},{5,3},{6,0},{7,1},{8,14},{9,15},{10,... | collective-permute-start | bytes 503816 | tf_op jit(solution)/shard_map/ppermute | solution.py:376
  49.9 6.6 %collective-permute-start.7 = (bf16[656,128]{1,0:T(8,128)(2,1)S(1)}, bf16[656,128]{1,0:T(8,128)(2,1)S(1)}, u32[]{:S(2)}, u32[]{:S(2)}) collective-permute-start(bf16[656,128]{1,0:T(8,128)(2,1)S(1)} %get-tuple-element.52), channel_id=1, source_target_pairs={{0,7},{1,6},{2,5},{3,4},{4,3},{5,2},{6,1},{7,0},{8,15},{9,14},{10,... | collective-permute-start | bytes 503816 | tf_op jit(solution)/shard_map/ppermute | solution.py:376
  56.6 16.1 %collective-permute-start.13 = (bf16[640,128]{1,0:T(8,128)(2,1)S(1)}, bf16[640,128]{1,0:T(8,128)(2,1)S(1)}, u32[]{:S(2)}, u32[]{:S(2)}) collective-permute-start(bf16[640,128]{1,0:T(8,128)(2,1)S(1)} %get-tuple-element.59), channel_id=1, source_target_pairs={{0,6},{1,7},{2,4},{3,5},{4,2},{5,3},{6,0},{7,1},{8,14},{9,15},{10,... | collective-permute-start | bytes 491528 | tf_op jit(solution)/shard_map/ppermute | solution.py:376
  58.8 13.8 %collective-permute-start.14 = (bf16[640,128]{1,0:T(8,128)(2,1)S(1)}, bf16[640,128]{1,0:T(8,128)(2,1)S(1)}, u32[]{:S(2)}, u32[]{:S(2)}) collective-permute-start(bf16[640,128]{1,0:T(8,128)(2,1)S(1)} %get-tuple-element.60), channel_id=1, source_target_pairs={{0,7},{1,6},{2,5},{3,4},{4,3},{5,2},{6,1},{7,0},{8,15},{9,14},{10,... | collective-permute-start | bytes 491528 | tf_op jit(solution)/shard_map/ppermute | solution.py:376
  61.4 1.0 copy-start.1
  62.3 10.3 %collective-permute-start.8 = (bf16[640,128]{1,0:T(8,128)(2,1)S(1)}, bf16[640,128]{1,0:T(8,128)(2,1)S(1)}, u32[]{:S(2)}, u32[]{:S(2)}) collective-permute-start(bf16[640,128]{1,0:T(8,128)(2,1)S(1)} %get-tuple-element.54), channel_id=1, source_target_pairs={{0,1},{1,0},{2,3},{3,2},{4,5},{5,4},{6,7},{7,6},{8,9},{9,8},{10,11... | collective-permute-start | bytes 491528 | tf_op jit(solution)/shard_map/ppermute | solution.py:376
  62.3 10.3 %collective-permute-start.9 = (bf16[640,128]{1,0:T(8,128)(2,1)S(1)}, bf16[640,128]{1,0:T(8,128)(2,1)S(1)}, u32[]{:S(2)}, u32[]{:S(2)}) collective-permute-start(bf16[640,128]{1,0:T(8,128)(2,1)S(1)} %get-tuple-element.55), channel_id=1, source_target_pairs={{0,2},{1,3},{2,0},{3,1},{4,6},{5,7},{6,4},{7,5},{8,10},{9,11},{10,... | collective-permute-start | bytes 491528 | tf_op jit(solution)/shard_map/ppermute | solution.py:376
  70.1 28.5 %collective-permute-start.16 = (f32[4,96,128]{2,1,0:T(8,128)S(1)}, f32[4,96,128]{2,1,0:T(8,128)S(1)}, u32[]{:S(2)}, u32[]{:S(2)}) collective-permute-start(f32[4,96,128]{2,1,0:T(8,128)S(1)} %get-tuple-element.62), channel_id=1, source_target_pairs={{0,8},{1,9},{2,10},{3,11},{4,12},{5,13},{6,14},{7,15},{8,0},{9,1},... | collective-permute-start | bytes 589832 | tf_op jit(solution)/shard_map/ppermute | solution.py:394
  78.8 13.7 %collective-permute-start.17 = (f32[1,96,128]{2,1,0:T(8,128)S(1)}, f32[1,96,128]{2,1,0:T(8,128)S(1)}, u32[]{:S(2)}, u32[]{:S(2)}) collective-permute-start(f32[1,96,128]{2,1,0:T(8,128)S(1)} %get-tuple-element.63), channel_id=1, source_target_pairs={{0,1},{1,2},{2,3},{3,4},{4,5},{5,6},{6,7},{7,8},{8,9},{9,10},{10,1... | collective-permute-start | bytes 147464 | tf_op jit(solution)/shard_map/ppermute | solution.py:399
  82.5 10.0 %collective-permute-start.19 = (f32[1,96,128]{2,1,0:T(8,128)S(1)}, f32[1,96,128]{2,1,0:T(8,128)S(1)}, u32[]{:S(2)}, u32[]{:S(2)}) collective-permute-start(f32[1,96,128]{2,1,0:T(8,128)S(1)} %get-tuple-element.65), channel_id=1, source_target_pairs={{1,0},{2,1},{3,2},{4,3},{5,4},{6,5},{7,6},{8,7},{9,8},{10,9},{11,1... | collective-permute-start | bytes 147464 | tf_op jit(solution)/shard_map/ppermute | solution.py:398
  84.4 8.1 %collective-permute-start.18 = (f32[1,96,128]{2,1,0:T(8,128)S(1)}, f32[1,96,128]{2,1,0:T(8,128)S(1)}, u32[]{:S(2)}, u32[]{:S(2)}) collective-permute-start(f32[1,96,128]{2,1,0:T(8,128)S(1)} %get-tuple-element.64), channel_id=1, source_target_pairs={{0,9},{1,10},{2,11},{3,12},{4,13},{5,14},{6,15},{8,1},{9,2},{10,3}... | collective-permute-start | bytes 147464 | tf_op jit(solution)/shard_map/ppermute | solution.py:396
  90.5 8.1 %collective-permute-start.20 = (f32[1,96,128]{2,1,0:T(8,128)S(1)}, f32[1,96,128]{2,1,0:T(8,128)S(1)}, u32[]{:S(2)}, u32[]{:S(2)}) collective-permute-start(f32[1,96,128]{2,1,0:T(8,128)S(1)} %get-tuple-element.66), channel_id=1, source_target_pairs={{0,7},{1,8},{2,9},{3,10},{4,11},{5,12},{6,13},{7,14},{9,0},{10,1},... | collective-permute-start | bytes 147464 | tf_op jit(solution)/shard_map/ppermute | solution.py:395

commit v4 on v3

--- a/solution.py
+++ b/solution.py
@@ -20,10 +20,12 @@
 ANY = pl.BlockSpec(memory_space=pl.ANY)
 
 
-def pack_kernel(half, apart, route_ref, target_ref, start_ref, source_ref, *rest):
-    packed_refs = rest[:-3]
-    slot_ref, count_ref, sem = rest[-3:]
+def pack_kernel(half, apart, route_ref, target_ref, start_ref, rows_ref, *rest):
+    packed_refs = rest[:-6]
+    slot_ref, count_ref, place_ref, source_ref, load_sem, sem = rest[-6:]
     items, channels, pixels = source_ref.shape
+    load = pltpu.make_async_copy(rows_ref, source_ref, load_sem)
+    load.start()
     side = lax.div(lax.axis_index("views"), half)
     here = lax.rem(lax.axis_index("views"), half)
     lane = lax.broadcasted_iota(jnp.int32, (1, pixels), 1)
@@ -38,27 +40,36 @@
         owner = route_ref[i]
         rest = target_ref[i] * DSPAN + start_ref[i]
         home = lax.rem(owner, half)
-        for t in range(SETS):
-
-            @pl.when((lax.div(owner, half) == side) == (t == 0))
-            def _():
-                place = count_ref[t * half + home]
-                count_ref[t * half + home] = place + 1
-                first = pl.multiple_of(place * channels, channels)
-                if apart:
-                    for k in range(half):
-
-                        @pl.when(home == here ^ k)
-                        def _():
-                            target = packed_refs[(1 - t) * half + k]
-                            target = target.at[pl.ds(first, channels), :]
-                            pltpu.make_async_copy(source_ref.at[i], target, sem).start()
-                else:
-                    target = packed_refs[1 - t].at[home, pl.ds(first, channels), :]
+        t = lax.rem(lax.div(owner, half) + side, SETS)
+        place = count_ref[t * half + home]
+        count_ref[t * half + home] = place + 1
+        place_ref[i] = place
+        value = jnp.full((1, pixels), rest.astype(jnp.float32))
+        line = slot_ref[pl.ds(home, 1), :]
+        slot_ref[pl.ds(home, 1), :] = jnp.where(lane == t * CAP + place, value, line)
+
+    load.wait()
+
+    @pl.loop(0, items)
+    def _(i):
+        owner = route_ref[i]
+        home = lax.rem(owner, half)
+        t = lax.rem(lax.div(owner, half) + side, SETS)
+        first = pl.multiple_of(place_ref[i] * channels, channels)
+        if apart:
+            for n, packed_ref in enumerate(packed_refs):
+
+                @pl.when((1 - t) * half + (home ^ here) == n)
+                def _():
+                    target = packed_ref.at[pl.ds(first, channels), :]
                     pltpu.make_async_copy(source_ref.at[i], target, sem).start()
-                value = jnp.full((1, pixels), rest.astype(jnp.float32))
-                line = slot_ref[pl.ds(home, 1), :]
-                slot_ref[pl.ds(home, 1), :] = jnp.where(lane == t * CAP + place, value, line)
+        else:
+            for n, packed_ref in enumerate(packed_refs):
+
+                @pl.when(1 - t == n)
+                def _():
+                    target = packed_ref.at[home, pl.ds(first, channels), :]
+                    pltpu.make_async_copy(source_ref.at[i], target, sem).start()
 
     @pl.loop(0, items)
     def _(i):
@@ -67,7 +78,7 @@
 
 
 def pack_rows(route, target, start, source, half, apart):
-    _, channels, pixels = source.shape
+    items, channels, pixels = source.shape
     lengths = (CAP * channels + NOTE, CAP * channels)
     if apart:
         shapes = [(length, pixels) for length in lengths for _ in range(half)]
@@ -77,9 +88,15 @@
     return pl.pallas_call(
         functools.partial(pack_kernel, half, apart),
         out_shape=outs + [jax.ShapeDtypeStruct((half, pixels), jnp.float32)],
-        in_specs=[SMEM, SMEM, SMEM, VMEM],
+        in_specs=[SMEM, SMEM, SMEM, ANY],
         out_specs=[pl.BlockSpec(memory_space=pltpu.HBM)] * len(shapes) + [VMEM],
-        scratch_shapes=[pltpu.SMEM((SETS * half,), jnp.int32), pltpu.SemaphoreType.DMA],
+        scratch_shapes=[
+            pltpu.SMEM((SETS * half,), jnp.int32),
+            pltpu.SMEM((items,), jnp.int32),
+            pltpu.VMEM(source.shape, source.dtype),
+            pltpu.SemaphoreType.DMA,
+            pltpu.SemaphoreType.DMA,
+        ],
         compiler_params=pltpu.CompilerParams(vmem_limit_bytes=16 << 20),
         name="pack_rows",
     )(keep(route), keep(target), keep(start), keep(source))
@@ -182,20 +199,18 @@
     )(reference)
 
 
-def set_kernel(
-    t, code_ref, note_ref, left_ref, weight_ref, edge_ref, *rest
-):
-    arrived_refs = rest[:-11]
-    main_ref, least_ref, most_ref = rest[-11:-8]
-    stack_ref, wide_ref, total_ref, canvas_ref, *fetched, sems = rest[-8:]
+def fetch_all(sources, targets, sems):
+    copies = [
+        pltpu.make_async_copy(source, target, sems.at[n])
+        for n, (source, target) in enumerate(zip(sources, targets))
+    ]
+    for copy in copies:
+        copy.start()
+    return copies
+
+
+def fill_canvas(t, code_ref, note_ref, arrived_refs, canvas_ref):
     rows, channels, pixels = canvas_ref.shape
-    fetches = [
-        pltpu.make_async_copy(source, target, sems.at[n])
-        for n, (source, target) in enumerate(zip((left_ref, weight_ref, edge_ref), fetched))
-    ]
-    for fetch in fetches:
-        fetch.start()
-    left_ref, weight_ref, edge_ref = fetched
     half = note_ref.shape[0]
     lane = lax.broadcasted_iota(jnp.int32, (channels, pixels), 1)
     canvas_ref[...] = jnp.zeros_like(canvas_ref)
@@ -206,7 +221,6 @@
         row = lax.div(note_ref[:, first + 1, :].astype(jnp.float32).astype(jnp.int32), DSPAN)
         for r in range(rows):
             counts[r] = counts[r] + jnp.where(named & (row == r), 1.0, 0.0)
-    counts = [1.0 / jnp.full((8, pixels), jnp.maximum(jnp.sum(c), 1.0)) for c in counts]
 
     def add_slots(home, arrived):
         for place in range(CAP):
@@ -229,83 +243,220 @@
         def _(home):
             add_slots(home, arrived_refs[0].at[home])
 
-    for fetch in fetches:
-        fetch.wait()
-    for r in range(rows):
-        mean = canvas_ref[r] * jnp.concatenate([counts[r]] * (channels // 8), axis=0)
-        for e in range(3):
-            stack_ref[r, e * channels : (e + 1) * channels, :] = shift_left(mean, e - 1)
-        edge = jnp.broadcast_to(mean[:, :1], (channels, pixels)) * edge_ref[...]
-        wide = jnp.dot(
-            left_ref[r, :, 2 * channels :], both_parts(edge), preferred_element_type=jnp.float32
-        )
-        total_ref[(rows + 2) * 3 + r] = wide[:, :pixels] + wide[:, pixels:]
-
+    return [1.0 / jnp.full((8, pixels), jnp.maximum(jnp.sum(c), 1.0)) for c in counts]
+
+
+def mean_of(canvas_ref, shares, r):
+    return canvas_ref[r] * jnp.concatenate([shares[r]] * (canvas_ref.shape[1] // 8), axis=0)
+
+
+def fill_stack(mean, stack):
+    channels = mean.shape[0]
+    for e in range(3):
+        stack[e * channels : (e + 1) * channels, :] = shift_left(mean, e - 1)
+
+
+def edge_dot(mean, left, edge_ref):
+    channels, pixels = mean.shape
+    edge = jnp.broadcast_to(mean[:, :1], (channels, pixels)) * edge_ref[...]
+    last = left[:, 2 * channels :]
+    wide = jnp.dot(last, both_parts(edge), preferred_element_type=jnp.float32)
+    return wide[:, :pixels] + wide[:, pixels:]
+
+
+def tap_dots(wanted, rows, stack_of, left_ref, weight_ref, wide_ref, total_ref):
+    pixels = total_ref.shape[1]
     done = set()
     for tap in range(9):
-        wide_ref[...] = jnp.broadcast_to(weight_ref[:, tap : tap + 1], wide_ref.shape)
-        for r in range(rows):
-            right = both_parts(stack_ref[r] * wide_ref[...])
+        sources = [r for r in range(rows) if r + 2 - tap // 3 in wanted]
+        if sources:
+            wide_ref[...] = jnp.broadcast_to(weight_ref[:, tap : tap + 1], wide_ref.shape)
+        for r in sources:
+            right = both_parts(stack_of(r)[...] * wide_ref[...])
             wide = jnp.dot(left_ref[r], right, preferred_element_type=jnp.float32)
             part = wide[:, :pixels] + wide[:, pixels:]
             place = (r + 2 - tap // 3) * 3 + tap % 3
             total_ref[place] = total_ref[place] + part if place in done else part
             done.add(place)
 
+
+def finish_row(row, rows, total_ref, edge_of):
+    pixels = total_ref.shape[1]
     x = pixels - 1 - lax.broadcasted_iota(jnp.int32, (pixels, pixels), 0)
     v = lax.broadcasted_iota(jnp.int32, (pixels, pixels), 1)
     inside = (x >= v) & (x - v < DISP)
     border = (x < DISP - 1) & ((v >= pixels - 2) | (v < 1))
-    for r in range(rows + 2):
-        total = jnp.where(inside, total_ref[3 * r + 1], 0.0)
-        for b in (0, 2):
-            kept = jnp.where(inside, total_ref[3 * r + b], 0.0)
-            total = total + pltpu.roll(kept, (b - 1) % pixels, 1)
-        for a in range(3):
-            if 0 <= r + a - 2 < rows:
-                edge = total_ref[(rows + 2) * 3 + r + a - 2]
-                moved = pltpu.roll(edge, (-8 * a) % pixels, 1) if a else edge
-                total = total + jnp.where(border, moved, 0.0)
-        total = pltpu.roll(total, 0, 1, stride=1, stride_axis=0)
-        kept = total.T[pixels - DISP :]
-        if r == 0:
+    total = jnp.where(inside, total_ref[3 * row + 1], 0.0)
+    for b in (0, 2):
+        kept = jnp.where(inside, total_ref[3 * row + b], 0.0)
+        total = total + pltpu.roll(kept, (b - 1) % pixels, 1)
+    for a in range(3):
+        if 0 <= row + a - 2 < rows:
+            edge = edge_of(row + a - 2)
+            moved = pltpu.roll(edge, (-8 * a) % pixels, 1) if a else edge
+            total = total + jnp.where(border, moved, 0.0)
+    total = pltpu.roll(total, 0, 1, stride=1, stride_axis=0)
+    return total.T[pixels - DISP :]
+
+
+def set_kernel(t, code_ref, note_ref, left_ref, weight_ref, edge_ref, *rest):
+    arrived_refs = rest[:-12]
+    main_ref, least_ref, most_ref = rest[-12:-9]
+    stack_ref, wide_ref, total_ref, term_ref, canvas_ref, *fetched, sems = rest[-9:]
+    rows = canvas_ref.shape[0]
+    copies = fetch_all((left_ref, weight_ref, edge_ref), fetched, sems)
+    left_ref, weight_ref, edge_ref = fetched
+    shares = fill_canvas(t, code_ref, note_ref, arrived_refs, canvas_ref)
+    for copy in copies:
+        copy.wait()
+    for r in range(rows):
+        mean = mean_of(canvas_ref, shares, r)
+        fill_stack(mean, stack_ref.at[r])
+        term_ref[r] = edge_dot(mean, left_ref[r], edge_ref)
+    wanted = range(rows + 2)
+    tap_dots(wanted, rows, lambda r: stack_ref.at[r], left_ref, weight_ref, wide_ref, total_ref)
+    for row in wanted:
+        kept = finish_row(row, rows, total_ref, lambda r: term_ref[r])
+        if row == 0:
             least_ref[0] = kept
-        elif r == rows + 1:
+        elif row == rows + 1:
             most_ref[0] = kept
         else:
-            main_ref[r - 1] = kept
+            main_ref[row - 1] = kept
+
+
+def ends_kernel(t, code_ref, note_ref, left_ref, weight_ref, edge_ref, *rest):
+    arrived_refs = rest[:-12]
+    least_ref, most_ref, stack_ref, term_ref, inner_ref = rest[-12:-7]
+    wide_ref, total_ref, canvas_ref, *fetched, sems = rest[-7:]
+    rows = canvas_ref.shape[0]
+    copies = fetch_all((left_ref, weight_ref, edge_ref), fetched, sems)
+    left_ref, weight_ref, edge_ref = fetched
+    shares = fill_canvas(t, code_ref, note_ref, arrived_refs, canvas_ref)
+    for copy in copies:
+        copy.wait()
+    place = {0: 0, rows - 1: 1}
+    for r in range(rows):
+        mean = mean_of(canvas_ref, shares, r)
+        if r in place:
+            fill_stack(mean, stack_ref.at[place[r]])
+            term_ref[place[r]] = edge_dot(mean, left_ref[r], edge_ref)
+        else:
+            inner_ref[r - 1] = mean
+    stack_of = lambda r: stack_ref.at[place[r]]
+    tap_dots((0, rows + 1), rows, stack_of, left_ref, weight_ref, wide_ref, total_ref)
+    least_ref[0] = finish_row(0, rows, total_ref, lambda r: term_ref[place[r]])
+    most_ref[0] = finish_row(rows + 1, rows, total_ref, lambda r: term_ref[place[r]])
+
+
+def middle_kernel(
+    ends_ref, term_ref, inner_ref, left_ref, weight_ref, edge_ref, main_ref,
+    stack_ref, wide_ref, total_ref, terms_ref, *rest,
+):
+    *fetched, sems = rest
+    rows = main_ref.shape[0]
+    copies = fetch_all((left_ref, weight_ref, edge_ref), fetched, sems)
+    left_ref, weight_ref, edge_ref = fetched
+    for copy in copies:
+        copy.wait()
+    place = {0: 0, rows - 1: 1}
+    for r in range(1, rows - 1):
+        fill_stack(inner_ref[r - 1], stack_ref.at[r - 1])
+        terms_ref[r - 1] = edge_dot(inner_ref[r - 1], left_ref[r], edge_ref)
+    stack_of = lambda r: ends_ref.at[place[r]] if r in place else stack_ref.at[r - 1]
+    term_of = lambda r: term_ref[place[r]] if r in place else terms_ref[r - 1]
+    wanted = range(1, rows + 1)
+    tap_dots(wanted, rows, stack_of, left_ref, weight_ref, wide_ref, total_ref)
+    for row in wanted:
+        main_ref[row - 1] = finish_row(row, rows, total_ref, term_of)
+
+
+def cost_of(products, pixels, depth, arrived):
+    return pl.CostEstimate(
+        flops=2 * products * pixels * 2 * pixels * depth,
+        bytes_accessed=2 * sum(part.size for part in arrived),
+        transcendentals=0,
+    )
+
+
+def float_shapes(shapes):
+    return [jax.ShapeDtypeStruct(shape, jnp.float32) for shape in shapes]
+
+
+def fetch_scratch(fixed):
+    return [pltpu.VMEM(part.shape, part.dtype) for part in fixed] + [
+        pltpu.SemaphoreType.DMA((len(fixed),))
+    ]
 
 
 def add_set(t, codes, note, left, weight, edge, *arrived):
     rows, pixels, depth = left.shape
-    channels = depth // 3
-    shapes = [(n, DISP, pixels) for n in (rows, 1, 1)]
-    left, weight, edge = keep(left), keep(weight), keep(edge)
+    fixed = [keep(left), keep(weight), keep(edge)]
     return pl.pallas_call(
         functools.partial(set_kernel, t),
-        out_shape=[jax.ShapeDtypeStruct(shape, jnp.float32) for shape in shapes],
+        out_shape=float_shapes([(n, DISP, pixels) for n in (rows, 1, 1)]),
         in_specs=[SMEM, VMEM, ANY, ANY, ANY] + [VMEM] * len(arrived),
         out_specs=[VMEM] * 3,
         scratch_shapes=[
             pltpu.VMEM((rows, depth, pixels), jnp.float32),
             pltpu.VMEM((depth, pixels), jnp.float32),
-            pltpu.VMEM(((rows + 2) * 3 + rows, pixels, pixels), jnp.float32),
-            pltpu.VMEM((rows, channels, pixels), jnp.float32),
-            pltpu.VMEM(left.shape, left.dtype),
-            pltpu.VMEM(weight.shape, weight.dtype),
-            pltpu.VMEM(edge.shape, edge.dtype),
-            pltpu.SemaphoreType.DMA((3,)),
-        ],
+            pltpu.VMEM(((rows + 2) * 3, pixels, pixels), jnp.float32),
+            pltpu.VMEM((rows, pixels, pixels), jnp.float32),
+            pltpu.VMEM((rows, depth // 3, pixels), jnp.float32),
+        ]
+        + fetch_scratch(fixed),
         compiler_params=pltpu.CompilerParams(
             vmem_limit_bytes=(11 << 20) + sum(2 * part.size for part in arrived)
         ),
-        cost_estimate=pl.CostEstimate(
-            flops=2 * rows * 9 * pixels * 2 * pixels * depth,
-            bytes_accessed=2 * sum(part.size for part in arrived),
-            transcendentals=0,
+        cost_estimate=cost_of(9 * rows, pixels, depth, arrived),
+        name="add_set",
+    )(codes, note, *fixed, *arrived)
+
+
+def add_ends(t, codes, note, left, weight, edge, *arrived):
+    rows, pixels, depth = left.shape
+    channels = depth // 3
+    fixed = [keep(left), keep(weight), keep(edge)]
+    shapes = [(1, DISP, pixels)] * 2
+    shapes += [(2, depth, pixels), (2, pixels, pixels), (rows - 2, channels, pixels)]
+    return pl.pallas_call(
+        functools.partial(ends_kernel, t),
+        out_shape=float_shapes(shapes),
+        in_specs=[SMEM, VMEM, ANY, ANY, ANY] + [VMEM] * len(arrived),
+        out_specs=[VMEM] * 5,
+        scratch_shapes=[
+            pltpu.VMEM((depth, pixels), jnp.float32),
+            pltpu.VMEM(((rows + 2) * 3, pixels, pixels), jnp.float32),
+            pltpu.VMEM((rows, channels, pixels), jnp.float32),
+        ]
+        + fetch_scratch(fixed),
+        compiler_params=pltpu.CompilerParams(
+            vmem_limit_bytes=(11 << 20) + sum(2 * part.size for part in arrived)
         ),
-        name="add_set",
-    )(codes, note, left, weight, edge, *arrived)
+        cost_estimate=cost_of(6, pixels, depth, arrived),
+        name="add_ends",
+    )(codes, note, *fixed, *arrived)
+
+
+def add_middle(ends, left, weight, edge):
+    rows, pixels, depth = left.shape
+    fixed = [keep(left), keep(weight), keep(edge)]
+    return pl.pallas_call(
+        middle_kernel,
+        out_shape=float_shapes([(rows, DISP, pixels)])[0],
+        in_specs=[VMEM] * 3 + [ANY] * 3,
+        out_specs=VMEM,
+        scratch_shapes=[
+            pltpu.VMEM((rows - 2, depth, pixels), jnp.float32),
+            pltpu.VMEM((depth, pixels), jnp.float32),
+            pltpu.VMEM(((rows + 2) * 3, pixels, pixels), jnp.float32),
+            pltpu.VMEM((rows - 2, pixels, pixels), jnp.float32),
+        ]
+        + fetch_scratch(fixed),
+        compiler_params=pltpu.CompilerParams(vmem_limit_bytes=12 << 20),
+        cost_estimate=cost_of(9 * rows - 6, pixels, depth, ends),
+        name="add_middle",
+    )(*ends, *fixed)
 
 
 def depth_kernel(own_ref, far_ref, before_ref, before_far_ref, after_ref, after_far_ref, out_ref):
@@ -394,9 +545,10 @@
     other_main = send(far_main, perm=home)
     other_low = send(far_low, perm=[(i, j - 1) for i, j in home if j > 0])
     other_high = send(far_high, perm=[(i, j + 1) for i, j in home if j + 1 < views])
-    own_main, own_low, own_high = add_set(0, codes, note, near, taps, edges, *arrived_own)
+    own_low, own_high, *ends = add_ends(0, codes, note, near, taps, edges, *arrived_own)
     own_low = send(own_low, perm=[(i, i - 1) for i in range(1, views)])
     own_high = send(own_high, perm=[(i, i + 1) for i in range(views - 1)])
+    own_main = add_middle(ends, near, taps, edges)
     return depth_rows(own_main, other_main, own_high, other_high, own_low, other_low)
 
 

time: 99.8 us -> 96.6 us (0.968)
  the two profiles are of different devices: /device:TPU:7 before, /device:TPU:5 now
where the time goes in v4:
time: 96.6 us; the launch traced here: 96.1 us
  starting transfers between devices  35.3 us (37%)
  waiting for transfers between devices  32.1 us (33%)
  Pallas kernels  20.9 us (22%)
  local copies, waits for them, and re-layouts  6.03 us (6%)
  other arithmetic  1.51 us (2%)
    ppermute x14, waiting for transfers between devices, swap_all(): arrived[k] = send(parts[k], perm=[(i, i ^ k) for i in range(views)])  31.5 us
    ppermute x14, starting transfers between devices, swap_all(): arrived[k] = send(parts[k], perm=[(i, i ^ k) for i in range(views)])  16.1 us
    ppermute x1, starting transfers between devices, compute(): send(far_high, perm=[(i, j + 1) for i, j in home if j + 1 < views])  6.34 us
    pallas_call x1, Pallas kernels, add_set(): pl.pallas_call(functools.partial(set_kernel, t), out_shape=float_shapes([...  6.14 us
    pallas_call x1, Pallas kernels, add_middle(): pl.pallas_call(middle_kernel, out_shape=float_shapes([(rows, DISP, pixels...  5.3 us
    pallas_call x1, Pallas kernels, pack_rows(): pl.pallas_call(functools.partial(pack_kernel, half, apart), out_shape=out...  3.82 us
    pallas_call x1, Pallas kernels, add_ends(): pl.pallas_call(functools.partial(ends_kernel, t), out_shape=float_shapes(...  3.66 us
    ppermute x1, starting transfers between devices, compute(): own_high = send(own_high, perm=[(i, i + 1) for i in range(views - 1)])  3.64 us
  transfers between devices with their start and end apart: 21, of which 8 were waited for; matrix products, arithmetic and copies ran while one was open for 5% of the time, Pallas kernels for 21%

profile of v4, /device:TPU:5, one launch (start us, length us, event | category | flops | bytes accessed | tf_op | source)
XLA Modules:
  0.0 96.1 jit_solution(27816195602204346)
XLA Ops:
  0.7 2.4 %collective-permute-start = (bf16[2,128]{1,0:T(2,128)(2,1)S(1)}, bf16[2,128]{1,0:T(2,128)(2,1)S(1)}, u32[]{:S(2)}, u32[]{:S(2)}) collective-permute-start(bf16[2,128]{1,0:T(2,128)(2,1)S(1)} %fusion.3.near_ref), channel_id=1, source_target_pairs={{0,8},{1,9},{2,10},{3,11},{4,12},{5,13},{6,14},{7,15},{8,0},{9,1},... | collective-permute-start | bytes 1544 | tf_op jit(solution)/shard_map/ppermute | solution.py:512
  3.2 3.8 %pack_rows.1 = (bf16[656,128]{1,0:T(8,128)(2,1)S(1)}, bf16[656,128]{1,0:T(8,128)(2,1)S(1)}, bf16[656,128]{1,0:T(8,128)(2,1)S(1)}, bf16[656,128]{1,0:T(8,128)(2,1...) custom-call(s32[12]{0:T(128)} %bitcast.51, ...), custom_call_target="tpu_custom_call" | custom-call | tf_op jit(solution)/shard_map/pack_rows/pallas_call | solution.py:88
  7.0 1.6 %collective-permute-start.10 = (bf16[640,128]{1,0:T(8,128)(2,1)}, bf16[640,128]{1,0:T(8,128)(2,1)S(1)}, u32[]{:S(2)}, u32[]{:S(2)}) collective-permute-start(bf16[640,128]{1,0:T(8,128)(2,1)} %get-tuple-element.58), channel_id=1, source_target_pairs={{0,3},{1,2},{2,1},{3,0},{4,7},{5,6},{6,5},{7,4},{8,11},{9,10},{10,... | collective-permute-start | bytes 491528 | tf_op jit(solution)/shard_map/ppermute | solution.py:527
  8.6 1.7 %collective-permute-start.11 = (bf16[640,128]{1,0:T(8,128)(2,1)}, bf16[640,128]{1,0:T(8,128)(2,1)S(1)}, u32[]{:S(2)}, u32[]{:S(2)}) collective-permute-start(bf16[640,128]{1,0:T(8,128)(2,1)} %get-tuple-element.59), channel_id=1, source_target_pairs={{0,4},{1,5},{2,6},{3,7},{4,0},{5,1},{6,2},{7,3},{8,12},{9,13},{10,... | collective-permute-start | bytes 491528 | tf_op jit(solution)/shard_map/ppermute | solution.py:527
  10.3 1.0 %broadcast_in_dim.3 = f32[40,8,3,3,3]{1,0,4,3,2:T(8,128)} broadcast(f32[40,3,3,3]{0,3,2,1:T(4,128)S(1)} %broadcast_multiply_fusion), dimensions={0,2,3,4} | broadcast | bytes 38880 | tf_op jit(solution)/shard_map/broadcast_in_dim | solution.py:538
  11.3 1.3 %reshape.13 = f32[320,3,3,3]{0,3,2,1:T(4,128)S(1)} reshape(f32[40,8,3,3,3]{1,0,4,3,2:T(8,128)} %broadcast_in_dim.3) | data formatting | bytes 69120 | tf_op jit(solution)/shard_map/reshape | solution.py:538
  12.9 0.8 pad_maximum_fusion.edge_ref
  14.4 1.0 %copy-done = bf16[4,128,960]{2,1,0:T(8,128)(2,1)} copy-done((bf16[4,128,960]{2,1,0:T(8,128)(2,1)}, bf16[4,128,960]{2,1,0:T(8,128)(2,1)S(1)}, u32[]{:S(2)}) %copy-start) | copy-done | bytes 983064
  15.8 0.8 pad.17.weight_ref
  17.2 1.0 %collective-permute-done.1.rest_1_ = bf16[656,128]{1,0:T(8,128)(2,1)S(1)} collective-permute-done((bf16[656,128]{1,0:T(8,128)(2,1)S(1)}, bf16[656,128]{1,0:T(8,128)(2,1)S(1)}, u32[]{:S(2)}, u32[]{:S(2)}) %collective-permute-start.1) | collective-permute-done | bytes 167968 | tf_op jit(solution)/shard_map/ppermute | solution.py:527
  18.2 1.2 %collective-permute-start.2 = (bf16[656,128]{1,0:T(8,128)(2,1)S(1)}, bf16[656,128]{1,0:T(8,128)(2,1)S(1)}, u32[]{:S(2)}, u32[]{:S(2)}) collective-permute-start(bf16[656,128]{1,0:T(8,128)(2,1)S(1)} %get-tuple-element.49), channel_id=1, source_target_pairs={{0,2},{1,3},{2,0},{3,1},{4,6},{5,7},{6,4},{7,5},{8,10},{9,11},{10,... | collective-permute-start | bytes 503816 | tf_op jit(solution)/shard_map/ppermute | solution.py:527
  19.4 4.3 %collective-permute-done.2.rest_2_ = bf16[656,128]{1,0:T(8,128)(2,1)S(1)} collective-permute-done((bf16[656,128]{1,0:T(8,128)(2,1)S(1)}, bf16[656,128]{1,0:T(8,128)(2,1)S(1)}, u32[]{:S(2)}, u32[]{:S(2)}) %collective-permute-start.2) | collective-permute-done | bytes 167968 | tf_op jit(solution)/shard_map/ppermute | solution.py:527
  23.7 2.3 %collective-permute-start.3 = (bf16[656,128]{1,0:T(8,128)(2,1)S(1)}, bf16[656,128]{1,0:T(8,128)(2,1)S(1)}, u32[]{:S(2)}, u32[]{:S(2)}) collective-permute-start(bf16[656,128]{1,0:T(8,128)(2,1)S(1)} %get-tuple-element.50), channel_id=1, source_target_pairs={{0,3},{1,2},{2,1},{3,0},{4,7},{5,6},{6,5},{7,4},{8,11},{9,10},{10,... | collective-permute-start | bytes 503816 | tf_op jit(solution)/shard_map/ppermute | solution.py:527
  26.0 5.1 %collective-permute-done.3.rest_3_ = bf16[656,128]{1,0:T(8,128)(2,1)S(1)} collective-permute-done((bf16[656,128]{1,0:T(8,128)(2,1)S(1)}, bf16[656,128]{1,0:T(8,128)(2,1)S(1)}, u32[]{:S(2)}, u32[]{:S(2)}) %collective-permute-start.3) | collective-permute-done | bytes 167968 | tf_op jit(solution)/shard_map/ppermute | solution.py:527
  31.1 1.4 %collective-permute-start.4 = (bf16[656,128]{1,0:T(8,128)(2,1)S(1)}, bf16[656,128]{1,0:T(8,128)(2,1)S(1)}, u32[]{:S(2)}, u32[]{:S(2)}) collective-permute-start(bf16[656,128]{1,0:T(8,128)(2,1)S(1)} %get-tuple-element.51), channel_id=1, source_target_pairs={{0,4},{1,5},{2,6},{3,7},{4,0},{5,1},{6,2},{7,3},{8,12},{9,13},{10,... | collective-permute-start | bytes 503816 | tf_op jit(solution)/shard_map/ppermute | solution.py:527
  32.6 4.0 %collective-permute-done.4.rest_4_ = bf16[656,128]{1,0:T(8,128)(2,1)S(1)} collective-permute-done((bf16[656,128]{1,0:T(8,128)(2,1)S(1)}, bf16[656,128]{1,0:T(8,128)(2,1)S(1)}, u32[]{:S(2)}, u32[]{:S(2)}) %collective-permute-start.4) | collective-permute-done | bytes 167968 | tf_op jit(solution)/shard_map/ppermute | solution.py:527
  36.5 2.6 %collective-permute-start.5 = (bf16[656,128]{1,0:T(8,128)(2,1)S(1)}, bf16[656,128]{1,0:T(8,128)(2,1)S(1)}, u32[]{:S(2)}, u32[]{:S(2)}) collective-permute-start(bf16[656,128]{1,0:T(8,128)(2,1)S(1)} %get-tuple-element.52), channel_id=1, source_target_pairs={{0,5},{1,4},{2,7},{3,6},{4,1},{5,0},{6,3},{7,2},{8,13},{9,12},{10,... | collective-permute-start | bytes 503816 | tf_op jit(solution)/shard_map/ppermute | solution.py:527
  39.1 4.6 %collective-permute-done.5.rest_5_ = bf16[656,128]{1,0:T(8,128)(2,1)S(1)} collective-permute-done((bf16[656,128]{1,0:T(8,128)(2,1)S(1)}, bf16[656,128]{1,0:T(8,128)(2,1)S(1)}, u32[]{:S(2)}, u32[]{:S(2)}) %collective-permute-start.5) | collective-permute-done | bytes 167968 | tf_op jit(solution)/shard_map/ppermute | solution.py:527
  43.8 6.3 %collective-permute-done.6.rest_6_ = bf16[656,128]{1,0:T(8,128)(2,1)S(1)} collective-permute-done((bf16[656,128]{1,0:T(8,128)(2,1)S(1)}, bf16[656,128]{1,0:T(8,128)(2,1)S(1)}, u32[]{:S(2)}, u32[]{:S(2)}) %collective-permute-start.6) | collective-permute-done | bytes 167968 | tf_op jit(solution)/shard_map/ppermute | solution.py:527
  50.1 1.1 %collective-permute-start.7 = (bf16[656,128]{1,0:T(8,128)(2,1)S(1)}, bf16[656,128]{1,0:T(8,128)(2,1)S(1)}, u32[]{:S(2)}, u32[]{:S(2)}) collective-permute-start(bf16[656,128]{1,0:T(8,128)(2,1)S(1)} %get-tuple-element.54), channel_id=1, source_target_pairs={{0,7},{1,6},{2,5},{3,4},{4,3},{5,2},{6,1},{7,0},{8,15},{9,14},{10,... | collective-permute-start | bytes 503816 | tf_op jit(solution)/shard_map/ppermute | solution.py:527
  51.2 6.1 %collective-permute-done.7.rest_7_ = bf16[656,128]{1,0:T(8,128)(2,1)S(1)} collective-permute-done((bf16[656,128]{1,0:T(8,128)(2,1)S(1)}, bf16[656,128]{1,0:T(8,128)(2,1)S(1)}, u32[]{:S(2)}, u32[]{:S(2)}) %collective-permute-start.7) | collective-permute-done | bytes 167968 | tf_op jit(solution)/shard_map/ppermute | solution.py:527
  57.3 0.8 collective-permute-start.13
  58.3 2.7 %collective-permute-start.14 = (bf16[640,128]{1,0:T(8,128)(2,1)S(1)}, bf16[640,128]{1,0:T(8,128)(2,1)S(1)}, u32[]{:S(2)}, u32[]{:S(2)}) collective-permute-start(bf16[640,128]{1,0:T(8,128)(2,1)S(1)} %get-tuple-element.62), channel_id=1, source_target_pairs={{0,7},{1,6},{2,5},{3,4},{4,3},{5,2},{6,1},{7,0},{8,15},{9,14},{10,... | collective-permute-start | bytes 491528 | tf_op jit(solution)/shard_map/ppermute | solution.py:527
  61.5 1.0 copy-done.1
  62.7 6.1 %add_set.1 = (f32[4,96,128]{2,1,0:T(8,128)S(1)}, f32[1,96,128]{2,1,0:T(8,128)S(1)}, f32[1,96,128]{2,1,0:T(8,128)S(1)}) custom-call(s32[32]{0:T(128)S(1)} %reshape.16.code_ref, bf16[8,16,128]{2,1,0:T(8,128)(2,1)S(1)} %constant_dynamic-update-slice_fusion.note_ref, bf16[4,128,960]{2,1,0:T(8,128)(2,1)} %copy-done.1, f32[960,128]{1,0:T(8,128)} %pad.17.weight_ref, ...), custom_call_target="tpu_custom_call" | custom-call | flops 2264924160 | bytes 1343488 | tf_op jit(solution)/shard_map/add_set/pallas_call | solution.py:395
  68.9 2.7 %collective-permute-start.16 = (f32[4,96,128]{2,1,0:T(8,128)S(1)}, f32[4,96,128]{2,1,0:T(8,128)S(1)}, u32[]{:S(2)}, u32[]{:S(2)}) collective-permute-start(f32[4,96,128]{2,1,0:T(8,128)S(1)} %get-tuple-element.66), channel_id=1, source_target_pairs={{0,8},{1,9},{2,10},{3,11},{4,12},{5,13},{6,14},{7,15},{8,0},{9,1},... | collective-permute-start | bytes 589832 | tf_op jit(solution)/shard_map/ppermute | solution.py:545
  71.6 3.7 %add_ends.1 = (f32[1,96,128]{2,1,0:T(8,128)S(1)}, f32[1,96,128]{2,1,0:T(8,128)S(1)}, f32[2,960,128]{2,1,0:T(8,128)S(1)}, f32[2,128,128]{2,1,0:T(8,128)S(1)}, f32[2,320,128]{2,1,0:T(8,128)S(1)}) custom-call(s32[32]{0:T(128)S(1)} %reshape.16.code_ref, bf16[8,16,128]{2,1,0:T(8,128)(2,1)S(1)} %constant_dynamic-update-slice_fusion.note_ref, ...), custom_call_target="tpu_custom_call" | custom-call | flops 377487360 | bytes 1310720 | tf_op jit(solution)/shard_map/add_ends/pallas_call | solution.py:422
  75.3 3.6 %collective-permute-start.17 = (f32[1,96,128]{2,1,0:T(8,128)S(1)}, f32[1,96,128]{2,1,0:T(8,128)S(1)}, u32[]{:S(2)}, u32[]{:S(2)}) collective-permute-start(f32[1,96,128]{2,1,0:T(8,128)S(1)} %get-tuple-element.67), channel_id=1, source_target_pairs={{0,1},{1,2},{2,3},{3,4},{4,5},{5,6},{6,7},{7,8},{8,9},{9,10},{10,1... | collective-permute-start | bytes 147464 | tf_op jit(solution)/shard_map/ppermute | solution.py:550
  79.0 1.9 %collective-permute-start.19 = (f32[1,96,128]{2,1,0:T(8,128)S(1)}, f32[1,96,128]{2,1,0:T(8,128)S(1)}, u32[]{:S(2)}, u32[]{:S(2)}) collective-permute-start(f32[1,96,128]{2,1,0:T(8,128)S(1)} %get-tuple-element.69), channel_id=1, source_target_pairs={{1,0},{2,1},{3,2},{4,3},{5,4},{6,5},{7,6},{8,7},{9,8},{10,9},{11,1... | collective-permute-start | bytes 147464 | tf_op jit(solution)/shard_map/ppermute | solution.py:549
  80.9 6.3 %collective-permute-start.18 = (f32[1,96,128]{2,1,0:T(8,128)S(1)}, f32[1,96,128]{2,1,0:T(8,128)S(1)}, u32[]{:S(2)}, u32[]{:S(2)}) collective-permute-start(f32[1,96,128]{2,1,0:T(8,128)S(1)} %get-tuple-element.68), channel_id=1, source_target_pairs={{0,9},{1,10},{2,11},{3,12},{4,13},{5,14},{6,15},{8,1},{9,2},{10,3}... | collective-permute-start | bytes 147464 | tf_op jit(solution)/shard_map/ppermute | solution.py:547
  87.2 2.1 %collective-permute-start.20 = (f32[1,96,128]{2,1,0:T(8,128)S(1)}, f32[1,96,128]{2,1,0:T(8,128)S(1)}, u32[]{:S(2)}, u32[]{:S(2)}) collective-permute-start(f32[1,96,128]{2,1,0:T(8,128)S(1)} %get-tuple-element.70), channel_id=1, source_target_pairs={{0,7},{1,8},{2,9},{3,10},{4,11},{5,12},{6,13},{7,14},{9,0},{10,1},... | collective-permute-start | bytes 147464 | tf_op jit(solution)/shard_map/ppermute | solution.py:546
  89.3 5.3 %add_middle.1.own_ref = f32[4,96,128]{2,1,0:T(8,128)S(1)} custom-call(f32[2,960,128]{2,1,0:T(8,128)S(1)} %get-tuple-element.63.ends_ref, f32[2,128,128]{2,1,0:T(8,128)S(1)} %get-tuple-element.64.term_ref, f32[2,320,128]{2,1,0:T(8,128)S(1)} %get-tuple-element.65.inner_ref, bf16[4,128,960]{2,1,0:T(8,128)(2,1)} %copy-done, f32[960,128]{1,0:T(8,128)} %pad.17.weight_ref, ...), custom_call_target="tpu_custom_call" | custom-call | flops 1887436800 | bytes 720896 | tf_op jit(solution)/shard_map/add_middle/pallas_call | solution.py:444
  (55 shorter events, 5.0 us)
Async XLA Ops:
  0.0 0.7 copy-start.4
  0.0 0.7 copy-start.5
  0.7 15.9 %collective-permute-start = (bf16[2,128]{1,0:T(2,128)(2,1)S(1)}, bf16[2,128]{1,0:T(2,128)(2,1)S(1)}, u32[]{:S(2)}, u32[]{:S(2)}) collective-permute-start(bf16[2,128]{1,0:T(2,128)(2,1)S(1)} %fusion.3.near_ref), channel_id=1, source_target_pairs={{0,8},{1,9},{2,10},{3,11},{4,12},{5,13},{6,14},{7,15},{8,0},{9,1},... | collective-permute-start | bytes 1544 | tf_op jit(solution)/shard_map/ppermute | solution.py:512
  3.1 55.2 %collective-permute-start.15 = (bf16[4,320,128]{2,1,0:T(8,128)(2,1)}, bf16[4,320,128]{2,1,0:T(8,128)(2,1)S(1)}, u32[]{:S(2)}, u32[]{:S(2)}) collective-permute-start(bf16[4,320,128]{2,1,0:T(8,128)(2,1)} %reference_ref.1), channel_id=1, source_target_pairs={{0,8},{1,9},{2,10},{3,11},{4,12},{5,13},{6,14},{7,15},{8,0},{9,1},... | collective-permute-start | bytes 983048 | tf_op jit(solution)/shard_map/ppermute | solution.py:513
  3.2 7.1 %copy-start.3 = (f32[40,3,3,3]{0,3,2,1:T(4,128)S(1)}, f32[40,3,3,3]{0,3,2,1:T(4,128)}, u32[]{:S(2)}) copy-start(f32[40,3,3,3]{0,3,2,1:T(4,128)} %param.11) | copy-start | bytes 12964
  7.0 55.5 %collective-permute-start.10 = (bf16[640,128]{1,0:T(8,128)(2,1)}, bf16[640,128]{1,0:T(8,128)(2,1)S(1)}, u32[]{:S(2)}, u32[]{:S(2)}) collective-permute-start(bf16[640,128]{1,0:T(8,128)(2,1)} %get-tuple-element.58), channel_id=1, source_target_pairs={{0,3},{1,2},{2,1},{3,0},{4,7},{5,6},{6,5},{7,4},{8,11},{9,10},{10,... | collective-permute-start | bytes 491528 | tf_op jit(solution)/shard_map/ppermute | solution.py:527
  8.6 53.9 %collective-permute-start.11 = (bf16[640,128]{1,0:T(8,128)(2,1)}, bf16[640,128]{1,0:T(8,128)(2,1)S(1)}, u32[]{:S(2)}, u32[]{:S(2)}) collective-permute-start(bf16[640,128]{1,0:T(8,128)(2,1)} %get-tuple-element.59), channel_id=1, source_target_pairs={{0,4},{1,5},{2,6},{3,7},{4,0},{5,1},{6,2},{7,3},{8,12},{9,13},{10,... | collective-permute-start | bytes 491528 | tf_op jit(solution)/shard_map/ppermute | solution.py:527
  10.3 58.6 %collective-permute-start.12 = (bf16[640,128]{1,0:T(8,128)(2,1)}, bf16[640,128]{1,0:T(8,128)(2,1)S(1)}, u32[]{:S(2)}, u32[]{:S(2)}) collective-permute-start(bf16[640,128]{1,0:T(8,128)(2,1)} %get-tuple-element.60), channel_id=1, source_target_pairs={{0,5},{1,4},{2,7},{3,6},{4,1},{5,0},{6,3},{7,2},{8,13},{9,12},{10,... | collective-permute-start | bytes 491528 | tf_op jit(solution)/shard_map/ppermute | solution.py:527
  12.9 1.0 %copy-start.2 = (bf16[4,320,128]{2,1,0:T(8,128)(2,1)S(1)}, bf16[4,320,128]{2,1,0:T(8,128)(2,1)}, u32[]{:S(2)}) copy-start(bf16[4,320,128]{2,1,0:T(8,128)(2,1)} %reference_ref.1) | copy-start | bytes 983044
  14.4 1.0 %copy-start = (bf16[4,128,960]{2,1,0:T(8,128)(2,1)}, bf16[4,128,960]{2,1,0:T(8,128)(2,1)S(1)}, u32[]{:S(2)}) copy-start(bf16[4,128,960]{2,1,0:T(8,128)(2,1)S(1)} %stack_left.2.left_ref) | copy-start | bytes 2949124
  16.7 1.5 %collective-permute-start.1 = (bf16[656,128]{1,0:T(8,128)(2,1)S(1)}, bf16[656,128]{1,0:T(8,128)(2,1)S(1)}, u32[]{:S(2)}, u32[]{:S(2)}) collective-permute-start(bf16[656,128]{1,0:T(8,128)(2,1)S(1)} %get-tuple-element.48), channel_id=1, source_target_pairs={{0,1},{1,0},{2,3},{3,2},{4,5},{5,4},{6,7},{7,6},{8,9},{9,8},{10,11... | collective-permute-start | bytes 503816 | tf_op jit(solution)/shard_map/ppermute | solution.py:527
  18.2 5.5 %collective-permute-start.2 = (bf16[656,128]{1,0:T(8,128)(2,1)S(1)}, bf16[656,128]{1,0:T(8,128)(2,1)S(1)}, u32[]{:S(2)}, u32[]{:S(2)}) collective-permute-start(bf16[656,128]{1,0:T(8,128)(2,1)S(1)} %get-tuple-element.49), channel_id=1, source_target_pairs={{0,2},{1,3},{2,0},{3,1},{4,6},{5,7},{6,4},{7,5},{8,10},{9,11},{10,... | collective-permute-start | bytes 503816 | tf_op jit(solution)/shard_map/ppermute | solution.py:527
  23.7 7.4 %collective-permute-start.3 = (bf16[656,128]{1,0:T(8,128)(2,1)S(1)}, bf16[656,128]{1,0:T(8,128)(2,1)S(1)}, u32[]{:S(2)}, u32[]{:S(2)}) collective-permute-start(bf16[656,128]{1,0:T(8,128)(2,1)S(1)} %get-tuple-element.50), channel_id=1, source_target_pairs={{0,3},{1,2},{2,1},{3,0},{4,7},{5,6},{6,5},{7,4},{8,11},{9,10},{10,... | collective-permute-start | bytes 503816 | tf_op jit(solution)/shard_map/ppermute | solution.py:527
  31.1 5.4 %collective-permute-start.4 = (bf16[656,128]{1,0:T(8,128)(2,1)S(1)}, bf16[656,128]{1,0:T(8,128)(2,1)S(1)}, u32[]{:S(2)}, u32[]{:S(2)}) collective-permute-start(bf16[656,128]{1,0:T(8,128)(2,1)S(1)} %get-tuple-element.51), channel_id=1, source_target_pairs={{0,4},{1,5},{2,6},{3,7},{4,0},{5,1},{6,2},{7,3},{8,12},{9,13},{10,... | collective-permute-start | bytes 503816 | tf_op jit(solution)/shard_map/ppermute | solution.py:527
  36.5 7.2 %collective-permute-start.5 = (bf16[656,128]{1,0:T(8,128)(2,1)S(1)}, bf16[656,128]{1,0:T(8,128)(2,1)S(1)}, u32[]{:S(2)}, u32[]{:S(2)}) collective-permute-start(bf16[656,128]{1,0:T(8,128)(2,1)S(1)} %get-tuple-element.52), channel_id=1, source_target_pairs={{0,5},{1,4},{2,7},{3,6},{4,1},{5,0},{6,3},{7,2},{8,13},{9,12},{10,... | collective-permute-start | bytes 503816 | tf_op jit(solution)/shard_map/ppermute | solution.py:527
  43.7 6.4 %collective-permute-start.6 = (bf16[656,128]{1,0:T(8,128)(2,1)S(1)}, bf16[656,128]{1,0:T(8,128)(2,1)S(1)}, u32[]{:S(2)}, u32[]{:S(2)}) collective-permute-start(bf16[656,128]{1,0:T(8,128)(2,1)S(1)} %get-tuple-element.53), channel_id=1, source_target_pairs={{0,6},{1,7},{2,4},{3,5},{4,2},{5,3},{6,0},{7,1},{8,14},{9,15},{10,... | collective-permute-start | bytes 503816 | tf_op jit(solution)/shard_map/ppermute | solution.py:527
  50.1 7.2 %collective-permute-start.7 = (bf16[656,128]{1,0:T(8,128)(2,1)S(1)}, bf16[656,128]{1,0:T(8,128)(2,1)S(1)}, u32[]{:S(2)}, u32[]{:S(2)}) collective-permute-start(bf16[656,128]{1,0:T(8,128)(2,1)S(1)} %get-tuple-element.54), channel_id=1, source_target_pairs={{0,7},{1,6},{2,5},{3,4},{4,3},{5,2},{6,1},{7,0},{8,15},{9,14},{10,... | collective-permute-start | bytes 503816 | tf_op jit(solution)/shard_map/ppermute | solution.py:527
  57.3 14.3 %collective-permute-start.13 = (bf16[640,128]{1,0:T(8,128)(2,1)}, bf16[640,128]{1,0:T(8,128)(2,1)S(1)}, u32[]{:S(2)}, u32[]{:S(2)}) collective-permute-start(bf16[640,128]{1,0:T(8,128)(2,1)} %get-tuple-element.61), channel_id=1, source_target_pairs={{0,6},{1,7},{2,4},{3,5},{4,2},{5,3},{6,0},{7,1},{8,14},{9,15},{10,... | collective-permute-start | bytes 491528 | tf_op jit(solution)/shard_map/ppermute | solution.py:527
  58.3 13.4 %collective-permute-start.14 = (bf16[640,128]{1,0:T(8,128)(2,1)S(1)}, bf16[640,128]{1,0:T(8,128)(2,1)S(1)}, u32[]{:S(2)}, u32[]{:S(2)}) collective-permute-start(bf16[640,128]{1,0:T(8,128)(2,1)S(1)} %get-tuple-element.62), channel_id=1, source_target_pairs={{0,7},{1,6},{2,5},{3,4},{4,3},{5,2},{6,1},{7,0},{8,15},{9,14},{10,... | collective-permute-start | bytes 491528 | tf_op jit(solution)/shard_map/ppermute | solution.py:527
  61.5 1.0 copy-start.1
  62.5 9.1 %collective-permute-start.8 = (bf16[640,128]{1,0:T(8,128)(2,1)S(1)}, bf16[640,128]{1,0:T(8,128)(2,1)S(1)}, u32[]{:S(2)}, u32[]{:S(2)}) collective-permute-start(bf16[640,128]{1,0:T(8,128)(2,1)S(1)} %get-tuple-element.56), channel_id=1, source_target_pairs={{0,1},{1,0},{2,3},{3,2},{4,5},{5,4},{6,7},{7,6},{8,9},{9,8},{10,11... | collective-permute-start | bytes 491528 | tf_op jit(solution)/shard_map/ppermute | solution.py:527
  62.5 9.1 %collective-permute-start.9 = (bf16[640,128]{1,0:T(8,128)(2,1)S(1)}, bf16[640,128]{1,0:T(8,128)(2,1)S(1)}, u32[]{:S(2)}, u32[]{:S(2)}) collective-permute-start(bf16[640,128]{1,0:T(8,128)(2,1)S(1)} %get-tuple-element.57), channel_id=1, source_target_pairs={{0,2},{1,3},{2,0},{3,1},{4,6},{5,7},{6,4},{7,5},{8,10},{9,11},{10,... | collective-permute-start | bytes 491528 | tf_op jit(solution)/shard_map/ppermute | solution.py:527
  68.9 26.5 %collective-permute-start.16 = (f32[4,96,128]{2,1,0:T(8,128)S(1)}, f32[4,96,128]{2,1,0:T(8,128)S(1)}, u32[]{:S(2)}, u32[]{:S(2)}) collective-permute-start(f32[4,96,128]{2,1,0:T(8,128)S(1)} %get-tuple-element.66), channel_id=1, source_target_pairs={{0,8},{1,9},{2,10},{3,11},{4,12},{5,13},{6,14},{7,15},{8,0},{9,1},... | collective-permute-start | bytes 589832 | tf_op jit(solution)/shard_map/ppermute | solution.py:545
  75.3 19.4 %collective-permute-start.17 = (f32[1,96,128]{2,1,0:T(8,128)S(1)}, f32[1,96,128]{2,1,0:T(8,128)S(1)}, u32[]{:S(2)}, u32[]{:S(2)}) collective-permute-start(f32[1,96,128]{2,1,0:T(8,128)S(1)} %get-tuple-element.67), channel_id=1, source_target_pairs={{0,1},{1,2},{2,3},{3,4},{4,5},{5,6},{6,7},{7,8},{8,9},{9,10},{10,1... | collective-permute-start | bytes 147464 | tf_op jit(solution)/shard_map/ppermute | solution.py:550
  79.0 15.7 %collective-permute-start.19 = (f32[1,96,128]{2,1,0:T(8,128)S(1)}, f32[1,96,128]{2,1,0:T(8,128)S(1)}, u32[]{:S(2)}, u32[]{:S(2)}) collective-permute-start(f32[1,96,128]{2,1,0:T(8,128)S(1)} %get-tuple-element.69), channel_id=1, source_target_pairs={{1,0},{2,1},{3,2},{4,3},{5,4},{6,5},{7,6},{8,7},{9,8},{10,9},{11,1... | collective-permute-start | bytes 147464 | tf_op jit(solution)/shard_map/ppermute | solution.py:549
  80.9 13.8 %collective-permute-start.18 = (f32[1,96,128]{2,1,0:T(8,128)S(1)}, f32[1,96,128]{2,1,0:T(8,128)S(1)}, u32[]{:S(2)}, u32[]{:S(2)}) collective-permute-start(f32[1,96,128]{2,1,0:T(8,128)S(1)} %get-tuple-element.68), channel_id=1, source_target_pairs={{0,9},{1,10},{2,11},{3,12},{4,13},{5,14},{6,15},{8,1},{9,2},{10,3}... | collective-permute-start | bytes 147464 | tf_op jit(solution)/shard_map/ppermute | solution.py:547
  87.2 8.1 %collective-permute-start.20 = (f32[1,96,128]{2,1,0:T(8,128)S(1)}, f32[1,96,128]{2,1,0:T(8,128)S(1)}, u32[]{:S(2)}, u32[]{:S(2)}) collective-permute-start(f32[1,96,128]{2,1,0:T(8,128)S(1)} %get-tuple-element.70), channel_id=1, source_target_pairs={{0,7},{1,8},{2,9},{3,10},{4,11},{5,12},{6,13},{7,14},{9,0},{10,1},... | collective-permute-start | bytes 147464 | tf_op jit(solution)/shard_map/ppermute | solution.py:546

commit v5 on v4

--- a/solution.py
+++ b/solution.py
@@ -34,6 +34,8 @@
     @pl.loop(0, SETS * half)
     def _(j):
         count_ref[j] = 0
+        for place in range(CAP):
+            place_ref[j * CAP + place] = -1
 
     @pl.loop(0, items)
     def _(i):
@@ -43,33 +45,29 @@
         t = lax.rem(lax.div(owner, half) + side, SETS)
         place = count_ref[t * half + home]
         count_ref[t * half + home] = place + 1
-        place_ref[i] = place
+        output = (1 - t) * half + (home ^ here if apart else home)
+        place_ref[output * CAP + place] = i
         value = jnp.full((1, pixels), rest.astype(jnp.float32))
         line = slot_ref[pl.ds(home, 1), :]
         slot_ref[pl.ds(home, 1), :] = jnp.where(lane == t * CAP + place, value, line)
 
     load.wait()
 
-    @pl.loop(0, items)
-    def _(i):
-        owner = route_ref[i]
-        home = lax.rem(owner, half)
-        t = lax.rem(lax.div(owner, half) + side, SETS)
-        first = pl.multiple_of(place_ref[i] * channels, channels)
+    def copy_slots(n, home):
+        packed_ref = packed_refs[n] if apart else packed_refs[n].at[home]
+        for place in range(CAP):
+            i = place_ref[((n if apart else n * half + home) * CAP) + place]
+
+            @pl.when(i >= 0)
+            def _():
+                target = packed_ref.at[place * channels : (place + 1) * channels, :]
+                pltpu.make_async_copy(source_ref.at[i], target, sem).start()
+
+    for n in range(len(packed_refs)):
         if apart:
-            for n, packed_ref in enumerate(packed_refs):
-
-                @pl.when((1 - t) * half + (home ^ here) == n)
-                def _():
-                    target = packed_ref.at[pl.ds(first, channels), :]
-                    pltpu.make_async_copy(source_ref.at[i], target, sem).start()
+            copy_slots(n, 0)
         else:
-            for n, packed_ref in enumerate(packed_refs):
-
-                @pl.when(1 - t == n)
-                def _():
-                    target = packed_ref.at[home, pl.ds(first, channels), :]
-                    pltpu.make_async_copy(source_ref.at[i], target, sem).start()
+            pl.loop(0, half)(functools.partial(copy_slots, n))
 
     @pl.loop(0, items)
     def _(i):
@@ -78,7 +76,7 @@
 
 
 def pack_rows(route, target, start, source, half, apart):
-    items, channels, pixels = source.shape
+    _, channels, pixels = source.shape
     lengths = (CAP * channels + NOTE, CAP * channels)
     if apart:
         shapes = [(length, pixels) for length in lengths for _ in range(half)]
@@ -92,7 +90,7 @@
         out_specs=[pl.BlockSpec(memory_space=pltpu.HBM)] * len(shapes) + [VMEM],
         scratch_shapes=[
             pltpu.SMEM((SETS * half,), jnp.int32),
-            pltpu.SMEM((items,), jnp.int32),
+            pltpu.SMEM((SETS * half * CAP,), jnp.int32),
             pltpu.VMEM(source.shape, source.dtype),
             pltpu.SemaphoreType.DMA,
             pltpu.SemaphoreType.DMA,
@@ -540,7 +538,7 @@
     taps = jnp.pad(taps, ((0, 0), (0, pixels - 9)))
     edges = jnp.pad(scaled[..., 2], ((0, 0), (0, 0), (0, 5))).reshape(-1, 24)
     edges = jnp.roll(jnp.pad(edges, ((0, 0), (0, pixels - 24))), -2, 1)
-    near, far = stack_left(reference_rows), stack_left(far_rows)
+    near, far = stack_left(keep(reference_rows)), stack_left(far_rows)
     far_main, far_low, far_high = add_set(1, codes, note, far, taps, edges, *arrived_far)
     other_main = send(far_main, perm=home)
     other_low = send(far_low, perm=[(i, j - 1) for i, j in home if j > 0])

time: 96.6 us -> 98.2 us (1.017)
  the two profiles are of different devices: /device:TPU:5 before, /device:TPU:7 now
where the time goes in v5:
time: 98.2 us; the launch traced here: 97.7 us
  starting transfers between devices  33.6 us (34%)
  waiting for transfers between devices  32.9 us (34%)
  Pallas kernels  21.8 us (22%)
  local copies, waits for them, and re-layouts  7.63 us (8%)
  other arithmetic  1.52 us (2%)
    ppermute x14, waiting for transfers between devices, swap_all(): arrived[k] = send(parts[k], perm=[(i, i ^ k) for i in range(views)])  32.2 us
    ppermute x14, starting transfers between devices, swap_all(): arrived[k] = send(parts[k], perm=[(i, i ^ k) for i in range(views)])  15.4 us
    ppermute x1, starting transfers between devices, compute(): send(far_high, perm=[(i, j + 1) for i, j in home if j + 1 < views])  6.17 us
    pallas_call x1, Pallas kernels, add_set(): pl.pallas_call(functools.partial(set_kernel, t), out_shape=float_shapes([...  6.14 us
    pallas_call x1, Pallas kernels, add_middle(): pl.pallas_call(middle_kernel, out_shape=float_shapes([(rows, DISP, pixels...  5.31 us
    pallas_call x1, Pallas kernels, pack_rows(): pl.pallas_call(functools.partial(pack_kernel, half, apart), out_shape=out...  3.84 us
    pallas_call x1, Pallas kernels, add_ends(): pl.pallas_call(functools.partial(ends_kernel, t), out_shape=float_shapes(...  3.65 us
    ppermute x1, starting transfers between devices, compute(): own_high = send(own_high, perm=[(i, i + 1) for i in range(views - 1)])  3.39 us
  transfers between devices with their start and end apart: 21, of which 9 were waited for; matrix products, arithmetic and copies ran while one was open for 7% of the time, Pallas kernels for 22%

profile of v5, /device:TPU:7, one launch (start us, length us, event | category | flops | bytes accessed | tf_op | source)
XLA Modules:
  0.0 97.7 jit_solution(231790381736068509)
XLA Ops:
  0.7 2.4 %collective-permute-start = (bf16[2,128]{1,0:T(2,128)(2,1)S(1)}, bf16[2,128]{1,0:T(2,128)(2,1)S(1)}, u32[]{:S(2)}, u32[]{:S(2)}) collective-permute-start(bf16[2,128]{1,0:T(2,128)(2,1)S(1)} %fusion.3.near_ref), channel_id=1, source_target_pairs={{0,8},{1,9},{2,10},{3,11},{4,12},{5,13},{6,14},{7,15},{8,0},{9,1},... | collective-permute-start | bytes 1544 | tf_op jit(solution)/shard_map/ppermute | solution.py:510
  3.2 3.8 %pack_rows.1 = (bf16[656,128]{1,0:T(8,128)(2,1)S(1)}, bf16[656,128]{1,0:T(8,128)(2,1)S(1)}, bf16[656,128]{1,0:T(8,128)(2,1)S(1)}, bf16[656,128]{1,0:T(8,128)(2,1...) custom-call(s32[12]{0:T(128)} %bitcast.51, ...), custom_call_target="tpu_custom_call" | custom-call | tf_op jit(solution)/shard_map/pack_rows/pallas_call | solution.py:86
  7.0 1.2 %collective-permute-start.10 = (bf16[640,128]{1,0:T(8,128)(2,1)}, bf16[640,128]{1,0:T(8,128)(2,1)S(1)}, u32[]{:S(2)}, u32[]{:S(2)}) collective-permute-start(bf16[640,128]{1,0:T(8,128)(2,1)} %get-tuple-element.58), channel_id=1, source_target_pairs={{0,3},{1,2},{2,1},{3,0},{4,7},{5,6},{6,5},{7,4},{8,11},{9,10},{10,... | collective-permute-start | bytes 491528 | tf_op jit(solution)/shard_map/ppermute | solution.py:525
  8.3 1.6 %collective-permute-start.11 = (bf16[640,128]{1,0:T(8,128)(2,1)}, bf16[640,128]{1,0:T(8,128)(2,1)S(1)}, u32[]{:S(2)}, u32[]{:S(2)}) collective-permute-start(bf16[640,128]{1,0:T(8,128)(2,1)} %get-tuple-element.59), channel_id=1, source_target_pairs={{0,4},{1,5},{2,6},{3,7},{4,0},{5,1},{6,2},{7,3},{8,12},{9,13},{10,... | collective-permute-start | bytes 491528 | tf_op jit(solution)/shard_map/ppermute | solution.py:525
  10.0 1.0 %broadcast_in_dim.3 = f32[40,8,3,3,3]{1,0,4,3,2:T(8,128)} broadcast(f32[40,3,3,3]{0,3,2,1:T(4,128)S(1)} %broadcast_multiply_fusion), dimensions={0,2,3,4} | broadcast | bytes 38880 | tf_op jit(solution)/shard_map/broadcast_in_dim | solution.py:536
  11.1 1.3 %reshape.13 = f32[320,3,3,3]{0,3,2,1:T(4,128)S(1)} reshape(f32[40,8,3,3,3]{1,0,4,3,2:T(8,128)} %broadcast_in_dim.3) | data formatting | bytes 69120 | tf_op jit(solution)/shard_map/reshape | solution.py:536
  13.5 1.5 %stack_left.2.left_ref = bf16[4,128,960]{2,1,0:T(8,128)(2,1)S(1)} custom-call(bf16[4,320,128]{2,1,0:T(8,128)(2,1)} %reference_ref.1), custom_call_target="tpu_custom_call" | custom-call | tf_op jit(solution)/shard_map/stack_left/pallas_call | solution.py:190
  15.0 1.0 %copy-done = bf16[4,128,960]{2,1,0:T(8,128)(2,1)} copy-done((bf16[4,128,960]{2,1,0:T(8,128)(2,1)}, bf16[4,128,960]{2,1,0:T(8,128)(2,1)S(1)}, u32[]{:S(2)}) %copy-start) | copy-done | bytes 983064
  16.1 1.0 %copy.21 = f32[960,9]{1,0:T(8,128)} copy(f32[960,9]{0,1:T(8,128)S(1)} %reshape.14) | data formatting | bytes 69120 | tf_op jit(solution)/shard_map/reshape | solution.py:537
  17.1 1.8 %pad.17.weight_ref = f32[960,128]{1,0:T(8,128)} pad(f32[960,9]{1,0:T(8,128)} %copy.21, f32[]{:T(128)} %constant.10.clone.1), padding=0_0x0_119 | pad | bytes 526084 | tf_op jit(solution)/shard_map/jit(_pad)/pad | solution.py:538
  19.3 1.2 %collective-permute-done.1.rest_1_ = bf16[656,128]{1,0:T(8,128)(2,1)S(1)} collective-permute-done((bf16[656,128]{1,0:T(8,128)(2,1)S(1)}, bf16[656,128]{1,0:T(8,128)(2,1)S(1)}, u32[]{:S(2)}, u32[]{:S(2)}) %collective-permute-start.1) | collective-permute-done | bytes 167968 | tf_op jit(solution)/shard_map/ppermute | solution.py:525
  20.5 1.1 %collective-permute-start.2 = (bf16[656,128]{1,0:T(8,128)(2,1)S(1)}, bf16[656,128]{1,0:T(8,128)(2,1)S(1)}, u32[]{:S(2)}, u32[]{:S(2)}) collective-permute-start(bf16[656,128]{1,0:T(8,128)(2,1)S(1)} %get-tuple-element.49), channel_id=1, source_target_pairs={{0,2},{1,3},{2,0},{3,1},{4,6},{5,7},{6,4},{7,5},{8,10},{9,11},{10,... | collective-permute-start | bytes 503816 | tf_op jit(solution)/shard_map/ppermute | solution.py:525
  21.7 4.5 %collective-permute-done.2.rest_2_ = bf16[656,128]{1,0:T(8,128)(2,1)S(1)} collective-permute-done((bf16[656,128]{1,0:T(8,128)(2,1)S(1)}, bf16[656,128]{1,0:T(8,128)(2,1)S(1)}, u32[]{:S(2)}, u32[]{:S(2)}) %collective-permute-start.2) | collective-permute-done | bytes 167968 | tf_op jit(solution)/shard_map/ppermute | solution.py:525
  26.2 2.1 %collective-permute-start.3 = (bf16[656,128]{1,0:T(8,128)(2,1)S(1)}, bf16[656,128]{1,0:T(8,128)(2,1)S(1)}, u32[]{:S(2)}, u32[]{:S(2)}) collective-permute-start(bf16[656,128]{1,0:T(8,128)(2,1)S(1)} %get-tuple-element.50), channel_id=1, source_target_pairs={{0,3},{1,2},{2,1},{3,0},{4,7},{5,6},{6,5},{7,4},{8,11},{9,10},{10,... | collective-permute-start | bytes 503816 | tf_op jit(solution)/shard_map/ppermute | solution.py:525
  28.3 5.1 %collective-permute-done.3.rest_3_ = bf16[656,128]{1,0:T(8,128)(2,1)S(1)} collective-permute-done((bf16[656,128]{1,0:T(8,128)(2,1)S(1)}, bf16[656,128]{1,0:T(8,128)(2,1)S(1)}, u32[]{:S(2)}, u32[]{:S(2)}) %collective-permute-start.3) | collective-permute-done | bytes 167968 | tf_op jit(solution)/shard_map/ppermute | solution.py:525
  33.4 1.4 %collective-permute-start.4 = (bf16[656,128]{1,0:T(8,128)(2,1)S(1)}, bf16[656,128]{1,0:T(8,128)(2,1)S(1)}, u32[]{:S(2)}, u32[]{:S(2)}) collective-permute-start(bf16[656,128]{1,0:T(8,128)(2,1)S(1)} %get-tuple-element.51), channel_id=1, source_target_pairs={{0,4},{1,5},{2,6},{3,7},{4,0},{5,1},{6,2},{7,3},{8,12},{9,13},{10,... | collective-permute-start | bytes 503816 | tf_op jit(solution)/shard_map/ppermute | solution.py:525
  34.8 4.0 %collective-permute-done.4.rest_4_ = bf16[656,128]{1,0:T(8,128)(2,1)S(1)} collective-permute-done((bf16[656,128]{1,0:T(8,128)(2,1)S(1)}, bf16[656,128]{1,0:T(8,128)(2,1)S(1)}, u32[]{:S(2)}, u32[]{:S(2)}) %collective-permute-start.4) | collective-permute-done | bytes 167968 | tf_op jit(solution)/shard_map/ppermute | solution.py:525
  38.8 2.6 %collective-permute-start.5 = (bf16[656,128]{1,0:T(8,128)(2,1)S(1)}, bf16[656,128]{1,0:T(8,128)(2,1)S(1)}, u32[]{:S(2)}, u32[]{:S(2)}) collective-permute-start(bf16[656,128]{1,0:T(8,128)(2,1)S(1)} %get-tuple-element.52), channel_id=1, source_target_pairs={{0,5},{1,4},{2,7},{3,6},{4,1},{5,0},{6,3},{7,2},{8,13},{9,12},{10,... | collective-permute-start | bytes 503816 | tf_op jit(solution)/shard_map/ppermute | solution.py:525
  41.4 4.7 %collective-permute-done.5.rest_5_ = bf16[656,128]{1,0:T(8,128)(2,1)S(1)} collective-permute-done((bf16[656,128]{1,0:T(8,128)(2,1)S(1)}, bf16[656,128]{1,0:T(8,128)(2,1)S(1)}, u32[]{:S(2)}, u32[]{:S(2)}) %collective-permute-start.5) | collective-permute-done | bytes 167968 | tf_op jit(solution)/shard_map/ppermute | solution.py:525
  46.1 6.3 %collective-permute-done.6.rest_6_ = bf16[656,128]{1,0:T(8,128)(2,1)S(1)} collective-permute-done((bf16[656,128]{1,0:T(8,128)(2,1)S(1)}, bf16[656,128]{1,0:T(8,128)(2,1)S(1)}, u32[]{:S(2)}, u32[]{:S(2)}) %collective-permute-start.6) | collective-permute-done | bytes 167968 | tf_op jit(solution)/shard_map/ppermute | solution.py:525
  52.4 1.1 %collective-permute-start.7 = (bf16[656,128]{1,0:T(8,128)(2,1)S(1)}, bf16[656,128]{1,0:T(8,128)(2,1)S(1)}, u32[]{:S(2)}, u32[]{:S(2)}) collective-permute-start(bf16[656,128]{1,0:T(8,128)(2,1)S(1)} %get-tuple-element.54), channel_id=1, source_target_pairs={{0,7},{1,6},{2,5},{3,4},{4,3},{5,2},{6,1},{7,0},{8,15},{9,14},{10,... | collective-permute-start | bytes 503816 | tf_op jit(solution)/shard_map/ppermute | solution.py:525
  53.5 6.1 %collective-permute-done.7.rest_7_ = bf16[656,128]{1,0:T(8,128)(2,1)S(1)} collective-permute-done((bf16[656,128]{1,0:T(8,128)(2,1)S(1)}, bf16[656,128]{1,0:T(8,128)(2,1)S(1)}, u32[]{:S(2)}, u32[]{:S(2)}) %collective-permute-start.7) | collective-permute-done | bytes 167968 | tf_op jit(solution)/shard_map/ppermute | solution.py:525
  60.6 2.7 %collective-permute-start.14 = (bf16[640,128]{1,0:T(8,128)(2,1)S(1)}, bf16[640,128]{1,0:T(8,128)(2,1)S(1)}, u32[]{:S(2)}, u32[]{:S(2)}) collective-permute-start(bf16[640,128]{1,0:T(8,128)(2,1)S(1)} %get-tuple-element.62), channel_id=1, source_target_pairs={{0,7},{1,6},{2,5},{3,4},{4,3},{5,2},{6,1},{7,0},{8,15},{9,14},{10,... | collective-permute-start | bytes 491528 | tf_op jit(solution)/shard_map/ppermute | solution.py:525
  63.8 0.9 copy-done.1
  65.0 6.1 %add_set.1 = (f32[4,96,128]{2,1,0:T(8,128)S(1)}, f32[1,96,128]{2,1,0:T(8,128)S(1)}, f32[1,96,128]{2,1,0:T(8,128)S(1)}) custom-call(s32[32]{0:T(128)S(1)} %reshape.16.code_ref, bf16[8,16,128]{2,1,0:T(8,128)(2,1)S(1)} %constant_dynamic-update-slice_fusion.note_ref, bf16[4,128,960]{2,1,0:T(8,128)(2,1)} %copy-done.1, f32[960,128]{1,0:T(8,128)} %pad.17.weight_ref, ...), custom_call_target="tpu_custom_call" | custom-call | flops 2264924160 | bytes 1343488 | tf_op jit(solution)/shard_map/add_set/pallas_call | solution.py:393
  71.1 2.2 %collective-permute-start.16 = (f32[4,96,128]{2,1,0:T(8,128)S(1)}, f32[4,96,128]{2,1,0:T(8,128)S(1)}, u32[]{:S(2)}, u32[]{:S(2)}) collective-permute-start(f32[4,96,128]{2,1,0:T(8,128)S(1)} %get-tuple-element.66), channel_id=1, source_target_pairs={{0,8},{1,9},{2,10},{3,11},{4,12},{5,13},{6,14},{7,15},{8,0},{9,1},... | collective-permute-start | bytes 589832 | tf_op jit(solution)/shard_map/ppermute | solution.py:543
  73.7 3.7 %add_ends.1 = (f32[1,96,128]{2,1,0:T(8,128)S(1)}, f32[1,96,128]{2,1,0:T(8,128)S(1)}, f32[2,960,128]{2,1,0:T(8,128)S(1)}, f32[2,128,128]{2,1,0:T(8,128)S(1)}, f32[2,320,128]{2,1,0:T(8,128)S(1)}) custom-call(s32[32]{0:T(128)S(1)} %reshape.16.code_ref, bf16[8,16,128]{2,1,0:T(8,128)(2,1)S(1)} %constant_dynamic-update-slice_fusion.note_ref, ...), custom_call_target="tpu_custom_call" | custom-call | flops 377487360 | bytes 1310720 | tf_op jit(solution)/shard_map/add_ends/pallas_call | solution.py:420
  77.3 3.4 %collective-permute-start.17 = (f32[1,96,128]{2,1,0:T(8,128)S(1)}, f32[1,96,128]{2,1,0:T(8,128)S(1)}, u32[]{:S(2)}, u32[]{:S(2)}) collective-permute-start(f32[1,96,128]{2,1,0:T(8,128)S(1)} %get-tuple-element.67), channel_id=1, source_target_pairs={{0,1},{1,2},{2,3},{3,4},{4,5},{5,6},{6,7},{7,8},{8,9},{9,10},{10,1... | collective-permute-start | bytes 147464 | tf_op jit(solution)/shard_map/ppermute | solution.py:548
  80.7 1.9 %collective-permute-start.19 = (f32[1,96,128]{2,1,0:T(8,128)S(1)}, f32[1,96,128]{2,1,0:T(8,128)S(1)}, u32[]{:S(2)}, u32[]{:S(2)}) collective-permute-start(f32[1,96,128]{2,1,0:T(8,128)S(1)} %get-tuple-element.69), channel_id=1, source_target_pairs={{1,0},{2,1},{3,2},{4,3},{5,4},{6,5},{7,6},{8,7},{9,8},{10,9},{11,1... | collective-permute-start | bytes 147464 | tf_op jit(solution)/shard_map/ppermute | solution.py:547
  82.7 6.2 %collective-permute-start.18 = (f32[1,96,128]{2,1,0:T(8,128)S(1)}, f32[1,96,128]{2,1,0:T(8,128)S(1)}, u32[]{:S(2)}, u32[]{:S(2)}) collective-permute-start(f32[1,96,128]{2,1,0:T(8,128)S(1)} %get-tuple-element.68), channel_id=1, source_target_pairs={{0,9},{1,10},{2,11},{3,12},{4,13},{5,14},{6,15},{8,1},{9,2},{10,3}... | collective-permute-start | bytes 147464 | tf_op jit(solution)/shard_map/ppermute | solution.py:545
  88.8 2.1 %collective-permute-start.20 = (f32[1,96,128]{2,1,0:T(8,128)S(1)}, f32[1,96,128]{2,1,0:T(8,128)S(1)}, u32[]{:S(2)}, u32[]{:S(2)}) collective-permute-start(f32[1,96,128]{2,1,0:T(8,128)S(1)} %get-tuple-element.70), channel_id=1, source_target_pairs={{0,7},{1,8},{2,9},{3,10},{4,11},{5,12},{6,13},{7,14},{9,0},{10,1},... | collective-permute-start | bytes 147464 | tf_op jit(solution)/shard_map/ppermute | solution.py:544
  90.9 5.3 %add_middle.1.own_ref = f32[4,96,128]{2,1,0:T(8,128)S(1)} custom-call(f32[2,960,128]{2,1,0:T(8,128)S(1)} %get-tuple-element.63.ends_ref, f32[2,128,128]{2,1,0:T(8,128)S(1)} %get-tuple-element.64.term_ref, f32[2,320,128]{2,1,0:T(8,128)S(1)} %get-tuple-element.65.inner_ref, bf16[4,128,960]{2,1,0:T(8,128)(2,1)} %copy-done, f32[960,128]{1,0:T(8,128)} %pad.17.weight_ref, ...), custom_call_target="tpu_custom_call" | custom-call | flops 1887436800 | bytes 720896 | tf_op jit(solution)/shard_map/add_middle/pallas_call | solution.py:442
  (53 shorter events, 6.0 us)
Async XLA Ops:
  0.0 0.7 copy-start.3
  0.0 0.7 copy-start.4
  0.7 18.2 %collective-permute-start = (bf16[2,128]{1,0:T(2,128)(2,1)S(1)}, bf16[2,128]{1,0:T(2,128)(2,1)S(1)}, u32[]{:S(2)}, u32[]{:S(2)}) collective-permute-start(bf16[2,128]{1,0:T(2,128)(2,1)S(1)} %fusion.3.near_ref), channel_id=1, source_target_pairs={{0,8},{1,9},{2,10},{3,11},{4,12},{5,13},{6,14},{7,15},{8,0},{9,1},... | collective-permute-start | bytes 1544 | tf_op jit(solution)/shard_map/ppermute | solution.py:510
  3.1 57.5 %collective-permute-start.15 = (bf16[4,320,128]{2,1,0:T(8,128)(2,1)}, bf16[4,320,128]{2,1,0:T(8,128)(2,1)S(1)}, u32[]{:S(2)}, u32[]{:S(2)}) collective-permute-start(bf16[4,320,128]{2,1,0:T(8,128)(2,1)} %reference_ref.1), channel_id=1, source_target_pairs={{0,8},{1,9},{2,10},{3,11},{4,12},{5,13},{6,14},{7,15},{8,0},{9,1},... | collective-permute-start | bytes 983048 | tf_op jit(solution)/shard_map/ppermute | solution.py:511
  3.2 6.9 %copy-start.2 = (f32[40,3,3,3]{0,3,2,1:T(4,128)S(1)}, f32[40,3,3,3]{0,3,2,1:T(4,128)}, u32[]{:S(2)}) copy-start(f32[40,3,3,3]{0,3,2,1:T(4,128)} %param.11) | copy-start | bytes 12964
  7.0 57.7 %collective-permute-start.10 = (bf16[640,128]{1,0:T(8,128)(2,1)}, bf16[640,128]{1,0:T(8,128)(2,1)S(1)}, u32[]{:S(2)}, u32[]{:S(2)}) collective-permute-start(bf16[640,128]{1,0:T(8,128)(2,1)} %get-tuple-element.58), channel_id=1, source_target_pairs={{0,3},{1,2},{2,1},{3,0},{4,7},{5,6},{6,5},{7,4},{8,11},{9,10},{10,... | collective-permute-start | bytes 491528 | tf_op jit(solution)/shard_map/ppermute | solution.py:525
  8.3 56.5 %collective-permute-start.11 = (bf16[640,128]{1,0:T(8,128)(2,1)}, bf16[640,128]{1,0:T(8,128)(2,1)S(1)}, u32[]{:S(2)}, u32[]{:S(2)}) collective-permute-start(bf16[640,128]{1,0:T(8,128)(2,1)} %get-tuple-element.59), channel_id=1, source_target_pairs={{0,4},{1,5},{2,6},{3,7},{4,0},{5,1},{6,2},{7,3},{8,12},{9,13},{10,... | collective-permute-start | bytes 491528 | tf_op jit(solution)/shard_map/ppermute | solution.py:525
  9.8 61.3 %collective-permute-start.12 = (bf16[640,128]{1,0:T(8,128)(2,1)S(1)}, bf16[640,128]{1,0:T(8,128)(2,1)S(1)}, u32[]{:S(2)}, u32[]{:S(2)}) collective-permute-start(bf16[640,128]{1,0:T(8,128)(2,1)S(1)} %get-tuple-element.60), channel_id=1, source_target_pairs={{0,5},{1,4},{2,7},{3,6},{4,1},{5,0},{6,3},{7,2},{8,13},{9,12},{10,... | collective-permute-start | bytes 491528 | tf_op jit(solution)/shard_map/ppermute | solution.py:525
  15.0 1.0 %copy-start = (bf16[4,128,960]{2,1,0:T(8,128)(2,1)}, bf16[4,128,960]{2,1,0:T(8,128)(2,1)S(1)}, u32[]{:S(2)}) copy-start(bf16[4,128,960]{2,1,0:T(8,128)(2,1)S(1)} %stack_left.2.left_ref) | copy-start | bytes 2949124
  19.1 1.5 %collective-permute-start.1 = (bf16[656,128]{1,0:T(8,128)(2,1)S(1)}, bf16[656,128]{1,0:T(8,128)(2,1)S(1)}, u32[]{:S(2)}, u32[]{:S(2)}) collective-permute-start(bf16[656,128]{1,0:T(8,128)(2,1)S(1)} %get-tuple-element.48), channel_id=1, source_target_pairs={{0,1},{1,0},{2,3},{3,2},{4,5},{5,4},{6,7},{7,6},{8,9},{9,8},{10,11... | collective-permute-start | bytes 503816 | tf_op jit(solution)/shard_map/ppermute | solution.py:525
  20.5 5.6 %collective-permute-start.2 = (bf16[656,128]{1,0:T(8,128)(2,1)S(1)}, bf16[656,128]{1,0:T(8,128)(2,1)S(1)}, u32[]{:S(2)}, u32[]{:S(2)}) collective-permute-start(bf16[656,128]{1,0:T(8,128)(2,1)S(1)} %get-tuple-element.49), channel_id=1, source_target_pairs={{0,2},{1,3},{2,0},{3,1},{4,6},{5,7},{6,4},{7,5},{8,10},{9,11},{10,... | collective-permute-start | bytes 503816 | tf_op jit(solution)/shard_map/ppermute | solution.py:525
  26.2 7.2 %collective-permute-start.3 = (bf16[656,128]{1,0:T(8,128)(2,1)S(1)}, bf16[656,128]{1,0:T(8,128)(2,1)S(1)}, u32[]{:S(2)}, u32[]{:S(2)}) collective-permute-start(bf16[656,128]{1,0:T(8,128)(2,1)S(1)} %get-tuple-element.50), channel_id=1, source_target_pairs={{0,3},{1,2},{2,1},{3,0},{4,7},{5,6},{6,5},{7,4},{8,11},{9,10},{10,... | collective-permute-start | bytes 503816 | tf_op jit(solution)/shard_map/ppermute | solution.py:525
  33.4 5.4 %collective-permute-start.4 = (bf16[656,128]{1,0:T(8,128)(2,1)S(1)}, bf16[656,128]{1,0:T(8,128)(2,1)S(1)}, u32[]{:S(2)}, u32[]{:S(2)}) collective-permute-start(bf16[656,128]{1,0:T(8,128)(2,1)S(1)} %get-tuple-element.51), channel_id=1, source_target_pairs={{0,4},{1,5},{2,6},{3,7},{4,0},{5,1},{6,2},{7,3},{8,12},{9,13},{10,... | collective-permute-start | bytes 503816 | tf_op jit(solution)/shard_map/ppermute | solution.py:525
  38.8 7.2 %collective-permute-start.5 = (bf16[656,128]{1,0:T(8,128)(2,1)S(1)}, bf16[656,128]{1,0:T(8,128)(2,1)S(1)}, u32[]{:S(2)}, u32[]{:S(2)}) collective-permute-start(bf16[656,128]{1,0:T(8,128)(2,1)S(1)} %get-tuple-element.52), channel_id=1, source_target_pairs={{0,5},{1,4},{2,7},{3,6},{4,1},{5,0},{6,3},{7,2},{8,13},{9,12},{10,... | collective-permute-start | bytes 503816 | tf_op jit(solution)/shard_map/ppermute | solution.py:525
  46.0 6.4 %collective-permute-start.6 = (bf16[656,128]{1,0:T(8,128)(2,1)S(1)}, bf16[656,128]{1,0:T(8,128)(2,1)S(1)}, u32[]{:S(2)}, u32[]{:S(2)}) collective-permute-start(bf16[656,128]{1,0:T(8,128)(2,1)S(1)} %get-tuple-element.53), channel_id=1, source_target_pairs={{0,6},{1,7},{2,4},{3,5},{4,2},{5,3},{6,0},{7,1},{8,14},{9,15},{10,... | collective-permute-start | bytes 503816 | tf_op jit(solution)/shard_map/ppermute | solution.py:525
  52.4 7.2 %collective-permute-start.7 = (bf16[656,128]{1,0:T(8,128)(2,1)S(1)}, bf16[656,128]{1,0:T(8,128)(2,1)S(1)}, u32[]{:S(2)}, u32[]{:S(2)}) collective-permute-start(bf16[656,128]{1,0:T(8,128)(2,1)S(1)} %get-tuple-element.54), channel_id=1, source_target_pairs={{0,7},{1,6},{2,5},{3,4},{4,3},{5,2},{6,1},{7,0},{8,15},{9,14},{10,... | collective-permute-start | bytes 503816 | tf_op jit(solution)/shard_map/ppermute | solution.py:525
  59.6 13.8 %collective-permute-start.13 = (bf16[640,128]{1,0:T(8,128)(2,1)S(1)}, bf16[640,128]{1,0:T(8,128)(2,1)S(1)}, u32[]{:S(2)}, u32[]{:S(2)}) collective-permute-start(bf16[640,128]{1,0:T(8,128)(2,1)S(1)} %get-tuple-element.61), channel_id=1, source_target_pairs={{0,6},{1,7},{2,4},{3,5},{4,2},{5,3},{6,0},{7,1},{8,14},{9,15},{10,... | collective-permute-start | bytes 491528 | tf_op jit(solution)/shard_map/ppermute | solution.py:525
  60.6 12.8 %collective-permute-start.14 = (bf16[640,128]{1,0:T(8,128)(2,1)S(1)}, bf16[640,128]{1,0:T(8,128)(2,1)S(1)}, u32[]{:S(2)}, u32[]{:S(2)}) collective-permute-start(bf16[640,128]{1,0:T(8,128)(2,1)S(1)} %get-tuple-element.62), channel_id=1, source_target_pairs={{0,7},{1,6},{2,5},{3,4},{4,3},{5,2},{6,1},{7,0},{8,15},{9,14},{10,... | collective-permute-start | bytes 491528 | tf_op jit(solution)/shard_map/ppermute | solution.py:525
  63.8 0.9 copy-start.1
  64.8 8.6 %collective-permute-start.8 = (bf16[640,128]{1,0:T(8,128)(2,1)S(1)}, bf16[640,128]{1,0:T(8,128)(2,1)S(1)}, u32[]{:S(2)}, u32[]{:S(2)}) collective-permute-start(bf16[640,128]{1,0:T(8,128)(2,1)S(1)} %get-tuple-element.56), channel_id=1, source_target_pairs={{0,1},{1,0},{2,3},{3,2},{4,5},{5,4},{6,7},{7,6},{8,9},{9,8},{10,11... | collective-permute-start | bytes 491528 | tf_op jit(solution)/shard_map/ppermute | solution.py:525
  64.8 8.9 %collective-permute-start.9 = (bf16[640,128]{1,0:T(8,128)(2,1)S(1)}, bf16[640,128]{1,0:T(8,128)(2,1)S(1)}, u32[]{:S(2)}, u32[]{:S(2)}) collective-permute-start(bf16[640,128]{1,0:T(8,128)(2,1)S(1)} %get-tuple-element.57), channel_id=1, source_target_pairs={{0,2},{1,3},{2,0},{3,1},{4,6},{5,7},{6,4},{7,5},{8,10},{9,11},{10,... | collective-permute-start | bytes 491528 | tf_op jit(solution)/shard_map/ppermute | solution.py:525
  71.1 25.8 %collective-permute-start.16 = (f32[4,96,128]{2,1,0:T(8,128)S(1)}, f32[4,96,128]{2,1,0:T(8,128)S(1)}, u32[]{:S(2)}, u32[]{:S(2)}) collective-permute-start(f32[4,96,128]{2,1,0:T(8,128)S(1)} %get-tuple-element.66), channel_id=1, source_target_pairs={{0,8},{1,9},{2,10},{3,11},{4,12},{5,13},{6,14},{7,15},{8,0},{9,1},... | collective-permute-start | bytes 589832 | tf_op jit(solution)/shard_map/ppermute | solution.py:543
  77.3 18.9 %collective-permute-start.17 = (f32[1,96,128]{2,1,0:T(8,128)S(1)}, f32[1,96,128]{2,1,0:T(8,128)S(1)}, u32[]{:S(2)}, u32[]{:S(2)}) collective-permute-start(f32[1,96,128]{2,1,0:T(8,128)S(1)} %get-tuple-element.67), channel_id=1, source_target_pairs={{0,1},{1,2},{2,3},{3,4},{4,5},{5,6},{6,7},{7,8},{8,9},{9,10},{10,1... | collective-permute-start | bytes 147464 | tf_op jit(solution)/shard_map/ppermute | solution.py:548
  80.7 15.5 %collective-permute-start.19 = (f32[1,96,128]{2,1,0:T(8,128)S(1)}, f32[1,96,128]{2,1,0:T(8,128)S(1)}, u32[]{:S(2)}, u32[]{:S(2)}) collective-permute-start(f32[1,96,128]{2,1,0:T(8,128)S(1)} %get-tuple-element.69), channel_id=1, source_target_pairs={{1,0},{2,1},{3,2},{4,3},{5,4},{6,5},{7,6},{8,7},{9,8},{10,9},{11,1... | collective-permute-start | bytes 147464 | tf_op jit(solution)/shard_map/ppermute | solution.py:547
  82.7 13.6 %collective-permute-start.18 = (f32[1,96,128]{2,1,0:T(8,128)S(1)}, f32[1,96,128]{2,1,0:T(8,128)S(1)}, u32[]{:S(2)}, u32[]{:S(2)}) collective-permute-start(f32[1,96,128]{2,1,0:T(8,128)S(1)} %get-tuple-element.68), channel_id=1, source_target_pairs={{0,9},{1,10},{2,11},{3,12},{4,13},{5,14},{6,15},{8,1},{9,2},{10,3}... | collective-permute-start | bytes 147464 | tf_op jit(solution)/shard_map/ppermute | solution.py:545
  88.8 8.1 %collective-permute-start.20 = (f32[1,96,128]{2,1,0:T(8,128)S(1)}, f32[1,96,128]{2,1,0:T(8,128)S(1)}, u32[]{:S(2)}, u32[]{:S(2)}) collective-permute-start(f32[1,96,128]{2,1,0:T(8,128)S(1)} %get-tuple-element.70), channel_id=1, source_target_pairs={{0,7},{1,8},{2,9},{3,10},{4,11},{5,12},{6,13},{7,14},{9,0},{10,1},... | collective-permute-start | bytes 147464 | tf_op jit(solution)/shard_map/ppermute | solution.py:544

commit v6 on v5

--- a/solution.py
+++ b/solution.py
@@ -14,6 +14,7 @@
 CAP = 2
 SETS = 2
 NOTE = 16
+GRANT = 11 << 20
 
 VMEM = pl.BlockSpec(memory_space=pltpu.VMEM)
 SMEM = pl.BlockSpec(memory_space=pltpu.SMEM)
@@ -95,7 +96,7 @@
             pltpu.SemaphoreType.DMA,
             pltpu.SemaphoreType.DMA,
         ],
-        compiler_params=pltpu.CompilerParams(vmem_limit_bytes=16 << 20),
+        compiler_params=pltpu.CompilerParams(vmem_limit_bytes=58 << 20),
         name="pack_rows",
     )(keep(route), keep(target), keep(start), keep(source))
 
@@ -144,7 +145,7 @@
             pltpu.SemaphoreType.DMA((count,)),
         ],
         input_output_aliases={3 + k: k for k in range(count)},
-        compiler_params=pltpu.CompilerParams(vmem_limit_bytes=4 << 20),
+        compiler_params=pltpu.CompilerParams(vmem_limit_bytes=58 << 20),
         name="add_note",
     )(slots, near, far, *packed)
 
@@ -349,14 +350,9 @@
 
 def middle_kernel(
     ends_ref, term_ref, inner_ref, left_ref, weight_ref, edge_ref, main_ref,
-    stack_ref, wide_ref, total_ref, terms_ref, *rest,
+    stack_ref, wide_ref, total_ref, terms_ref,
 ):
-    *fetched, sems = rest
     rows = main_ref.shape[0]
-    copies = fetch_all((left_ref, weight_ref, edge_ref), fetched, sems)
-    left_ref, weight_ref, edge_ref = fetched
-    for copy in copies:
-        copy.wait()
     place = {0: 0, rows - 1: 1}
     for r in range(1, rows - 1):
         fill_stack(inner_ref[r - 1], stack_ref.at[r - 1])
@@ -404,7 +400,7 @@
         ]
         + fetch_scratch(fixed),
         compiler_params=pltpu.CompilerParams(
-            vmem_limit_bytes=(11 << 20) + sum(2 * part.size for part in arrived)
+            vmem_limit_bytes=GRANT + sum(2 * part.size for part in arrived)
         ),
         cost_estimate=cost_of(9 * rows, pixels, depth, arrived),
         name="add_set",
@@ -429,7 +425,7 @@
         ]
         + fetch_scratch(fixed),
         compiler_params=pltpu.CompilerParams(
-            vmem_limit_bytes=(11 << 20) + sum(2 * part.size for part in arrived)
+            vmem_limit_bytes=GRANT + sum(2 * part.size for part in arrived)
         ),
         cost_estimate=cost_of(6, pixels, depth, arrived),
         name="add_ends",
@@ -438,23 +434,21 @@
 
 def add_middle(ends, left, weight, edge):
     rows, pixels, depth = left.shape
-    fixed = [keep(left), keep(weight), keep(edge)]
     return pl.pallas_call(
         middle_kernel,
         out_shape=float_shapes([(rows, DISP, pixels)])[0],
-        in_specs=[VMEM] * 3 + [ANY] * 3,
+        in_specs=[VMEM] * 6,
         out_specs=VMEM,
         scratch_shapes=[
             pltpu.VMEM((rows - 2, depth, pixels), jnp.float32),
             pltpu.VMEM((depth, pixels), jnp.float32),
             pltpu.VMEM(((rows + 2) * 3, pixels, pixels), jnp.float32),
             pltpu.VMEM((rows - 2, pixels, pixels), jnp.float32),
-        ]
-        + fetch_scratch(fixed),
-        compiler_params=pltpu.CompilerParams(vmem_limit_bytes=12 << 20),
+        ],
+        compiler_params=pltpu.CompilerParams(vmem_limit_bytes=14 << 20),
         cost_estimate=cost_of(9 * rows - 6, pixels, depth, ends),
         name="add_middle",
-    )(*ends, *fixed)
+    )(*ends, left, weight, edge)
 
 
 def depth_kernel(own_ref, far_ref, before_ref, before_far_ref, after_ref, after_far_ref, out_ref):

time: 98.2 us -> 97.7 us (level)
  local copies, waits for them, and re-layouts: 7.63 us -> 5.19 us
  waiting for transfers between devices: 32.9 us -> 35 us
    pallas_call x1, Pallas kernels: 5.31 us -> 3.79 us  [add_middle(): pl.pallas_call(middle_kernel, out_shape=float_shapes([(rows, DISP, pixels...]
    ppermute x1, waiting for transfers between devices: 0.65 us -> 2.13 us  [compute(): other_low = send(far_low, perm=[(i, j - 1) for i, j in home if j > 0])]
    pallas_call x1, Pallas kernels: 0.14 us -> 1.46 us  [add_note(): pl.pallas_call(functools.partial(note_kernel, count), out_shape=[jax.Shap...]
    unnamed x18 -> x40, local copies, waits for them, and re-layouts: 2.01 us -> 3.28 us
    reshape x1, local copies, waits for them, and re-layouts: 1.31 us -> 0.25 us  [compute(): scaled = jnp.repeat(conv_weight / CG, CG, axis=0)]
    pad x1, local copies, waits for them, and re-layouts: 1.85 us -> 0.83 us  [compute(): taps = jnp.pad(taps, ((0, 0), (0, pixels - 9)))]
  transfers between devices with their start and end apart: 21 -> 21, of which waited for: 9 -> 8; matrix products, arithmetic and copies ran while one was open for 7% -> 4% of each run, Pallas kernels for 22% -> 21%
where the time goes in v6:
time: 97.7 us; the launch traced here: 97.3 us
  waiting for transfers between devices  35 us (36%)
  starting transfers between devices  33.8 us (35%)
  Pallas kernels  21.4 us (22%)
  local copies, waits for them, and re-layouts  5.19 us (5%)
  other arithmetic  1.52 us (2%)
    ppermute x14, waiting for transfers between devices, swap_all(): arrived[k] = send(parts[k], perm=[(i, i ^ k) for i in range(views)])  32.9 us
    ppermute x14, starting transfers between devices, swap_all(): arrived[k] = send(parts[k], perm=[(i, i ^ k) for i in range(views)])  15.2 us
    pallas_call x1, Pallas kernels, add_set(): pl.pallas_call(functools.partial(set_kernel, t), out_shape=float_shapes([...  6.14 us
    ppermute x1, starting transfers between devices, compute(): send(far_high, perm=[(i, j + 1) for i, j in home if j + 1 < views])  6.02 us
    pallas_call x1, Pallas kernels, add_middle(): pl.pallas_call(middle_kernel, out_shape=float_shapes([(rows, DISP, pixels...  3.79 us
    ppermute x1, starting transfers between devices, compute(): own_high = send(own_high, perm=[(i, i + 1) for i in range(views - 1)])  3.68 us
    pallas_call x1, Pallas kernels, add_ends(): pl.pallas_call(functools.partial(ends_kernel, t), out_shape=float_shapes(...  3.62 us
    pallas_call x1, Pallas kernels, pack_rows(): pl.pallas_call(functools.partial(pack_kernel, half, apart), out_shape=out...  3.61 us
  transfers between devices with their start and end apart: 21, of which 8 were waited for; matrix products, arithmetic and copies ran while one was open for 4% of the time, Pallas kernels for 21%

profile of v6, /device:TPU:7, one launch (start us, length us, event | category | flops | bytes accessed | tf_op | source)
XLA Modules:
  0.0 97.3 jit_solution(7988385519544590965)
XLA Ops:
  0.7 2.4 %collective-permute-start = (bf16[2,128]{1,0:T(2,128)(2,1)S(1)}, bf16[2,128]{1,0:T(2,128)(2,1)S(1)}, u32[]{:S(2)}, u32[]{:S(2)}) collective-permute-start(bf16[2,128]{1,0:T(2,128)(2,1)S(1)} %fusion.3.near_ref), channel_id=1, source_target_pairs={{0,8},{1,9},{2,10},{3,11},{4,12},{5,13},{6,14},{7,15},{8,0},{9,1},... | collective-permute-start | bytes 1544 | tf_op jit(solution)/shard_map/ppermute | solution.py:504
  3.2 3.6 %pack_rows.1 = (bf16[656,128]{1,0:T(8,128)(2,1)}, bf16[656,128]{1,0:T(8,128)(2,1)}, bf16[656,128]{1,0:T(8,128)(2,1)}, bf16[656,128]{1,0:T(8,128)(2,1)}, bf16[656...) custom-call(s32[12]{0:T(128)} %bitcast.51, ...), custom_call_target="tpu_custom_call" | custom-call | tf_op jit(solution)/shard_map/pack_rows/pallas_call | solution.py:87
  6.8 1.3 %collective-permute-start.10 = (bf16[640,128]{1,0:T(8,128)(2,1)}, bf16[640,128]{1,0:T(8,128)(2,1)S(1)}, u32[]{:S(2)}, u32[]{:S(2)}) collective-permute-start(bf16[640,128]{1,0:T(8,128)(2,1)} %get-tuple-element.58), channel_id=1, source_target_pairs={{0,3},{1,2},{2,1},{3,0},{4,7},{5,6},{6,5},{7,4},{8,11},{9,10},{10,... | collective-permute-start | bytes 491528 | tf_op jit(solution)/shard_map/ppermute | solution.py:519
  8.1 1.3 %collective-permute-start.11 = (bf16[640,128]{1,0:T(8,128)(2,1)}, bf16[640,128]{1,0:T(8,128)(2,1)S(1)}, u32[]{:S(2)}, u32[]{:S(2)}) collective-permute-start(bf16[640,128]{1,0:T(8,128)(2,1)} %get-tuple-element.59), channel_id=1, source_target_pairs={{0,4},{1,5},{2,6},{3,7},{4,0},{5,1},{6,2},{7,3},{8,12},{9,13},{10,... | collective-permute-start | bytes 491528 | tf_op jit(solution)/shard_map/ppermute | solution.py:519
  10.5 0.8 pad_maximum_fusion.edge_ref
  11.3 1.5 %stack_left.2.left_ref = bf16[4,128,960]{2,1,0:T(8,128)(2,1)S(1)} custom-call(bf16[4,320,128]{2,1,0:T(8,128)(2,1)} %reference_ref.1), custom_call_target="tpu_custom_call" | custom-call | tf_op jit(solution)/shard_map/stack_left/pallas_call | solution.py:191
  12.8 1.0 %copy-done = bf16[4,128,960]{2,1,0:T(8,128)(2,1)} copy-done((bf16[4,128,960]{2,1,0:T(8,128)(2,1)}, bf16[4,128,960]{2,1,0:T(8,128)(2,1)S(1)}, u32[]{:S(2)}) %copy-start) | copy-done | bytes 983064
  14.1 0.8 pad.17.weight_ref
  15.5 1.5 %add_note.1 = (bf16[656,128]{1,0:T(8,128)(2,1)}, bf16[656,128]{1,0:T(8,128)(2,1)}, bf16[656,128]{1,0:T(8,128)(2,1)}, bf16[656,128]{1,0:T(8,128)(2,1)}, bf16[656,...) custom-call(f32[8,128]{1,0:T(8,128)} %get-tuple-element.38.slot_ref,, ...), custom_call_target="tpu_custom_call", output_to_operand_aliasing={{0}: (3, {}), {1}: (4, {}), {2}: (5, {}), {3}: (6, {}), {4}... | custom-call | tf_op jit(solution)/shard_map/add_note/pallas_call | solution.py:138
  18.6 1.1 %collective-permute-start.2 = (bf16[656,128]{1,0:T(8,128)(2,1)}, bf16[656,128]{1,0:T(8,128)(2,1)S(1)}, u32[]{:S(2)}, u32[]{:S(2)}) collective-permute-start(bf16[656,128]{1,0:T(8,128)(2,1)} %get-tuple-element.49), channel_id=1, source_target_pairs={{0,2},{1,3},{2,0},{3,1},{4,6},{5,7},{6,4},{7,5},{8,10},{9,11},{10,... | collective-permute-start | bytes 503816 | tf_op jit(solution)/shard_map/ppermute | solution.py:519
  19.8 4.7 %collective-permute-done.2.rest_2_ = bf16[656,128]{1,0:T(8,128)(2,1)S(1)} collective-permute-done((bf16[656,128]{1,0:T(8,128)(2,1)}, bf16[656,128]{1,0:T(8,128)(2,1)S(1)}, u32[]{:S(2)}, u32[]{:S(2)}) %collective-permute-start.2) | collective-permute-done | bytes 167968 | tf_op jit(solution)/shard_map/ppermute | solution.py:519
  24.4 2.1 %collective-permute-start.3 = (bf16[656,128]{1,0:T(8,128)(2,1)}, bf16[656,128]{1,0:T(8,128)(2,1)S(1)}, u32[]{:S(2)}, u32[]{:S(2)}) collective-permute-start(bf16[656,128]{1,0:T(8,128)(2,1)} %get-tuple-element.50), channel_id=1, source_target_pairs={{0,3},{1,2},{2,1},{3,0},{4,7},{5,6},{6,5},{7,4},{8,11},{9,10},{10,... | collective-permute-start | bytes 503816 | tf_op jit(solution)/shard_map/ppermute | solution.py:519
  26.6 5.3 %collective-permute-done.3.rest_3_ = bf16[656,128]{1,0:T(8,128)(2,1)S(1)} collective-permute-done((bf16[656,128]{1,0:T(8,128)(2,1)}, bf16[656,128]{1,0:T(8,128)(2,1)S(1)}, u32[]{:S(2)}, u32[]{:S(2)}) %collective-permute-start.3) | collective-permute-done | bytes 167968 | tf_op jit(solution)/shard_map/ppermute | solution.py:519
  31.9 1.3 %collective-permute-start.4 = (bf16[656,128]{1,0:T(8,128)(2,1)}, bf16[656,128]{1,0:T(8,128)(2,1)S(1)}, u32[]{:S(2)}, u32[]{:S(2)}) collective-permute-start(bf16[656,128]{1,0:T(8,128)(2,1)} %get-tuple-element.51), channel_id=1, source_target_pairs={{0,4},{1,5},{2,6},{3,7},{4,0},{5,1},{6,2},{7,3},{8,12},{9,13},{10,... | collective-permute-start | bytes 503816 | tf_op jit(solution)/shard_map/ppermute | solution.py:519
  33.2 4.3 %collective-permute-done.4.rest_4_ = bf16[656,128]{1,0:T(8,128)(2,1)S(1)} collective-permute-done((bf16[656,128]{1,0:T(8,128)(2,1)}, bf16[656,128]{1,0:T(8,128)(2,1)S(1)}, u32[]{:S(2)}, u32[]{:S(2)}) %collective-permute-start.4) | collective-permute-done | bytes 167968 | tf_op jit(solution)/shard_map/ppermute | solution.py:519
  37.5 2.5 %collective-permute-start.5 = (bf16[656,128]{1,0:T(8,128)(2,1)}, bf16[656,128]{1,0:T(8,128)(2,1)S(1)}, u32[]{:S(2)}, u32[]{:S(2)}) collective-permute-start(bf16[656,128]{1,0:T(8,128)(2,1)} %get-tuple-element.52), channel_id=1, source_target_pairs={{0,5},{1,4},{2,7},{3,6},{4,1},{5,0},{6,3},{7,2},{8,13},{9,12},{10,... | collective-permute-start | bytes 503816 | tf_op jit(solution)/shard_map/ppermute | solution.py:519
  40.0 5.0 %collective-permute-done.5.rest_5_ = bf16[656,128]{1,0:T(8,128)(2,1)S(1)} collective-permute-done((bf16[656,128]{1,0:T(8,128)(2,1)}, bf16[656,128]{1,0:T(8,128)(2,1)S(1)}, u32[]{:S(2)}, u32[]{:S(2)}) %collective-permute-start.5) | collective-permute-done | bytes 167968 | tf_op jit(solution)/shard_map/ppermute | solution.py:519
  45.1 6.5 %collective-permute-done.6.rest_6_ = bf16[656,128]{1,0:T(8,128)(2,1)S(1)} collective-permute-done((bf16[656,128]{1,0:T(8,128)(2,1)}, bf16[656,128]{1,0:T(8,128)(2,1)S(1)}, u32[]{:S(2)}, u32[]{:S(2)}) %collective-permute-start.6) | collective-permute-done | bytes 167968 | tf_op jit(solution)/shard_map/ppermute | solution.py:519
  51.6 1.1 %collective-permute-start.7 = (bf16[656,128]{1,0:T(8,128)(2,1)}, bf16[656,128]{1,0:T(8,128)(2,1)S(1)}, u32[]{:S(2)}, u32[]{:S(2)}) collective-permute-start(bf16[656,128]{1,0:T(8,128)(2,1)} %get-tuple-element.54), channel_id=1, source_target_pairs={{0,7},{1,6},{2,5},{3,4},{4,3},{5,2},{6,1},{7,0},{8,15},{9,14},{10,... | collective-permute-start | bytes 503816 | tf_op jit(solution)/shard_map/ppermute | solution.py:519
  52.8 6.3 %collective-permute-done.7.rest_7_ = bf16[656,128]{1,0:T(8,128)(2,1)S(1)} collective-permute-done((bf16[656,128]{1,0:T(8,128)(2,1)}, bf16[656,128]{1,0:T(8,128)(2,1)S(1)}, u32[]{:S(2)}, u32[]{:S(2)}) %collective-permute-start.7) | collective-permute-done | bytes 167968 | tf_op jit(solution)/shard_map/ppermute | solution.py:519
  59.0 0.8 collective-permute-start.13
  60.0 2.7 %collective-permute-start.14 = (bf16[640,128]{1,0:T(8,128)(2,1)S(1)}, bf16[640,128]{1,0:T(8,128)(2,1)S(1)}, u32[]{:S(2)}, u32[]{:S(2)}) collective-permute-start(bf16[640,128]{1,0:T(8,128)(2,1)S(1)} %copy-done.14), channel_id=1, source_target_pairs={{0,7},{1,6},{2,5},{3,4},{4,3},{5,2},{6,1},{7,0},{8,15},{9,14},{10,... | collective-permute-start | bytes 491528 | tf_op jit(solution)/shard_map/ppermute | solution.py:519
  63.3 1.0 %copy-done.3 = bf16[4,128,960]{2,1,0:T(8,128)(2,1)} copy-done((bf16[4,128,960]{2,1,0:T(8,128)(2,1)}, bf16[4,128,960]{2,1,0:T(8,128)(2,1)S(1)}, u32[]{:S(2)}) %copy-start.3) | copy-done | bytes 983064
  64.5 6.1 %add_set.1 = (f32[4,96,128]{2,1,0:T(8,128)S(1)}, f32[1,96,128]{2,1,0:T(8,128)S(1)}, f32[1,96,128]{2,1,0:T(8,128)S(1)}) custom-call(s32[32]{0:T(128)S(1)} %reshape.16.code_ref, bf16[8,16,128]{2,1,0:T(8,128)(2,1)S(1)} %constant_dynamic-update-slice_fusion.note_ref, bf16[4,128,960]{2,1,0:T(8,128)(2,1)} %copy-done.3, f32[960,128]{1,0:T(8,128)} %pad.17.weight_ref, ...), custom_call_target="tpu_custom_call" | custom-call | flops 2264924160 | bytes 1343488 | tf_op jit(solution)/shard_map/add_set/pallas_call | solution.py:389
  70.7 2.4 %collective-permute-start.16 = (f32[4,96,128]{2,1,0:T(8,128)S(1)}, f32[4,96,128]{2,1,0:T(8,128)S(1)}, u32[]{:S(2)}, u32[]{:S(2)}) collective-permute-start(f32[4,96,128]{2,1,0:T(8,128)S(1)} %get-tuple-element.66), channel_id=1, source_target_pairs={{0,8},{1,9},{2,10},{3,11},{4,12},{5,13},{6,14},{7,15},{8,0},{9,1},... | collective-permute-start | bytes 589832 | tf_op jit(solution)/shard_map/ppermute | solution.py:537
  73.1 3.6 %add_ends.1 = (f32[1,96,128]{2,1,0:T(8,128)S(1)}, f32[1,96,128]{2,1,0:T(8,128)S(1)}, f32[2,960,128]{2,1,0:T(8,128)S(1)}, f32[2,128,128]{2,1,0:T(8,128)S(1)}, f32[2,320,128]{2,1,0:T(8,128)S(1)}) custom-call(s32[32]{0:T(128)S(1)} %reshape.16.code_ref, bf16[8,16,128]{2,1,0:T(8,128)(2,1)S(1)} %constant_dynamic-update-slice_fusion.note_ref, ...), custom_call_target="tpu_custom_call" | custom-call | flops 377487360 | bytes 1310720 | tf_op jit(solution)/shard_map/add_ends/pallas_call | solution.py:416
  76.8 3.7 %collective-permute-start.17 = (f32[1,96,128]{2,1,0:T(8,128)S(1)}, f32[1,96,128]{2,1,0:T(8,128)S(1)}, u32[]{:S(2)}, u32[]{:S(2)}) collective-permute-start(f32[1,96,128]{2,1,0:T(8,128)S(1)} %get-tuple-element.67), channel_id=1, source_target_pairs={{0,1},{1,2},{2,3},{3,4},{4,5},{5,6},{6,7},{7,8},{8,9},{9,10},{10,1... | collective-permute-start | bytes 147464 | tf_op jit(solution)/shard_map/ppermute | solution.py:542
  80.4 1.9 %collective-permute-start.19 = (f32[1,96,128]{2,1,0:T(8,128)S(1)}, f32[1,96,128]{2,1,0:T(8,128)S(1)}, u32[]{:S(2)}, u32[]{:S(2)}) collective-permute-start(f32[1,96,128]{2,1,0:T(8,128)S(1)} %get-tuple-element.69), channel_id=1, source_target_pairs={{1,0},{2,1},{3,2},{4,3},{5,4},{6,5},{7,6},{8,7},{9,8},{10,9},{11,1... | collective-permute-start | bytes 147464 | tf_op jit(solution)/shard_map/ppermute | solution.py:541
  82.4 6.0 %collective-permute-start.18 = (f32[1,96,128]{2,1,0:T(8,128)S(1)}, f32[1,96,128]{2,1,0:T(8,128)S(1)}, u32[]{:S(2)}, u32[]{:S(2)}) collective-permute-start(f32[1,96,128]{2,1,0:T(8,128)S(1)} %get-tuple-element.68), channel_id=1, source_target_pairs={{0,9},{1,10},{2,11},{3,12},{4,13},{5,14},{6,15},{8,1},{9,2},{10,3}... | collective-permute-start | bytes 147464 | tf_op jit(solution)/shard_map/ppermute | solution.py:539
  88.4 2.1 %collective-permute-start.20 = (f32[1,96,128]{2,1,0:T(8,128)S(1)}, f32[1,96,128]{2,1,0:T(8,128)S(1)}, u32[]{:S(2)}, u32[]{:S(2)}) collective-permute-start(f32[1,96,128]{2,1,0:T(8,128)S(1)} %get-tuple-element.70), channel_id=1, source_target_pairs={{0,7},{1,8},{2,9},{3,10},{4,11},{5,12},{6,13},{7,14},{9,0},{10,1},... | collective-permute-start | bytes 147464 | tf_op jit(solution)/shard_map/ppermute | solution.py:538
  90.5 3.8 %add_middle.1.own_ref = f32[4,96,128]{2,1,0:T(8,128)S(1)} custom-call(f32[2,960,128]{2,1,0:T(8,128)S(1)} %get-tuple-element.63.ends_ref, f32[2,128,128]{2,1,0:T(8,128)S(1)} %get-tuple-element.64.term_ref, f32[2,320,128]{2,1,0:T(8,128)S(1)} %get-tuple-element.65.inner_ref, bf16[4,128,960]{2,1,0:T(8,128)(2,1)S(1)} %copy-done.1, f32[960,128]{1,0:T(8,128)S(1)} %copy-done.2, ...), custom_call_target="tpu_custom_call" | custom-call | flops 1887436800 | bytes 720896 | tf_op jit(solution)/shard_map/add_middle/pallas_call | solution.py:437
  94.4 2.1 %collective-permute-done.20.after_far_ref = f32[1,96,128]{2,1,0:T(8,128)S(1)} collective-permute-done((f32[1,96,128]{2,1,0:T(8,128)S(1)}, f32[1,96,128]{2,1,0:T(8,128)S(1)}, u32[]{:S(2)}, u32[]{:S(2)}) %collective-permute-start.20) | collective-permute-done | bytes 49184 | tf_op jit(solution)/shard_map/ppermute | solution.py:538
  (75 shorter events, 6.0 us)
Async XLA Ops:
  0.7 2.5 %copy-start.10 = (bf16[2,128]{1,0:T(2,128)(2,1)}, bf16[2,128]{1,0:T(2,128)(2,1)S(1)}, u32[]{:S(2)}) copy-start(bf16[2,128]{1,0:T(2,128)(2,1)S(1)} %fusion.3.near_ref) | copy-start | bytes 1540
  0.7 14.2 %collective-permute-start = (bf16[2,128]{1,0:T(2,128)(2,1)S(1)}, bf16[2,128]{1,0:T(2,128)(2,1)S(1)}, u32[]{:S(2)}, u32[]{:S(2)}) collective-permute-start(bf16[2,128]{1,0:T(2,128)(2,1)S(1)} %fusion.3.near_ref), channel_id=1, source_target_pairs={{0,8},{1,9},{2,10},{3,11},{4,12},{5,13},{6,14},{7,15},{8,0},{9,1},... | collective-permute-start | bytes 1544 | tf_op jit(solution)/shard_map/ppermute | solution.py:504
  3.1 56.9 %collective-permute-start.15 = (bf16[4,320,128]{2,1,0:T(8,128)(2,1)}, bf16[4,320,128]{2,1,0:T(8,128)(2,1)S(1)}, u32[]{:S(2)}, u32[]{:S(2)}) collective-permute-start(bf16[4,320,128]{2,1,0:T(8,128)(2,1)} %reference_ref.1), channel_id=1, source_target_pairs={{0,8},{1,9},{2,10},{3,11},{4,12},{5,13},{6,14},{7,15},{8,0},{9,1},... | collective-permute-start | bytes 983048 | tf_op jit(solution)/shard_map/ppermute | solution.py:505
  3.2 6.6 %copy-start.7 = (f32[40,3,3,3]{0,3,2,1:T(4,128)S(1)}, f32[40,3,3,3]{0,3,2,1:T(4,128)}, u32[]{:S(2)}) copy-start(f32[40,3,3,3]{0,3,2,1:T(4,128)} %param.11) | copy-start | bytes 12964
  6.8 57.5 %collective-permute-start.10 = (bf16[640,128]{1,0:T(8,128)(2,1)}, bf16[640,128]{1,0:T(8,128)(2,1)S(1)}, u32[]{:S(2)}, u32[]{:S(2)}) collective-permute-start(bf16[640,128]{1,0:T(8,128)(2,1)} %get-tuple-element.58), channel_id=1, source_target_pairs={{0,3},{1,2},{2,1},{3,0},{4,7},{5,6},{6,5},{7,4},{8,11},{9,10},{10,... | collective-permute-start | bytes 491528 | tf_op jit(solution)/shard_map/ppermute | solution.py:519
  8.1 56.1 %collective-permute-start.11 = (bf16[640,128]{1,0:T(8,128)(2,1)}, bf16[640,128]{1,0:T(8,128)(2,1)S(1)}, u32[]{:S(2)}, u32[]{:S(2)}) collective-permute-start(bf16[640,128]{1,0:T(8,128)(2,1)} %get-tuple-element.59), channel_id=1, source_target_pairs={{0,4},{1,5},{2,6},{3,7},{4,0},{5,1},{6,2},{7,3},{8,12},{9,13},{10,... | collective-permute-start | bytes 491528 | tf_op jit(solution)/shard_map/ppermute | solution.py:519
  9.5 61.2 %collective-permute-start.12 = (bf16[640,128]{1,0:T(8,128)(2,1)}, bf16[640,128]{1,0:T(8,128)(2,1)S(1)}, u32[]{:S(2)}, u32[]{:S(2)}) collective-permute-start(bf16[640,128]{1,0:T(8,128)(2,1)} %get-tuple-element.60), channel_id=1, source_target_pairs={{0,5},{1,4},{2,7},{3,6},{4,1},{5,0},{6,3},{7,2},{8,13},{9,12},{10,... | collective-permute-start | bytes 491528 | tf_op jit(solution)/shard_map/ppermute | solution.py:519
  15.5 43.6 %copy-start.15 = (bf16[640,128]{1,0:T(8,128)(2,1)S(1)}, bf16[640,128]{1,0:T(8,128)(2,1)}, u32[]{:S(2)}) copy-start(bf16[640,128]{1,0:T(8,128)(2,1)} %get-tuple-element.61) | copy-start | bytes 491524
  15.5 44.5 %copy-start.14 = (bf16[640,128]{1,0:T(8,128)(2,1)S(1)}, bf16[640,128]{1,0:T(8,128)(2,1)}, u32[]{:S(2)}) copy-start(bf16[640,128]{1,0:T(8,128)(2,1)} %get-tuple-element.62) | copy-start | bytes 491524
  17.0 1.7 %collective-permute-start.1 = (bf16[656,128]{1,0:T(8,128)(2,1)}, bf16[656,128]{1,0:T(8,128)(2,1)S(1)}, u32[]{:S(2)}, u32[]{:S(2)}) collective-permute-start(bf16[656,128]{1,0:T(8,128)(2,1)} %get-tuple-element.48), channel_id=1, source_target_pairs={{0,1},{1,0},{2,3},{3,2},{4,5},{5,4},{6,7},{7,6},{8,9},{9,8},{10,11... | collective-permute-start | bytes 503816 | tf_op jit(solution)/shard_map/ppermute | solution.py:519
  18.6 5.8 %collective-permute-start.2 = (bf16[656,128]{1,0:T(8,128)(2,1)}, bf16[656,128]{1,0:T(8,128)(2,1)S(1)}, u32[]{:S(2)}, u32[]{:S(2)}) collective-permute-start(bf16[656,128]{1,0:T(8,128)(2,1)} %get-tuple-element.49), channel_id=1, source_target_pairs={{0,2},{1,3},{2,0},{3,1},{4,6},{5,7},{6,4},{7,5},{8,10},{9,11},{10,... | collective-permute-start | bytes 503816 | tf_op jit(solution)/shard_map/ppermute | solution.py:519
  24.4 7.4 %collective-permute-start.3 = (bf16[656,128]{1,0:T(8,128)(2,1)}, bf16[656,128]{1,0:T(8,128)(2,1)S(1)}, u32[]{:S(2)}, u32[]{:S(2)}) collective-permute-start(bf16[656,128]{1,0:T(8,128)(2,1)} %get-tuple-element.50), channel_id=1, source_target_pairs={{0,3},{1,2},{2,1},{3,0},{4,7},{5,6},{6,5},{7,4},{8,11},{9,10},{10,... | collective-permute-start | bytes 503816 | tf_op jit(solution)/shard_map/ppermute | solution.py:519
  31.9 5.6 %collective-permute-start.4 = (bf16[656,128]{1,0:T(8,128)(2,1)}, bf16[656,128]{1,0:T(8,128)(2,1)S(1)}, u32[]{:S(2)}, u32[]{:S(2)}) collective-permute-start(bf16[656,128]{1,0:T(8,128)(2,1)} %get-tuple-element.51), channel_id=1, source_target_pairs={{0,4},{1,5},{2,6},{3,7},{4,0},{5,1},{6,2},{7,3},{8,12},{9,13},{10,... | collective-permute-start | bytes 503816 | tf_op jit(solution)/shard_map/ppermute | solution.py:519
  37.5 7.5 %collective-permute-start.5 = (bf16[656,128]{1,0:T(8,128)(2,1)}, bf16[656,128]{1,0:T(8,128)(2,1)S(1)}, u32[]{:S(2)}, u32[]{:S(2)}) collective-permute-start(bf16[656,128]{1,0:T(8,128)(2,1)} %get-tuple-element.52), channel_id=1, source_target_pairs={{0,5},{1,4},{2,7},{3,6},{4,1},{5,0},{6,3},{7,2},{8,13},{9,12},{10,... | collective-permute-start | bytes 503816 | tf_op jit(solution)/shard_map/ppermute | solution.py:519
  45.1 6.6 %collective-permute-start.6 = (bf16[656,128]{1,0:T(8,128)(2,1)}, bf16[656,128]{1,0:T(8,128)(2,1)S(1)}, u32[]{:S(2)}, u32[]{:S(2)}) collective-permute-start(bf16[656,128]{1,0:T(8,128)(2,1)} %get-tuple-element.53), channel_id=1, source_target_pairs={{0,6},{1,7},{2,4},{3,5},{4,2},{5,3},{6,0},{7,1},{8,14},{9,15},{10,... | collective-permute-start | bytes 503816 | tf_op jit(solution)/shard_map/ppermute | solution.py:519
  51.6 7.4 %collective-permute-start.7 = (bf16[656,128]{1,0:T(8,128)(2,1)}, bf16[656,128]{1,0:T(8,128)(2,1)S(1)}, u32[]{:S(2)}, u32[]{:S(2)}) collective-permute-start(bf16[656,128]{1,0:T(8,128)(2,1)} %get-tuple-element.54), channel_id=1, source_target_pairs={{0,7},{1,6},{2,5},{3,4},{4,3},{5,2},{6,1},{7,0},{8,15},{9,14},{10,... | collective-permute-start | bytes 503816 | tf_op jit(solution)/shard_map/ppermute | solution.py:519
  59.0 14.0 %collective-permute-start.13 = (bf16[640,128]{1,0:T(8,128)(2,1)S(1)}, bf16[640,128]{1,0:T(8,128)(2,1)S(1)}, u32[]{:S(2)}, u32[]{:S(2)}) collective-permute-start(bf16[640,128]{1,0:T(8,128)(2,1)S(1)} %copy-done.15), channel_id=1, source_target_pairs={{0,6},{1,7},{2,4},{3,5},{4,2},{5,3},{6,0},{7,1},{8,14},{9,15},{10,... | collective-permute-start | bytes 491528 | tf_op jit(solution)/shard_map/ppermute | solution.py:519
  60.0 4.3 %copy-start.13 = (bf16[640,128]{1,0:T(8,128)(2,1)S(1)}, bf16[640,128]{1,0:T(8,128)(2,1)}, u32[]{:S(2)}) copy-start(bf16[640,128]{1,0:T(8,128)(2,1)} %get-tuple-element.56) | copy-start | bytes 491524
  60.0 4.3 %copy-start.12 = (bf16[640,128]{1,0:T(8,128)(2,1)S(1)}, bf16[640,128]{1,0:T(8,128)(2,1)}, u32[]{:S(2)}) copy-start(bf16[640,128]{1,0:T(8,128)(2,1)} %get-tuple-element.57) | copy-start | bytes 491524
  60.0 4.5 %copy-start.5 = (bf16[656,128]{1,0:T(8,128)(2,1)S(1)}, bf16[656,128]{1,0:T(8,128)(2,1)}, u32[]{:S(2)}) copy-start(bf16[656,128]{1,0:T(8,128)(2,1)} %get-tuple-element.47.rest_0_) | copy-start | bytes 503812
  60.0 13.0 %collective-permute-start.14 = (bf16[640,128]{1,0:T(8,128)(2,1)S(1)}, bf16[640,128]{1,0:T(8,128)(2,1)S(1)}, u32[]{:S(2)}, u32[]{:S(2)}) collective-permute-start(bf16[640,128]{1,0:T(8,128)(2,1)S(1)} %copy-done.14), channel_id=1, source_target_pairs={{0,7},{1,6},{2,5},{3,4},{4,3},{5,2},{6,1},{7,0},{8,15},{9,14},{10,... | collective-permute-start | bytes 491528 | tf_op jit(solution)/shard_map/ppermute | solution.py:519
  64.3 8.8 %collective-permute-start.8 = (bf16[640,128]{1,0:T(8,128)(2,1)S(1)}, bf16[640,128]{1,0:T(8,128)(2,1)S(1)}, u32[]{:S(2)}, u32[]{:S(2)}) collective-permute-start(bf16[640,128]{1,0:T(8,128)(2,1)S(1)} %copy-done.13), channel_id=1, source_target_pairs={{0,1},{1,0},{2,3},{3,2},{4,5},{5,4},{6,7},{7,6},{8,9},{9,8},{10,11... | collective-permute-start | bytes 491528 | tf_op jit(solution)/shard_map/ppermute | solution.py:519
  64.3 8.8 %copy-start.6 = (bf16[640,128]{1,0:T(8,128)(2,1)S(1)}, bf16[640,128]{1,0:T(8,128)(2,1)}, u32[]{:S(2)}) copy-start(bf16[640,128]{1,0:T(8,128)(2,1)} %get-tuple-element.55.rest_0_) | copy-start | bytes 491524
  64.3 8.8 %collective-permute-start.9 = (bf16[640,128]{1,0:T(8,128)(2,1)S(1)}, bf16[640,128]{1,0:T(8,128)(2,1)S(1)}, u32[]{:S(2)}, u32[]{:S(2)}) collective-permute-start(bf16[640,128]{1,0:T(8,128)(2,1)S(1)} %copy-done.12), channel_id=1, source_target_pairs={{0,2},{1,3},{2,0},{3,1},{4,6},{5,7},{6,4},{7,5},{8,10},{9,11},{10,... | collective-permute-start | bytes 491528 | tf_op jit(solution)/shard_map/ppermute | solution.py:519
  70.7 25.8 %collective-permute-start.16 = (f32[4,96,128]{2,1,0:T(8,128)S(1)}, f32[4,96,128]{2,1,0:T(8,128)S(1)}, u32[]{:S(2)}, u32[]{:S(2)}) collective-permute-start(f32[4,96,128]{2,1,0:T(8,128)S(1)} %get-tuple-element.66), channel_id=1, source_target_pairs={{0,8},{1,9},{2,10},{3,11},{4,12},{5,13},{6,14},{7,15},{8,0},{9,1},... | collective-permute-start | bytes 589832 | tf_op jit(solution)/shard_map/ppermute | solution.py:537
  73.1 17.4 %copy-start.1 = (bf16[4,128,960]{2,1,0:T(8,128)(2,1)S(1)}, bf16[4,128,960]{2,1,0:T(8,128)(2,1)}, u32[]{:S(2)}) copy-start(bf16[4,128,960]{2,1,0:T(8,128)(2,1)} %copy-done) | copy-start | bytes 2949124
  73.1 17.4 %copy-start.2 = (f32[960,128]{1,0:T(8,128)S(1)}, f32[960,128]{1,0:T(8,128)}, u32[]{:S(2)}) copy-start(f32[960,128]{1,0:T(8,128)} %pad.17.weight_ref) | copy-start | bytes 1474564
  73.1 17.4 %copy-start.4 = (f32[320,128]{1,0:T(8,128)S(1)}, f32[320,128]{1,0:T(8,128)}, u32[]{:S(2)}) copy-start(f32[320,128]{1,0:T(8,128)} %pad_maximum_fusion.edge_ref) | copy-start | bytes 491524
  76.8 17.6 %collective-permute-start.17 = (f32[1,96,128]{2,1,0:T(8,128)S(1)}, f32[1,96,128]{2,1,0:T(8,128)S(1)}, u32[]{:S(2)}, u32[]{:S(2)}) collective-permute-start(f32[1,96,128]{2,1,0:T(8,128)S(1)} %get-tuple-element.67), channel_id=1, source_target_pairs={{0,1},{1,2},{2,3},{3,4},{4,5},{5,6},{6,7},{7,8},{8,9},{9,10},{10,1... | collective-permute-start | bytes 147464 | tf_op jit(solution)/shard_map/ppermute | solution.py:542
  80.4 13.9 %collective-permute-start.19 = (f32[1,96,128]{2,1,0:T(8,128)S(1)}, f32[1,96,128]{2,1,0:T(8,128)S(1)}, u32[]{:S(2)}, u32[]{:S(2)}) collective-permute-start(f32[1,96,128]{2,1,0:T(8,128)S(1)} %get-tuple-element.69), channel_id=1, source_target_pairs={{1,0},{2,1},{3,2},{4,3},{5,4},{6,5},{7,6},{8,7},{9,8},{10,9},{11,1... | collective-permute-start | bytes 147464 | tf_op jit(solution)/shard_map/ppermute | solution.py:541
  82.4 12.0 %collective-permute-start.18 = (f32[1,96,128]{2,1,0:T(8,128)S(1)}, f32[1,96,128]{2,1,0:T(8,128)S(1)}, u32[]{:S(2)}, u32[]{:S(2)}) collective-permute-start(f32[1,96,128]{2,1,0:T(8,128)S(1)} %get-tuple-element.68), channel_id=1, source_target_pairs={{0,9},{1,10},{2,11},{3,12},{4,13},{5,14},{6,15},{8,1},{9,2},{10,3}... | collective-permute-start | bytes 147464 | tf_op jit(solution)/shard_map/ppermute | solution.py:539
  88.4 8.1 %collective-permute-start.20 = (f32[1,96,128]{2,1,0:T(8,128)S(1)}, f32[1,96,128]{2,1,0:T(8,128)S(1)}, u32[]{:S(2)}, u32[]{:S(2)}) collective-permute-start(f32[1,96,128]{2,1,0:T(8,128)S(1)} %get-tuple-element.70), channel_id=1, source_target_pairs={{0,7},{1,8},{2,9},{3,10},{4,11},{5,12},{6,13},{7,14},{9,0},{10,1},... | collective-permute-start | bytes 147464 | tf_op jit(solution)/shard_map/ppermute | solution.py:538
  (5 other events, 3.9 us)
